TPU v7x, 32 devices: a whole 2x2x4 slice. The times are simulated.
32 devices in a mesh: dp: 4 (over y, x), expert: 8 (over z, core).
Axes of the slice: x: 2, y: 2, z: 4, core: 2. Of those that a mesh axis runs over, the one named last changes fastest.
Arguments:
- block_input: bfloat16 [20480, 1024], P(('dp', 'expert')), may hold values from -6 to 6
- routes: int32 [20480, 2], P(('dp', 'expert')), may hold values from 0 to 7, all different within a row; in each aligned block of 640 rows (0 to 639, 640 to 1279, ...) at most 200 rows name the same one
- item_lengths: int32 [32, 2], P(('dp', 'expert')), may hold values from 64 to 512, as said below
- w_qkv: bfloat16 [1024, 3072], replicated, may hold values from -0.1875 to 0.1875
- w_attn_out: bfloat16 [1024, 1024], replicated, may hold values from -1 to 1
- rel_table: float32 [32, 16], replicated, may hold values from -4 to 4
- gain_attn: float32 [1024], replicated, may hold values from 0.25 to 1.75
- gain_moe: float32 [1024], replicated, may hold values from 0.25 to 1.75
- w_router: bfloat16 [1024, 8], replicated, may hold values from -0.125 to 0.125
- w_gate: bfloat16 [8, 1024, 2816], P('expert'), may hold values from -0.1875 to 0.1875
- w_up: bfloat16 [8, 1024, 2816], P('expert'), may hold values from -0.1875 to 0.1875
- w_down: bfloat16 [8, 2816, 1024], P('expert'), may hold values from -0.15625 to 0.15625
- cotangent: bfloat16 [20480, 1024], P(('dp', 'expert')), may hold values from -6 to 6
Outputs:
- output: bfloat16 [20480, 1024], P(('dp', 'expert'))
- grad_input: float32 [20480, 1024], P(('dp', 'expert'))
- grad_qkv: float32 [1024, 3072], P(('dp', 'expert'))
- grad_attn_out: float32 [1024, 1024], P(('dp', 'expert'))
- grad_rel_table: float32 [512], P(('dp', 'expert'))
- grad_gain_attn: float32 [1024], P(('dp', 'expert'))
- grad_gain_moe: float32 [1024], P(('dp', 'expert'))
- grad_router: float32 [1024, 8], P(('dp', 'expert'))
- grad_gate: float32 [8, 1024, 2816], P('expert', None, 'dp')
- grad_up: float32 [8, 1024, 2816], P('expert', None, 'dp')
- grad_down: float32 [8, 2816, 1024], P('expert', None, 'dp')
Inputs may be any that keep to these rules, and one draw needn't show every extreme that they name: `routes`: A row names two different experts. In each aligned block of 640 rows no expert is named by more than 200 rows, a bound that some block reaches. `item_lengths`: columns 0 to 0 lie between 256 and 512, the others between 64 and 128; both upper ends are reached.
All inputs are finite; a program needn't handle non-finite values.
Results may differ from a plain program's by a relative error of at most 0.019.
Values may be sent and summed in bfloat16 or wider, within the bound.
No kernel may reach another device: no remote copies, remote signals or barrier semaphores. Data moves between devices by JAX's collectives and lax.ppermute only.
A program may use at most 320 MiB of HBM per device.

v0:
```python
import jax
import jax.numpy as jnp
from jax import lax
from jax.sharding import PartitionSpec as P

TOP = 2
LONG_LEN = 512
SHORT_LEN = 128
LONG_DEV = 1
SHORT_DEV = 1
TOK_DEV = 640


BOUNDS = (12, 16, 23, 32, 46, 64, 91)
EPSILON = 1e-06
HIGHEST = lax.Precision.HIGHEST


def bucket_onehot(length, buckets):
    places = jnp.arange(length, dtype=jnp.int32)
    offset = places[None, :] - places[:, None]
    distance = jnp.abs(offset)
    far = 8 + sum(((distance >= bound).astype(jnp.int32) for bound in BOUNDS))
    table = jnp.where(distance < 8, distance, far) + 16 * (offset > 0).astype(jnp.int32)
    labels = jnp.arange(buckets, dtype=jnp.int32)
    return (table[:, :, None] == labels[None, None, :]).astype(jnp.float32)


def gaussian_unit(value):
    return (
        0.5
        * value
        * (1.0 + jnp.tanh(0.7978845608028654 * (value + 0.044715 * value * value * value)))
    )


def gated_product(gate_pre, up_pre):
    return gaussian_unit(gate_pre) * up_pre


def normalize_forward(value, gain):
    scale = lax.rsqrt(jnp.mean(value * value, axis=-1, keepdims=True) + EPSILON)
    unit = value * scale
    return (unit * gain, unit, scale)


def normalize_backward(grad, unit, scale, gain):
    gain_grad = jnp.sum(grad * unit, axis=0)
    along = grad * gain
    inner = jnp.mean(along * unit, axis=-1, keepdims=True)
    return (scale * (along - unit * inner), gain_grad)


def split_heads(proj, heads):
    count, length = (proj.shape[0], proj.shape[1])
    parted = proj.reshape(count, length, 3, heads, -1)
    return (parted[:, :, 0], parted[:, :, 1], parted[:, :, 2])


def masked_scores(query, keys, bias, lengths):
    length = query.shape[1]
    scores = (
        jnp.einsum("nqhd,nkhd->nhqk", query, keys, preferred_element_type=jnp.float32) * 0.125
        + bias[None]
    )
    valid = jnp.arange(length, dtype=jnp.int32)[None, :] < lengths[:, None]
    return jnp.where(valid[:, None, None, :], scores, -1e30)


def attention_forward(items, lengths, w_qkv, bias):
    count, length = (items.shape[0], items.shape[1])
    heads = bias.shape[0]
    proj = jnp.einsum("nld,de->nle", items, w_qkv, preferred_element_type=jnp.float32).astype(
        jnp.bfloat16
    )
    query, keys, values = split_heads(proj, heads)
    masked = masked_scores(query, keys, bias, lengths)
    highest = jnp.max(masked, axis=-1, keepdims=True)
    exps = jnp.exp(masked - highest)
    total = jnp.sum(exps, axis=-1, keepdims=True)
    weights = (exps / total).astype(jnp.bfloat16)
    mixed = jnp.einsum("nhqk,nkhd->nqhd", weights, values, preferred_element_type=jnp.float32)
    mixed = mixed.astype(jnp.bfloat16).reshape(count * length, -1)
    return (proj, mixed, highest + jnp.log(total))


def attention_backward(proj, log_total, lengths, bias, onehot, mixed_grad):
    count, length = (proj.shape[0], proj.shape[1])
    heads = bias.shape[0]
    query, keys, values = split_heads(proj, heads)
    probs = jnp.exp(masked_scores(query, keys, bias, lengths) - log_total)
    weights = probs.astype(jnp.bfloat16)
    head_grad = mixed_grad.reshape(count, length, heads, -1)
    probs_grad = jnp.einsum(
        "nqhd,nkhd->nhqk", head_grad, values, preferred_element_type=jnp.float32
    )
    values_grad = jnp.einsum(
        "nhqk,nqhd->nkhd", weights, head_grad, preferred_element_type=jnp.float32
    )
    inner = jnp.sum(probs_grad * probs, axis=-1, keepdims=True)
    scores_grad = (probs * (probs_grad - inner)).astype(jnp.bfloat16)
    table_grad = jnp.einsum(
        "nhqk,qkb->bh", scores_grad, onehot.astype(jnp.bfloat16), preferred_element_type=jnp.float32
    )
    query_grad = (
        jnp.einsum("nhqk,nkhd->nqhd", scores_grad, keys, preferred_element_type=jnp.float32) * 0.125
    )
    keys_grad = (
        jnp.einsum("nhqk,nqhd->nkhd", scores_grad, query, preferred_element_type=jnp.float32)
        * 0.125
    )
    proj_grad = jnp.stack([query_grad, keys_grad, values_grad], axis=2).astype(jnp.bfloat16)
    return (proj_grad.reshape(count * length, -1), table_grad)


def on_device(
    block_input,
    routes,
    item_lengths,
    w_qkv,
    w_attn_out,
    rel_table,
    gain_attn,
    gain_moe,
    w_router,
    w_gate,
    w_up,
    w_down,
    cotangent,
):
    width = block_input.shape[1]
    experts = w_router.shape[1]
    local = w_gate.shape[0]
    capacity = TOK_DEV * TOP * 5 // (4 * experts)
    buckets = rel_table.shape[0]
    split_at = LONG_DEV * LONG_LEN
    inputs = block_input.astype(jnp.float32)
    normed, unit_one, scale_one = normalize_forward(inputs, gain_attn)
    attn_in = normed.astype(jnp.bfloat16)
    groups = (
        (attn_in[:split_at].reshape(LONG_DEV, LONG_LEN, width), item_lengths[0, :LONG_DEV]),
        (attn_in[split_at:].reshape(SHORT_DEV, SHORT_LEN, width), item_lengths[0, LONG_DEV:]),
    )
    kept = []
    mixed_parts = []
    for items, lengths in groups:
        onehot = bucket_onehot(items.shape[1], buckets)
        bias = jnp.einsum("qkb,bh->hqk", onehot, rel_table, precision=HIGHEST)
        proj, mixed, log_total = attention_forward(items, lengths, w_qkv, bias)
        kept.append((proj, log_total, lengths, bias, onehot))
        mixed_parts.append(mixed)
    mixed_all = jnp.concatenate(mixed_parts, axis=0)
    attn = jnp.dot(mixed_all, w_attn_out, preferred_element_type=jnp.float32)
    resid = inputs + attn
    second, unit_two, scale_two = normalize_forward(resid, gain_moe)
    moe_in = second.astype(jnp.bfloat16)
    logits = jnp.dot(moe_in, w_router, preferred_element_type=jnp.float32)
    labels = jnp.arange(experts, dtype=jnp.int32)
    picks = [routes[:, rank : rank + 1] == labels[None, :] for rank in range(TOP)]
    chosen = jnp.stack([jnp.sum(jnp.where(pick, logits, 0.0), axis=1) for pick in picks], axis=1)
    highest = jnp.max(chosen, axis=1, keepdims=True)
    exps = jnp.exp(chosen - highest)
    gates = exps / jnp.sum(exps, axis=1, keepdims=True)
    flat = routes.reshape(-1)
    member = (flat[:, None] == labels[None, :]).astype(jnp.int32)
    before = jnp.cumsum(member, axis=0, dtype=jnp.int32) - member
    position = jnp.sum(before * member, axis=1)
    target = (flat * capacity + position).reshape(-1, TOP)
    places = jnp.arange(experts * capacity, dtype=jnp.int32)
    routing = [
        (target[:, rank : rank + 1] == places[None, :]).astype(jnp.bfloat16) for rank in range(TOP)
    ]
    either = routing[0]
    rank = 1
    either = either + routing[rank]
    outgoing = jnp.einsum("tp,td->pd", either, moe_in, preferred_element_type=jnp.float32)
    outgoing = outgoing.astype(jnp.bfloat16).reshape(experts, capacity, width)
    received = lax.all_to_all(outgoing, "expert", split_axis=0, concat_axis=0, tiled=True)
    sources = received.shape[0] // local
    slots = received.shape[1]
    grouped = received.reshape(sources, local, slots, width)
    gate_pre = jnp.einsum("nekd,edf->nekf", grouped, w_gate, preferred_element_type=jnp.float32)
    up_pre = jnp.einsum("nekd,edf->nekf", grouped, w_up, preferred_element_type=jnp.float32)
    hidden = gated_product(gate_pre, up_pre).astype(jnp.bfloat16)
    result = jnp.einsum("nekf,efd->nekd", hidden, w_down, preferred_element_type=jnp.float32)
    result = result.astype(jnp.bfloat16).reshape(received.shape)
    returned = lax.all_to_all(result, "expert", split_axis=0, concat_axis=0, tiled=True)
    inner_shape = (sources * local, slots, -1)
    combined, arrived, gate_pre, up_pre, hidden = (
        returned,
        received,
        gate_pre.reshape(inner_shape),
        up_pre.reshape(inner_shape),
        hidden.reshape(inner_shape),
    )
    combined_flat = combined.reshape(experts * capacity, width)
    picked = [
        jnp.dot(route, combined_flat, preferred_element_type=jnp.float32) for route in routing
    ]
    mixture = gates[:, 0:1] * picked[0]
    rank = 1
    mixture = mixture + gates[:, rank : rank + 1] * picked[rank]
    output = (resid + mixture).astype(jnp.bfloat16)
    upstream = cotangent.astype(jnp.float32)
    sendback = jnp.zeros((experts * capacity, width), jnp.float32)
    for rank in range(TOP):
        gated = (gates[:, rank : rank + 1] * upstream).astype(jnp.bfloat16)
        sendback = sendback + jnp.einsum(
            "tp,td->pd", routing[rank], gated, preferred_element_type=jnp.float32
        )
    sendback = sendback.astype(jnp.bfloat16).reshape(experts, capacity, width)
    gate_grads = [jnp.sum(upstream * picked[rank], axis=1) for rank in range(TOP)]
    average = gates[:, 0] * gate_grads[0]
    rank = 1
    average = average + gates[:, rank] * gate_grads[rank]
    dlogits = jnp.zeros_like(logits)
    for rank in range(TOP):
        logit_grad = gates[:, rank] * (gate_grads[rank] - average)
        dlogits = dlogits + jnp.where(picks[rank], logit_grad[:, None], 0.0)
    dlogits = dlogits.astype(jnp.bfloat16)
    router_grad = jnp.einsum("td,te->de", moe_in, dlogits, preferred_element_type=jnp.float32)
    moe_in_grad = jnp.einsum("te,de->td", dlogits, w_router, preferred_element_type=jnp.float32)
    arriving = lax.all_to_all(sendback, "expert", split_axis=0, concat_axis=0, tiled=True)
    sources = arriving.shape[0] // local
    slots = arriving.shape[1]
    grads_grouped = arriving.reshape(sources, local, slots, width)
    rows_grouped = arrived.reshape(sources, local, slots, width)
    hidden_grouped = hidden.reshape(sources, local, slots, -1)
    hidden_grad = jnp.einsum(
        "nekd,efd->nekf", grads_grouped, w_down, preferred_element_type=jnp.float32
    )
    down_grad = jnp.einsum(
        "nekf,nekd->efd", hidden_grouped, grads_grouped, preferred_element_type=jnp.float32
    )
    _, pullback = jax.vjp(
        gated_product, gate_pre.reshape(hidden_grouped.shape), up_pre.reshape(hidden_grouped.shape)
    )
    gate_pre_grad, up_pre_grad = pullback(hidden_grad)
    gate_pre_grad = gate_pre_grad.astype(jnp.bfloat16)
    up_pre_grad = up_pre_grad.astype(jnp.bfloat16)
    gate_grad = jnp.einsum(
        "nekd,nekf->edf", rows_grouped, gate_pre_grad, preferred_element_type=jnp.float32
    )
    up_grad = jnp.einsum(
        "nekd,nekf->edf", rows_grouped, up_pre_grad, preferred_element_type=jnp.float32
    )
    pair_grad = jnp.einsum(
        "nekf,edf->nekd", gate_pre_grad, w_gate, preferred_element_type=jnp.float32
    )
    pair_grad = pair_grad + jnp.einsum(
        "nekf,edf->nekd", up_pre_grad, w_up, preferred_element_type=jnp.float32
    )
    pair_grad = pair_grad.astype(jnp.bfloat16).reshape(arriving.shape)
    back_rows = lax.all_to_all(
        pair_grad, "expert", split_axis=0, concat_axis=0, tiled=True
    ).reshape(experts * capacity, width)
    moe_in_grad = moe_in_grad + jnp.einsum(
        "tp,pd->td", either, back_rows, preferred_element_type=jnp.float32
    )
    resid_norm_grad, gain_moe_grad = normalize_backward(moe_in_grad, unit_two, scale_two, gain_moe)
    resid_grad = upstream + resid_norm_grad
    attn_grad = resid_grad.astype(jnp.bfloat16)
    out_weight_grad = jnp.einsum(
        "te,td->ed", mixed_all, attn_grad, preferred_element_type=jnp.float32
    )
    mixed_grad = jnp.einsum(
        "td,ed->te", attn_grad, w_attn_out, preferred_element_type=jnp.float32
    ).astype(jnp.bfloat16)
    pieces = (mixed_grad[:split_at], mixed_grad[split_at:])
    proj_parts = []
    table_grad = jnp.zeros(rel_table.shape, jnp.float32)
    for saved, piece in zip(kept, pieces):
        proj, log_total, lengths, bias, onehot = saved
        proj_grad, table_part = attention_backward(proj, log_total, lengths, bias, onehot, piece)
        proj_parts.append(proj_grad)
        table_grad = table_grad + table_part
    proj_grad_all = jnp.concatenate(proj_parts, axis=0)
    qkv_grad = jnp.einsum("td,te->de", attn_in, proj_grad_all, preferred_element_type=jnp.float32)
    attn_in_grad = jnp.einsum("te,de->td", proj_grad_all, w_qkv, preferred_element_type=jnp.float32)
    input_norm_grad, gain_attn_grad = normalize_backward(
        attn_in_grad, unit_one, scale_one, gain_attn
    )
    input_grad = resid_grad + input_norm_grad
    shared = (
        qkv_grad,
        out_weight_grad,
        table_grad.reshape(-1),
        gain_attn_grad,
        gain_moe_grad,
        router_grad,
    )
    shared = (
        lax.psum_scatter(shared[0], ("dp", "expert"), scatter_dimension=0, tiled=True),
        lax.psum_scatter(shared[1], ("dp", "expert"), scatter_dimension=0, tiled=True),
        lax.psum_scatter(shared[2], ("dp", "expert"), scatter_dimension=0, tiled=True),
        lax.psum_scatter(shared[3], ("dp", "expert"), scatter_dimension=0, tiled=True),
        lax.psum_scatter(shared[4], ("dp", "expert"), scatter_dimension=0, tiled=True),
        lax.psum_scatter(shared[5], ("dp", "expert"), scatter_dimension=0, tiled=True),
    )
    expert_sums = (
        lax.psum_scatter(
            gate_grad.astype(jnp.bfloat16), "dp", scatter_dimension=2, tiled=True
        ).astype(jnp.float32),
        lax.psum_scatter(
            up_grad.astype(jnp.bfloat16), "dp", scatter_dimension=2, tiled=True
        ).astype(jnp.float32),
        lax.psum_scatter(
            down_grad.astype(jnp.bfloat16), "dp", scatter_dimension=2, tiled=True
        ).astype(jnp.float32),
    )
    return (
        output,
        input_grad,
        shared[0],
        shared[1],
        shared[2],
        shared[3],
        shared[4],
        shared[5],
        expert_sums[0],
        expert_sums[1],
        expert_sums[2],
    )


def solution(mesh):
    return jax.shard_map(
        on_device,
        mesh=mesh,
        in_specs=(
            P(("dp", "expert"), None),
            P(("dp", "expert"), None),
            P(("dp", "expert"), None),
            P(),
            P(),
            P(),
            P(),
            P(),
            P(),
            P("expert", None, None),
            P("expert", None, None),
            P("expert", None, None),
            P(("dp", "expert"), None),
        ),
        out_specs=(
            P(("dp", "expert"), None),
            P(("dp", "expert"), None),
            P(("dp", "expert"), None),
            P(("dp", "expert"), None),
            P(("dp", "expert")),
            P(("dp", "expert")),
            P(("dp", "expert")),
            P(("dp", "expert"), None),
            P("expert", None, "dp"),
            P("expert", None, "dp"),
            P("expert", None, "dp"),
        ),
        check_vma=False,
    )
```

profile of v0, /device:TPU:0, one launch (start us, length us, event | category | flops | bytes accessed | tf_op | source)
XLA Modules:
  0.0 1047.9 jit_solution(16198955926232588722)
XLA Ops:
  51.8 15.0 %fusion = f32[512,512,16]{0,2,1:T(8,128)} fusion(s32[512,512]{0,1:T(8,128)} %fusion.109, f32[32,16]{0,1:T(8,128)S(1)} %copy-done.53), kind=kOutput, calls=%fused_computation.2 | convolution fusion | flops 1619001344 | bytes 17827840 | tf_op jit(solution)/shard_map/qkb,bh->hqk/dot_general | solution.py:148
  66.8 23.3 %fusion.160 = (f32[16,512]{1,0:T(8,128)S(1)}, f32[16,512,512]{1,2,0:T(8,128)}) fusion(f32[512,512,16]{0,2,1:T(8,128)} %fusion, bf16[1,512,3,16,64]{1,4,3,2,0:T(8,128)(2,1)S(1)} %bitcast.285, pred[512]{0:T(512)(128)(4,1)S(1)} %copy-done.68), kind=kOutput, calls=%fused_computation.248 | convolution fusion | flops 553639936 | bytes 35684864 | tf_op jit(solution)/shard_map/nqhd,nkhd->nhqk/dot_general | solution.py:63
  114.4 80.6 %all_to_all.20 = bf16[8,200,1024]{2,1,0:T(8,128)(2,1)S(1)} all-to-all(bf16[8,200,1024]{2,1,0:T(8,128)(2,1)S(1)} %bitcast.302), channel_id=1, replica_groups=mesh['dp'=4,'expert'=8] {'expert'}, dimensions={0} | all-to-all | bytes 6553600 | tf_op jit(solution)/shard_map/all_to_all | solution.py:178
  195.1 13.4 %fusion.35 = f32[8,200,2816]{2,1,0:T(8,128)S(1)} fusion(bf16[8,200,1024]{2,1,0:T(8,128)(2,1)S(1)} %all_to_all.20, bf16[1,1024,2816]{2,1,0:T(8,128)(2,1)} %param.23), kind=kOutput, calls=%fused_computation.59 | convolution fusion | flops 9227468800 | bytes 27066368 | tf_op jit(solution)/shard_map/nekd,edf->nekf/dot_general | solution.py:183
  208.5 18.9 %fusion.38 = f32[8,200,2816]{2,1,0:T(8,128)} fusion(bf16[8,200,1024]{2,1,0:T(8,128)(2,1)S(1)} %all_to_all.20, bf16[1,1024,2816]{2,1,0:T(8,128)(2,1)} %param.22), kind=kOutput, calls=%fused_computation.62 | convolution fusion | flops 9227468800 | bytes 27066368 | tf_op jit(solution)/shard_map/nekd,edf->nekf/dot_general | solution.py:182
  227.4 13.6 %fusion.17 = bf16[8,200,2816]{2,1,0:T(8,128)(2,1)} fusion(f32[8,200,2816]{2,1,0:T(8,128)S(1)} %fusion.35, f32[8,200,2816]{2,1,0:T(8,128)} %fusion.38), kind=kLoop, calls=%fused_computation.38 | loop fusion | flops 45056000 | bytes 45056000 | tf_op jit(solution)/shard_map/reshape.71
  241.0 15.1 %fusion.67 = bf16[8,200,1024]{2,1,0:T(8,128)(2,1)} fusion(bf16[8,200,2816]{2,1,0:T(8,128)(2,1)} %fusion.17, bf16[1,2816,1024]{2,1,0:T(8,128)(2,1)} %param.24), kind=kOutput, calls=%fused_computation.112 | convolution fusion | flops 9229107200 | bytes 18055168 | tf_op jit(solution)/shard_map/nekf,efd->nekd/dot_general | solution.py:185
  261.3 73.7 %all-to-all-done.1 = bf16[8,200,1024]{2,1,0:T(8,128)(2,1)} async-done(((bf16[8,200,1024]{2,1,0:T(8,128)(2,1)}), bf16[8,200,1024]{2,1,0:T(8,128)(2,1)}, u32[]{:S(2)}, u32[]{:S(2)}) %all-to-all-start.1) | async-done | bytes 3276832 | tf_op jit(solution)/shard_map/all_to_all | solution.py:187
  360.8 75.8 %all-to-all-done.2 = bf16[8,200,1024]{2,1,0:T(8,128)(2,1)} async-done(((bf16[8,200,1024]{2,1,0:T(8,128)(2,1)}), bf16[8,200,1024]{2,1,0:T(8,128)(2,1)}, u32[]{:S(2)}, u32[]{:S(2)}) %all-to-all-start.2) | async-done | bytes 3276832 | tf_op jit(solution)/shard_map/all_to_all | solution.py:223
  436.7 16.7 %fusion.29 = f32[8,200,2816]{2,1,0:T(8,128)} fusion(bf16[8,200,1024]{2,1,0:T(8,128)(2,1)} %all-to-all-done.2, bf16[1,2816,1024]{2,1,0:T(8,128)(2,1)} %param.24), kind=kOutput, calls=%fused_computation.53 | convolution fusion | flops 9227468800 | bytes 27066368 | tf_op jit(solution)/shard_map/nekd,efd->nekf/dot_general | solution.py:229
  453.4 26.6 %fusion.18 = (bf16[8,200,2816]{2,1,0:T(8,128)(2,1)}, bf16[8,1,200,2816]{3,2,0,1:T(8,128)(2,1)S(1)}) fusion(f32[8,200,2816]{2,1,0:T(8,128)} %fusion.29, f32[8,200,2816]{2,1,0:T(8,128)} %fusion.38, f32[8,200,2816]{2,1,0:T(8,128)} %copy-done.2), kind=kLoop, calls=%fused_computation.39 | loop fusion | flops 126156800 | bytes 72089600 | tf_op jit(solution)/shard_map/reshape.80
  483.5 12.9 %fusion.28 = bf16[1,1024,2816]{2,1,0:T(8,128)(2,1)} fusion(bf16[8,200,1024]{2,1,0:T(8,128)(2,1)S(1)} %copy-done.18, bf16[8,1,200,2816]{3,2,0,1:T(8,128)(2,1)S(1)} %get-tuple-element.86), kind=kOutput, calls=%fused_computation.50 | convolution fusion | flops 9230352384 | bytes 18055168 | tf_op jit(solution)/shard_map/nekd,nekf->edf/dot_general | solution.py:241
  496.4 26.6 %copy.153 = bf16[1,1024,2816]{1,0,2:T(2,128)(2,1)} copy(bf16[1,1024,2816]{2,1,0:T(8,128)(2,1)} %fusion.28) | data formatting | bytes 11534336
  532.2 16.6 %fusion.42 = bf16[1,1024,2816]{2,1,0:T(8,128)(2,1)} fusion(bf16[8,200,1024]{2,1,0:T(8,128)(2,1)} %copy-done.17, bf16[8,200,2816]{2,1,0:T(8,128)(2,1)} %get-tuple-element.85), kind=kOutput, calls=%fused_computation.69 | convolution fusion | flops 9230352384 | bytes 18055168 | tf_op jit(solution)/shard_map/nekd,nekf->edf/dot_general | solution.py:244
  548.8 26.7 %copy.155 = bf16[1,1024,2816]{1,0,2:T(2,128)(2,1)} copy(bf16[1,1024,2816]{2,1,0:T(8,128)(2,1)} %fusion.42) | data formatting | bytes 11534336
  585.6 16.2 %fusion.43 = bf16[1,2816,1024]{2,1,0:T(8,128)(2,1)} fusion(bf16[8,200,2816]{2,1,0:T(8,128)(2,1)} %fusion.17, bf16[8,200,1024]{2,1,0:T(8,128)(2,1)} %all-to-all-done.2), kind=kOutput, calls=%fused_computation.70 | convolution fusion | flops 9230352384 | bytes 18055168 | tf_op jit(solution)/shard_map/nekf,nekd->efd/dot_general | solution.py:232
  601.9 13.7 %fusion.21 = f32[8,200,1024]{2,1,0:T(8,128)S(1)} fusion(bf16[8,1,200,2816]{3,2,0,1:T(8,128)(2,1)} %copy-done.13, bf16[1,1024,2816]{2,1,0:T(8,128)(2,1)} %param.22), kind=kOutput, calls=%fused_computation.42 | convolution fusion | flops 9227468800 | bytes 21331968 | tf_op jit(solution)/shard_map/nekf,edf->nekd/dot_general | solution.py:247
  615.6 14.1 %add_convert_fusion = bf16[8,200,1024]{2,1,0:T(8,128)(2,1)S(1)} fusion(f32[8,200,1024]{2,1,0:T(8,128)S(1)} %fusion.21, bf16[8,200,2816]{2,1,0:T(8,128)(2,1)} %get-tuple-element.85, bf16[1,1024,2816]{2,1,0:T(8,128)(2,1)} %param.23), kind=kOutput, calls=%fused_computation.48 | convolution fusion | flops 9230745600 | bytes 24608768 | tf_op jit(solution)/shard_map/nekf,edf->nekd/dot_general | solution.py:250
  629.8 76.8 %all_to_all.21 = bf16[8,200,1024]{2,1,0:T(8,128)(2,1)S(1)} all-to-all(bf16[8,200,1024]{2,1,0:T(8,128)(2,1)S(1)} %add_convert_fusion), channel_id=1, replica_groups=mesh['dp'=4,'expert'=8] {'expert'}, dimensions={0} | all-to-all | bytes 6553600 | tf_op jit(solution)/shard_map/all_to_all | solution.py:254
  733.6 11.0 %multiply_reduce_fusion = (f32[16,512]{1,0:T(8,128)S(1)}, f32[16,512,512]{1,2,0:T(8,128)}) fusion(f32[16,512,512]{1,2,0:T(8,128)} %get-tuple-element.94, f32[16,512]{1,0:T(8,128)S(1)} %log_add_fusion, bf16[512,16,64]{0,2,1:T(8,128)(2,1)S(1)} %bitcast.293, bf16[1,512,3,16,64]{1,4,3,2,0:T(8,128)(2,1)S(1)} %bitcast.286), kind=kOutput, calls=%fused_computation.27 | convolution fusion | flops 549445632 | bytes 35717120 | tf_op jit(solution)/shard_map/nqhd,nkhd->nhqk/dot_general | solution.py:94
  744.7 11.8 %multiply_convert_fusion = bf16[16,512,512]{1,2,0:T(8,128)(2,1)S(1)} fusion(f32[16,512,512]{1,2,0:T(8,128)} %get-tuple-element.102, f32[16,512,512]{1,2,0:T(8,128)} %get-tuple-element.94, f32[16,512]{1,0:T(8,128)S(1)} %get-tuple-element.101, f32[16,512]{1,0:T(8,128)S(1)} %log_add_fusion), kind=kLoop, calls=%fused_computation.26 | loop fusion | flops 16777216 | bytes 42008576 | tf_op jit(solution)/shard_map/convert_element_type | solution.py:101
  781.1 13.0 %fusion.106 = f32[32,16]{0,1:T(8,128)S(1)} fusion(bf16[16,512,512]{1,2,0:T(8,128)(2,1)} %copy-done.1, s32[512,512]{0,1:T(8,128)} %fusion.109), kind=kOutput, calls=%fused_computation.152 | convolution fusion | flops 293601280 | bytes 9439232 | tf_op jit(solution)/shard_map/nhqk,qkb->bh/dot_general | solution.py:102
  805.1 39.8 %all-reduce.3 = (f32[512]{0:T(512)S(1)}, f32[1024]{0:T(1024)S(1)}, f32[1024]{0:T(1024)S(1)}) all-reduce(f32[512]{0:T(512)S(1)} %reshape.522, f32[1024]{0:T(1024)S(1)} %get-tuple-element.68, f32[1024]{0:T(1024)S(1)} %get-tuple-element.66), channel_id=4, replica_groups=mesh['dp'=4,'expert'=8] {'dp','expert'}, use_global_device_ids=true, to_apply=%region_20.21.clone | all-reduce | flops 2560 | bytes 20480
  885.6 155.0 %reduce-scatter.13.cloned.1.call-done = f32[32,3072]{1,0:T(8,128)} async-done(((f32[1024,3072]{1,0:T(8,128)}), f32[32,3072]{1,0:T(8,128)}) %reduce-scatter.13.cloned.1.call-update) | async-done | bytes 393232 | tf_op jit(solution)/shard_map/reduce_scatter | solution.py:293
  (260 shorter events, 225.1 us)
Async XLA Ops:
  7.2 100.5 %copy-start = (bf16[1024,1024]{1,0:T(8,128)(2,1)S(1)}, bf16[1024,1024]{1,0:T(8,128)(2,1)}, u32[]{:S(2)}) copy-start(bf16[1024,1024]{1,0:T(8,128)(2,1)} %param.17) | copy-start | bytes 6291460
  7.3 34.5 %copy-start.30 = (s32[128,128]{0,1:T(8,128)}, s32[128,128]{0,1:T(8,128)S(1)}, u32[]{:S(2)}) copy-start(s32[128,128]{0,1:T(8,128)S(1)} %fusion.133) | copy-start | bytes 196612
  20.9 18.5 %copy-start.44 = (s32[640,2]{0,1:T(2,128)S(1)}, s32[640,2]{0,1:T(2,128)}, u32[]{:S(2)}) copy-start(s32[640,2]{0,1:T(2,128)} %param.14) | copy-start | bytes 15364
  20.9 20.9 %copy-start.53 = (f32[32,16]{0,1:T(8,128)S(1)}, f32[32,16]{0,1:T(8,128)}, u32[]{:S(2)}) copy-start(f32[32,16]{0,1:T(8,128)} %param.18) | copy-start | bytes 6148
  39.5 307.4 %copy-start.64 = (s32[640]{0:T(1024)}, s32[640]{0:T(1024)S(1)}, u32[]{:S(2)}) copy-start(s32[640]{0:T(1024)S(1)} %get-tuple-element.81) | copy-start | bytes 7684
  39.5 310.4 %copy-start.62 = (s32[640]{0:T(1024)}, s32[640]{0:T(1024)S(1)}, u32[]{:S(2)}) copy-start(s32[640]{0:T(1024)S(1)} %get-tuple-element.80) | copy-start | bytes 7684
  51.8 15.0 %copy-start.3 = (bf16[512,3072]{0,1:T(8,128)(2,1)S(1)}, bf16[512,3072]{0,1:T(8,128)(2,1)}, u32[]{:S(2)}) copy-start(bf16[512,3072]{0,1:T(8,128)(2,1)} %copy.121) | copy-start | bytes 9437188
  51.8 15.0 %copy-start.68 = (pred[512]{0:T(512)(128)(4,1)S(1)}, pred[512]{0:T(512)(128)(4,1)}, u32[]{:S(2)}) copy-start(pred[512]{0:T(512)(128)(4,1)} %iota_compare_fusion.16) | copy-start | bytes 1540
  208.5 18.9 %copy-start.2 = (f32[8,200,2816]{2,1,0:T(8,128)}, f32[8,200,2816]{2,1,0:T(8,128)S(1)}, u32[]{:S(2)}) copy-start(f32[8,200,2816]{2,1,0:T(8,128)S(1)} %fusion.35) | copy-start | bytes 54067204
  256.1 79.0 %all-to-all-start.1 = ((bf16[8,200,1024]{2,1,0:T(8,128)(2,1)}), bf16[8,200,1024]{2,1,0:T(8,128)(2,1)}, u32[]{:S(2)}, u32[]{:S(2)}) async-start(bf16[8,200,1024]{2,1,0:T(8,128)(2,1)} %fusion.67), calls=%async_computation.1 | async-start | bytes 6553600 | tf_op jit(solution)/shard_map/all_to_all | solution.py:187
  260.7 98.6 %copy-start.38 = (s32[640]{0:T(1024)}, s32[640]{0:T(1024)S(1)}, u32[]{:S(2)}) copy-start(s32[640]{0:T(1024)S(1)} %get-tuple-element.78) | copy-start | bytes 7684
  260.8 98.6 %copy-start.40 = (s32[640]{0:T(1024)}, s32[640]{0:T(1024)S(1)}, u32[]{:S(2)}) copy-start(s32[640]{0:T(1024)S(1)} %get-tuple-element.79) | copy-start | bytes 7684
  354.8 81.9 %all-to-all-start.2 = ((bf16[8,200,1024]{2,1,0:T(8,128)(2,1)}), bf16[8,200,1024]{2,1,0:T(8,128)(2,1)}, u32[]{:S(2)}, u32[]{:S(2)}) async-start(bf16[8,200,1024]{2,1,0:T(8,128)(2,1)} %bitcast.300), calls=%async_computation.2 | async-start | bytes 6553600 | tf_op jit(solution)/shard_map/all_to_all | solution.py:223
  359.3 420.4 %reduce-scatter.19.cloned.1.call-start = ((), (), s32[]{:S(2)}) async-start(), calls=%async_computation.13 | async-start | bytes 540672
  360.8 490.5 %reduce-scatter.21.cloned.1.call-start = ((), (), s32[]{:S(2)}) async-start(), calls=%async_computation.14 | async-start | bytes 7208960
  453.4 30.1 %copy-start.18 = (bf16[8,200,1024]{2,1,0:T(8,128)(2,1)S(1)}, bf16[8,200,1024]{2,1,0:T(8,128)(2,1)}, u32[]{:S(2)}) copy-start(bf16[8,200,1024]{2,1,0:T(8,128)(2,1)} %copy-done.17) | copy-start | bytes 9830404
  532.1 334.7 %reduce-scatter.23.cloned.1.call-start = ((), (), s32[]{:S(2)}) async-start(), calls=%async_computation.15 | async-start | bytes 7208960
  585.6 296.8 %reduce-scatter.17.cloned.1.call-start = ((), (), s32[]{:S(2)}) async-start(), calls=%async_computation.12 | async-start | bytes 7208960 | tf_op jit(solution)/shard_map/reduce_scatter | solution.py:307
  601.9 283.7 %reduce-scatter.15.cloned.1.call-start = ((), (), s32[]{:S(2)}) async-start(), calls=%async_computation.11 | async-start | bytes 4325376 | tf_op jit(solution)/shard_map/reduce_scatter | solution.py:294
  629.8 76.8 %copy-start.63 = (s32[640]{0:T(1024)S(1)}, s32[640]{0:T(1024)}, u32[]{:S(2)}) copy-start(s32[640]{0:T(1024)} %copy-done.62) | copy-start | bytes 7684
  629.8 76.8 %copy-start.65 = (s32[640]{0:T(1024)S(1)}, s32[640]{0:T(1024)}, u32[]{:S(2)}) copy-start(s32[640]{0:T(1024)} %copy-done.64) | copy-start | bytes 7684
  719.9 320.7 %reduce-scatter.13.cloned.1.call-start = ((), (), s32[]{:S(2)}) async-start(), calls=%async_computation.10 | async-start | bytes 12976128 | tf_op jit(solution)/shard_map/reduce_scatter | solution.py:293
  732.3 37.7 %copy-start.27 = (bf16[1,128,3,16,64]{1,4,3,2,0:T(8,128)(2,1)}, bf16[1,128,3,16,64]{1,4,3,2,0:T(8,128)(2,1)S(1)}, u32[]{:S(2)}) copy-start(bf16[1,128,3,16,64]{1,4,3,2,0:T(8,128)(2,1)S(1)} %pad_maximum_fusion.7) | copy-start | bytes 2359300
  781.1 13.7 %copy-start.57 = (f32[1024]{0:T(1024)S(1)}, f32[1024]{0:T(1024)}, u32[]{:S(2)}) copy-start(f32[1024]{0:T(1024)} %param.19) | copy-start | bytes 12292
  (59 other events, 289.4 us)
Sparse Core Ops, SparseCore 0:
  362.4 137.8 reduce-scatter.18
  532.3 64.7 reduce-scatter.20
  600.3 65.7 reduce-scatter.22
  669.2 65.7 reduce-scatter.16
  737.9 142.7 reduce-scatter.14
  888.2 152.3 reduce-scatter.12
where the time goes:
time: 1060 us; the launch traced here: 1050 us
  waiting for transfers between devices  305 us (29%)
  matrix products  295 us (28%)
  blocking collectives  197 us (19%)
  local copies, waits for them, and re-layouts  141 us (13%)
  other arithmetic  85.1 us (8%)
  between operations  15.7 us (1%)
    reduce_scatter x1, waiting for transfers between devices, on_device(): lax.psum_scatter(shared[0], ('dp', 'expert'), scatter_dimension=0, tiled=...  155 us
    unnamed x165, local copies, waits for them, and re-layouts  122 us
    all_to_all x1, blocking collectives, on_device(): lax.all_to_all(outgoing, 'expert', split_axis=0, concat_axis=0, tiled=True)  80.6 us
    all_to_all x1, blocking collectives, on_device(): lax.all_to_all(pair_grad, 'expert', split_axis=0, concat_axis=0, tiled=True)  76.8 us
    all_to_all x1, waiting for transfers between devices, on_device(): lax.all_to_all(sendback, 'expert', split_axis=0, concat_axis=0, tiled=True)  75.8 us
    all_to_all x1, waiting for transfers between devices, on_device(): lax.all_to_all(result, 'expert', split_axis=0, concat_axis=0, tiled=True)  73.7 us
    another operation x4, other arithmetic  45.9 us
    unnamed x1, blocking collectives  39.8 us
  transfers between devices with their start and end apart: 8, of which 3 were waited for; matrix products, arithmetic and copies ran while one was open for 31% of the time, Pallas kernels for 0%

commit v1 on v0

v1 whole, which is shorter than its diff:
```python
import jax
import jax.numpy as jnp
from jax import lax
from jax.experimental import pallas as pl
from jax.experimental.pallas import tpu as pltpu
from jax.sharding import PartitionSpec as P

TOP = 2
LONG_LEN = 512
SHORT_LEN = 128
TOK_DEV = 640
BOUNDS = (12, 16, 23, 32, 46, 64, 91)
EPSILON = 1e-06
HIGHEST = lax.Precision.HIGHEST
TILE = 128
FT = 256
NEG = -1e30
NN = (((1,), (0,)), ((), ()))
NT = (((1,), (1,)), ((), ()))
TN = (((0,), (0,)), ((), ()))
CURVE = 0.7978845608028654
CUBE = 0.044715


def dot(a, b, dims=NN):
    return lax.dot_general(a, b, dims, preferred_element_type=jnp.float32)


def normalize_forward(value, gain):
    scale = lax.rsqrt(jnp.mean(value * value, axis=-1, keepdims=True) + EPSILON)
    unit = value * scale
    return (unit * gain, unit, scale)


def normalize_backward(grad, unit, scale, gain):
    gain_grad = jnp.sum(grad * unit, axis=0)
    along = grad * gain
    inner = jnp.mean(along * unit, axis=-1, keepdims=True)
    return (scale * (along - unit * inner), gain_grad)


def bias_strip(bias_row):
    wide = jnp.broadcast_to(bias_row, (TILE, bias_row.shape[1]))
    return pltpu.roll(wide, 0, 1, stride=1, stride_axis=0)


def bias_tile(strip, bias_row, step):
    if abs(step) <= 1:
        start = 2 * TILE - step * TILE
        return strip[:, start : start + TILE]
    last = bias_row.shape[1] - 1
    return bias_row[:, 0:1] if step > 0 else bias_row[:, last : last + 1]


def items_of(tokens, lengths_ref):
    return ((0, LONG_LEN, lengths_ref[0, 0], LONG_LEN // 2), (LONG_LEN, tokens, lengths_ref[0, 1], SHORT_LEN // 2))


def attention_forward_kernel(lengths_ref, bias_ref, q_ref, k_ref, v_ref, mixed_ref, stat_ref, score_ref, exp_ref):
    tokens, lanes = q_ref.shape
    size = lanes // 2
    lane = lax.broadcasted_iota(jnp.int32, (1, lanes), 1)
    values_t = v_ref[...].T
    for start, stop, visible, sure in items_of(tokens, lengths_ref):
        length = stop - start
        count = length // TILE
        outs = []
        for head in range(2):
            bias_row = bias_ref[0, head : head + 1, :]
            strip = bias_strip(bias_row)
            own = (lane >= head * size) & (lane < (head + 1) * size)
            query = jnp.where(own, q_ref[start:stop, :] * 0.125, 0.0).astype(jnp.bfloat16)
            score_ref[0:length, 0:length] = dot(k_ref[start:stop, :], query, NT)
            totals = []
            for col in range(count):
                cols = slice(col * TILE, (col + 1) * TILE)
                top = None
                for row in range(count):
                    rows = slice(row * TILE, (row + 1) * TILE)
                    tile = score_ref[rows, cols] + bias_tile(strip, bias_row, row - col)
                    if (row + 1) * TILE > sure:
                        place = lax.broadcasted_iota(jnp.int32, (TILE, 1), 0) + row * TILE
                        tile = jnp.where(place < visible, tile, NEG)
                    score_ref[rows, cols] = tile
                    peak = jnp.max(tile, axis=0, keepdims=True)
                    top = peak if top is None else jnp.maximum(top, peak)
                total = jnp.zeros((1, TILE), jnp.float32)
                for row in range(count):
                    rows = slice(row * TILE, (row + 1) * TILE)
                    tile = jnp.exp(score_ref[rows, cols] - top)
                    total = total + jnp.sum(tile, axis=0, keepdims=True)
                    exp_ref[rows, cols] = tile.astype(jnp.bfloat16)
                totals.append(total)
                stat_ref[0, head : head + 1, start + col * TILE : start + (col + 1) * TILE] = top + jnp.log(total)
            total = jnp.concatenate(totals, axis=1)
            out = dot(values_t[head * size : (head + 1) * size, start:stop], exp_ref[0:length, 0:length])
            outs.append(out / total)
        mixed_ref[start:stop, :] = jnp.concatenate(outs, axis=0).T.astype(jnp.bfloat16)


def attention_forward(lengths, bias, proj):
    tokens, width = proj.shape[0], proj.shape[1] // 3
    lanes = TILE
    pairs = width // lanes
    return pl.pallas_call(
        attention_forward_kernel,
        grid=(pairs,),
        in_specs=[
            pl.BlockSpec(memory_space=pltpu.SMEM),
            pl.BlockSpec((1, 2, bias.shape[2]), lambda p: (p, 0, 0)),
            pl.BlockSpec((tokens, lanes), lambda p: (0, p)),
            pl.BlockSpec((tokens, lanes), lambda p: (0, pairs + p)),
            pl.BlockSpec((tokens, lanes), lambda p: (0, 2 * pairs + p)),
        ],
        out_specs=[
            pl.BlockSpec((tokens, lanes), lambda p: (0, p)),
            pl.BlockSpec((1, 2, tokens), lambda p: (p, 0, 0)),
        ],
        out_shape=[
            jax.ShapeDtypeStruct((tokens, width), jnp.bfloat16),
            jax.ShapeDtypeStruct((pairs, 2, tokens), jnp.float32),
        ],
        scratch_shapes=[pltpu.VMEM((LONG_LEN, LONG_LEN), jnp.float32), pltpu.VMEM((LONG_LEN, LONG_LEN), jnp.bfloat16)],
        name="attention_forward",
    )(lengths, bias, proj, proj, proj)


def attention_backward_kernel(
    lengths_ref, bias_ref, stat_ref, q_ref, k_ref, v_ref, mixed_ref, grad_ref, proj_ref, table_ref,
    score_ref, slope_ref, weight_ref, change_ref,
):
    tokens, lanes = q_ref.shape
    size = lanes // 2
    lane = lax.broadcasted_iota(jnp.int32, (1, lanes), 1)
    keys_t = k_ref[...].T
    product = (grad_ref[...].astype(jnp.float32) * mixed_ref[...].astype(jnp.float32)).T
    table_ref[...] = jnp.zeros_like(table_ref)
    for start, stop, visible, sure in items_of(tokens, lengths_ref):
        length = stop - start
        count = length // TILE
        query_grads, key_grads, value_grads = [], [], []
        for head in range(2):
            bias_row = bias_ref[0, head : head + 1, :]
            strip = bias_strip(bias_row)
            own = (lane >= head * size) & (lane < (head + 1) * size)
            query = jnp.where(own, q_ref[start:stop, :] * 0.125, 0.0).astype(jnp.bfloat16)
            grad = jnp.where(own, grad_ref[start:stop, :], 0.0).astype(jnp.bfloat16)
            score_ref[0:length, 0:length] = dot(k_ref[start:stop, :], query, NT)
            slope_ref[0:length, 0:length] = dot(v_ref[start:stop, :], grad, NT)
            inner = jnp.sum(product[head * size : (head + 1) * size, start:stop], axis=0, keepdims=True)
            sums = {-1: None, 0: None, 1: None}
            far = {-1: None, 1: None}
            for col in range(count):
                cols = slice(col * TILE, (col + 1) * TILE)
                base = stat_ref[0, head : head + 1, start + col * TILE : start + (col + 1) * TILE]
                middle = inner[:, cols]
                for row in range(count):
                    rows = slice(row * TILE, (row + 1) * TILE)
                    step = row - col
                    tile = score_ref[rows, cols] + (bias_tile(strip, bias_row, step) - base)
                    if (row + 1) * TILE > sure:
                        place = lax.broadcasted_iota(jnp.int32, (TILE, 1), 0) + row * TILE
                        tile = jnp.where(place < visible, tile, NEG)
                    tile = jnp.exp(tile)
                    weight_ref[rows, cols] = tile.astype(jnp.bfloat16)
                    tile = tile * (slope_ref[rows, cols] - middle)
                    change_ref[rows, cols] = tile.astype(jnp.bfloat16)
                    if abs(step) <= 1:
                        sums[step] = tile if sums[step] is None else sums[step] + tile
                    else:
                        side = 1 if step > 0 else -1
                        part = jnp.sum(tile, axis=0, keepdims=True)
                        far[side] = part if far[side] is None else far[side] + part
            for step, value in sums.items():
                if value is not None:
                    at = TILE - step * TILE
                    table_ref[0, head, 0:TILE, at : at + TILE] += value
            for side, value in far.items():
                if value is not None:
                    at = TILE - side * TILE
                    table_ref[0, head, TILE : TILE + 1, at : at + TILE] = value
            value_grads.append(dot(weight_ref[0:length, 0:length], grad))
            key_grads.append(dot(change_ref[0:length, 0:length], query))
            query_grads.append(dot(keys_t[head * size : (head + 1) * size, start:stop], change_ref[0:length, 0:length]))
        proj_ref[0, start:stop, :] = (jnp.concatenate(query_grads, axis=0).T * 0.125).astype(jnp.bfloat16)
        proj_ref[1, start:stop, :] = (key_grads[0] + key_grads[1]).astype(jnp.bfloat16)
        proj_ref[2, start:stop, :] = (value_grads[0] + value_grads[1]).astype(jnp.bfloat16)


def attention_backward(lengths, bias, stat, proj, mixed, grad):
    tokens, width = mixed.shape
    lanes = TILE
    pairs = width // lanes
    return pl.pallas_call(
        attention_backward_kernel,
        grid=(pairs,),
        in_specs=[
            pl.BlockSpec(memory_space=pltpu.SMEM),
            pl.BlockSpec((1, 2, bias.shape[2]), lambda p: (p, 0, 0)),
            pl.BlockSpec((1, 2, tokens), lambda p: (p, 0, 0)),
            pl.BlockSpec((tokens, lanes), lambda p: (0, p)),
            pl.BlockSpec((tokens, lanes), lambda p: (0, pairs + p)),
            pl.BlockSpec((tokens, lanes), lambda p: (0, 2 * pairs + p)),
            pl.BlockSpec((tokens, lanes), lambda p: (0, p)),
            pl.BlockSpec((tokens, lanes), lambda p: (0, p)),
        ],
        out_specs=[
            pl.BlockSpec((3, tokens, lanes), lambda p: (0, 0, p)),
            pl.BlockSpec((1, 2, TILE + 8, 3 * TILE), lambda p: (p, 0, 0, 0)),
        ],
        out_shape=[
            jax.ShapeDtypeStruct((3, tokens, width), jnp.bfloat16),
            jax.ShapeDtypeStruct((pairs, 2, TILE + 8, 3 * TILE), jnp.float32),
        ],
        scratch_shapes=[
            pltpu.VMEM((LONG_LEN, LONG_LEN), jnp.float32),
            pltpu.VMEM((LONG_LEN, LONG_LEN), jnp.float32),
            pltpu.VMEM((LONG_LEN, LONG_LEN), jnp.bfloat16),
            pltpu.VMEM((LONG_LEN, LONG_LEN), jnp.bfloat16),
        ],
        name="attention_backward",
    )(lengths, bias, stat, proj, proj, proj, mixed, grad)


def bucket_of(offset):
    distance = jnp.abs(offset)
    far = 8 + sum(((distance >= bound).astype(jnp.int32) for bound in BOUNDS))
    return jnp.where(distance < 8, distance, far) + 16 * (offset > 0).astype(jnp.int32)


def bias_rows(rel_table):
    bucket = bucket_of(2 * TILE - jnp.arange(4 * TILE, dtype=jnp.int32))
    onehot = (bucket[:, None] == jnp.arange(rel_table.shape[0], dtype=jnp.int32)[None, :]).astype(jnp.float32)
    return jnp.einsum("xb,bh->hx", onehot, rel_table, precision=HIGHEST).reshape(-1, 2, 4 * TILE)


def table_sums(tiles, buckets):
    row = jnp.arange(TILE + 8, dtype=jnp.int32)[:, None]
    col = jnp.arange(3 * TILE, dtype=jnp.int32)[None, :]
    near = bucket_of(row - col + TILE)
    far = jnp.where(col < TILE, buckets - 1, buckets // 2 - 1)
    bucket = jnp.where(row < TILE, near, far)
    onehot = (bucket[:, :, None] == jnp.arange(buckets, dtype=jnp.int32)).astype(jnp.float32)
    return jnp.einsum("ghrc,rcb->bgh", tiles, onehot, precision=HIGHEST).reshape(buckets, -1)


def expert_kernel(x_ref, slope_ref, wg_ref, wu_ref, hidden_ref, gate_ref, up_ref, pair_ref, dots_ref, acc_ref, *, parts):
    step = pl.program_id(0)
    rows = x_ref.shape[0] // parts

    @pl.when(step == 0)
    def _():
        acc_ref[...] = jnp.zeros_like(acc_ref)
        dots_ref[...] = jnp.zeros_like(dots_ref)

    for part in range(parts):
        span = slice(part * rows, (part + 1) * rows)
        x = x_ref[span, :]
        gate = dot(x, wg_ref[...])
        up = dot(x, wu_ref[...])
        slope = slope_ref[span, :].astype(jnp.float32)
        square = gate * gate
        turn = jnp.tanh(gate * (CURVE + (CURVE * CUBE) * square))
        rise = 0.5 + 0.5 * turn
        unit = gate * rise
        bend = rise + (0.5 * gate) * (1.0 - turn * turn) * (CURVE + (3 * CURVE * CUBE) * square)
        hidden = (unit * up).astype(jnp.bfloat16)
        hidden_ref[span, :] = hidden
        both = hidden.astype(jnp.float32) * slope
        dots_ref[span, :] += both[:, 0:TILE] + both[:, TILE : 2 * TILE]
        gate_grad = (slope * up * bend).astype(jnp.bfloat16)
        up_grad = (slope * unit).astype(jnp.bfloat16)
        gate_ref[span, :] = gate_grad
        up_ref[span, :] = up_grad
        acc_ref[span, :] += dot(gate_grad, wg_ref[...], NT) + dot(up_grad, wu_ref[...], NT)

    @pl.when(step == pl.num_programs(0) - 1)
    def _():
        pair_ref[...] = acc_ref[...].astype(jnp.bfloat16)


def expert_rows(x, slope, wg, wu, parts=4):
    n, d = x.shape
    f = wg.shape[1]
    tile = pl.BlockSpec((n, FT), lambda i: (0, i))
    weight = pl.BlockSpec((d, FT), lambda i: (0, i))
    whole = pl.BlockSpec((n, d), lambda i: (0, 0))
    return pl.pallas_call(
        lambda *refs: expert_kernel(*refs, parts=parts),
        grid=(f // FT,),
        in_specs=[whole, tile, weight, weight],
        out_specs=[tile, tile, tile, whole, pl.BlockSpec((n, TILE), lambda i: (0, 0))],
        out_shape=[jax.ShapeDtypeStruct((n, f), jnp.bfloat16)] * 3
        + [jax.ShapeDtypeStruct((n, d), jnp.bfloat16), jax.ShapeDtypeStruct((n, TILE), jnp.float32)],
        scratch_shapes=[pltpu.VMEM((n, d), jnp.float32)],
        name="expert_rows",
    )(x, slope, wg, wu)


def slope_kernel(u_ref, wd_ref, out_ref):
    out_ref[...] = dot(u_ref[...], wd_ref[...], NT).astype(jnp.bfloat16)


def slope_rows(u, wd):
    n, d = u.shape
    f = wd.shape[0]
    return pl.pallas_call(
        slope_kernel,
        grid=(f // FT,),
        in_specs=[pl.BlockSpec((n, d), lambda i: (0, 0)), pl.BlockSpec((FT, d), lambda i: (i, 0))],
        out_specs=pl.BlockSpec((n, FT), lambda i: (0, i)),
        out_shape=jax.ShapeDtypeStruct((n, f), jnp.bfloat16),
        name="slope_rows",
    )(u, wd)


def down_kernel(h_ref, u_ref, out_ref):
    out_ref[...] = dot(h_ref[...], u_ref[...], TN).astype(jnp.bfloat16)


def down_grads(h, u):
    n, f = h.shape
    d = u.shape[1]
    return pl.pallas_call(
        down_kernel,
        grid=(f // FT,),
        in_specs=[pl.BlockSpec((n, FT), lambda i: (0, i)), pl.BlockSpec((n, d), lambda i: (0, 0))],
        out_specs=pl.BlockSpec((FT, d), lambda i: (i, 0)),
        out_shape=jax.ShapeDtypeStruct((f, d), jnp.bfloat16),
        name="down_grads",
    )(h, u)


def gate_up_kernel(g_ref, p_ref, x_ref, out_ref):
    d = x_ref.shape[1]
    out_ref[:, 0:d] = dot(g_ref[...], x_ref[...], TN).astype(jnp.bfloat16)
    out_ref[:, d : 2 * d] = dot(p_ref[...], x_ref[...], TN).astype(jnp.bfloat16)


def gate_up_grads(g, p, x):
    n, f = g.shape
    d = x.shape[1]
    tile = pl.BlockSpec((n, FT), lambda i: (0, i))
    return pl.pallas_call(
        gate_up_kernel,
        grid=(f // FT,),
        in_specs=[tile, tile, pl.BlockSpec((n, d), lambda i: (0, 0))],
        out_specs=pl.BlockSpec((FT, 2 * d), lambda i: (i, 0)),
        out_shape=jax.ShapeDtypeStruct((f, 2 * d), jnp.bfloat16),
        name="gate_up_grads",
    )(g, p, x)


def on_device(
    block_input,
    routes,
    item_lengths,
    w_qkv,
    w_attn_out,
    rel_table,
    gain_attn,
    gain_moe,
    w_router,
    w_gate,
    w_up,
    w_down,
    cotangent,
):
    tokens, width = block_input.shape
    experts = w_router.shape[1]
    capacity = TOK_DEV * TOP * 5 // (4 * experts)
    buckets = rel_table.shape[0]
    slots = experts * capacity
    ways = lax.axis_size("expert")
    copies = lax.axis_size("dp")
    core = lax.axis_index("expert") % 2
    labels = jnp.arange(experts, dtype=jnp.int32)
    picks = [routes[:, rank : rank + 1] == labels[None, :] for rank in range(TOP)]
    named = (picks[0] | picks[1]).astype(jnp.bfloat16)
    ticks = jnp.arange(tokens, dtype=jnp.int32)
    earlier = (ticks[:, None] > ticks[None, :]).astype(jnp.bfloat16)
    count = dot(earlier, named)
    starts = (labels * capacity).astype(jnp.float32)
    target = [
        jnp.sum(jnp.where(pick, count + starts[None, :], 0.0), axis=1, keepdims=True).astype(jnp.int32)
        for pick in picks
    ]
    places = jnp.arange(slots, dtype=jnp.int32)
    routing = [(target[rank] == places[None, :]) for rank in range(TOP)]
    either = (routing[0] | routing[1]).astype(jnp.bfloat16)

    def pack(rows):
        return dot(either, rows, TN).astype(jnp.bfloat16)

    def exchange(rows):
        shape = rows.shape
        return lax.all_to_all(
            rows.reshape((experts, capacity) + shape[1:]), "expert", split_axis=0, concat_axis=0, tiled=True
        ).reshape(shape)

    packed = pack(cotangent)
    packed, block_input = lax.optimization_barrier((packed, block_input))
    raw = exchange(packed)
    inputs = block_input.astype(jnp.float32)
    normed, unit_one, scale_one = normalize_forward(inputs, gain_attn)
    attn_in = normed.astype(jnp.bfloat16)
    bias = bias_rows(rel_table)
    proj = dot(attn_in, w_qkv).astype(jnp.bfloat16)
    mixed, stat = attention_forward(item_lengths, bias, proj)
    attn = dot(mixed, w_attn_out)
    resid = inputs + attn
    second, unit_two, scale_two = normalize_forward(resid, gain_moe)
    moe_in = second.astype(jnp.bfloat16)
    packed = pack(moe_in)
    packed, raw = lax.optimization_barrier((packed, raw))
    rows = exchange(packed)
    logits = dot(moe_in, w_router)
    chosen = jnp.stack([jnp.sum(jnp.where(pick, logits, 0.0), axis=1) for pick in picks], axis=1)
    highest = jnp.max(chosen, axis=1, keepdims=True)
    exps = jnp.exp(chosen - highest)
    gates = exps / jnp.sum(exps, axis=1, keepdims=True)
    gated = jnp.where(routing[0], gates[:, 0:1], 0.0) + jnp.where(routing[1], gates[:, 1:2], 0.0)
    slot_gates = exchange(jnp.sum(gated, axis=0))[:, None]
    gated = gated.astype(jnp.bfloat16)
    gate_weight, up_weight, down_weight = w_gate[0], w_up[0], w_down[0]
    slope = slope_rows(raw, down_weight)
    hidden, gate_pre_grad, up_pre_grad, pair_grad, dots = expert_rows(rows, slope, gate_weight, up_weight)
    back = exchange(pair_grad)
    slot_dots = exchange(jnp.sum(dots, axis=1))[None, :]
    gated_raw = (raw.astype(jnp.float32) * slot_gates).astype(jnp.bfloat16)
    gated_rows = (rows.astype(jnp.float32) * slot_gates).astype(jnp.bfloat16)
    down_grad = down_grads(hidden, gated_raw)
    down_sum = lax.psum_scatter(down_grad, "dp", scatter_dimension=1, tiled=True)
    gate_up_grad = gate_up_grads(gate_pre_grad, up_pre_grad, gated_rows)
    gate_up_sum = lax.psum_scatter(gate_up_grad, "dp", scatter_dimension=0, tiled=True)
    result = dot(hidden, down_weight).astype(jnp.bfloat16)
    back, result, down_grad, gate_up_grad = lax.optimization_barrier((back, result, down_grad, gate_up_grad))
    returned = exchange(result)

    def halve(grad):
        parts = grad.reshape(copies, ways // 2, 2, -1, grad.shape[1])
        away = lax.dynamic_index_in_dim(parts, 1 - core, 2, keepdims=False).astype(jnp.bfloat16)
        mine = lax.dynamic_index_in_dim(parts, core, 2, keepdims=False)
        other = lax.ppermute(away, "expert", [(k, k ^ 1) for k in range(ways)])
        return (mine + other.astype(jnp.float32)).astype(jnp.bfloat16)

    def over_all(grad):
        half = halve(grad)
        half = lax.all_to_all(half, "dp", split_axis=0, concat_axis=0, tiled=True)
        part = jnp.sum(half.astype(jnp.float32), axis=0).astype(jnp.bfloat16)
        groups = [list(range(0, ways, 2)), list(range(1, ways, 2))]
        part = lax.all_to_all(
            part, "expert", split_axis=0, concat_axis=0, axis_index_groups=groups, tiled=True
        )
        return jnp.sum(part.astype(jnp.float32), axis=0)

    gate_grads = [jnp.sum(jnp.where(routing[rank], slot_dots, 0.0), axis=1) for rank in range(TOP)]
    average = gates[:, 0] * gate_grads[0] + gates[:, 1] * gate_grads[1]
    dlogits = jnp.zeros_like(logits)
    for rank in range(TOP):
        logit_grad = gates[:, rank] * (gate_grads[rank] - average)
        dlogits = dlogits + jnp.where(picks[rank], logit_grad[:, None], 0.0)
    dlogits = dlogits.astype(jnp.bfloat16)
    router_grad = dot(moe_in, dlogits, TN)
    moe_in_grad = dot(dlogits, w_router, NT) + dot(gated, back)
    upstream = cotangent.astype(jnp.float32)
    resid_norm_grad, gain_moe_grad = normalize_backward(moe_in_grad, unit_two, scale_two, gain_moe)
    resid_grad = upstream + resid_norm_grad
    attn_grad = resid_grad.astype(jnp.bfloat16)
    out_weight_sum = over_all(dot(mixed, attn_grad, TN))
    mixed_grad = dot(attn_grad, w_attn_out, NT).astype(jnp.bfloat16)
    proj_grad, tiles = attention_backward(item_lengths, bias, stat, proj, mixed, mixed_grad)
    table_grad = table_sums(tiles, buckets)
    qkv_grad = jnp.concatenate([dot(attn_in, proj_grad[k], TN) for k in range(3)], axis=1)
    qkv_sum = over_all(qkv_grad)
    attn_in_grad = sum(dot(proj_grad[k], w_qkv[:, k * width : (k + 1) * width], NT) for k in range(3))
    input_norm_grad, gain_attn_grad = normalize_backward(attn_in_grad, unit_one, scale_one, gain_attn)
    input_grad = resid_grad + input_norm_grad
    output = (resid + dot(gated, returned)).astype(jnp.bfloat16)
    devices = copies * ways
    small = (table_grad.reshape(-1), gain_attn_grad, gain_moe_grad, router_grad)
    sizes = [part.size // devices for part in small]
    together = jnp.concatenate([part.reshape(devices, -1) for part in small], axis=1)
    together = lax.all_to_all(together, ("dp", "expert"), split_axis=0, concat_axis=0, tiled=True)
    together = jnp.sum(together, axis=0)
    at = [sum(sizes[:k]) for k in range(5)]
    table_sum, attn_sum, moe_sum, router_sum = [together[at[k] : at[k + 1]] for k in range(4)]
    return (
        output,
        input_grad,
        qkv_sum,
        out_weight_sum,
        table_sum,
        attn_sum,
        moe_sum,
        router_sum.reshape(-1, experts),
        gate_up_sum[:, :width].astype(jnp.float32).T[None],
        gate_up_sum[:, width:].astype(jnp.float32).T[None],
        down_sum.astype(jnp.float32)[None],
    )


def solution(mesh):
    return jax.shard_map(
        on_device,
        mesh=mesh,
        in_specs=(
            P(("dp", "expert"), None),
            P(("dp", "expert"), None),
            P(("dp", "expert"), None),
            P(),
            P(),
            P(),
            P(),
            P(),
            P(),
            P("expert", None, None),
            P("expert", None, None),
            P("expert", None, None),
            P(("dp", "expert"), None),
        ),
        out_specs=(
            P(("dp", "expert"), None),
            P(("dp", "expert"), None),
            P(("dp", "expert"), None),
            P(("dp", "expert"), None),
            P(("dp", "expert")),
            P(("dp", "expert")),
            P(("dp", "expert")),
            P(("dp", "expert"), None),
            P("expert", None, "dp"),
            P("expert", None, "dp"),
            P("expert", None, "dp"),
        ),
        check_vma=False,
    )
```

time: 1060 us -> 652 us (0.62)
  matrix products: 295 us -> 86.9 us
  Pallas kernels: 0 us -> 154 us
  blocking collectives: 197 us -> 48.4 us
  local copies, waits for them, and re-layouts: 141 us -> 28.5 us
  waiting for transfers between devices: 305 us -> 226 us
  other arithmetic: 85.1 us -> 44.5 us
  starting transfers between devices: 9.33 us -> 40 us
    dot_general x40 -> x21, matrix products: 293 us -> 86.9 us  [the longest x19 80.8 us: dot(): return lax.dot_general(a, b, dims, preferred_element_type=jnp.float32)]
    reduce_scatter x3 -> x2, waiting for transfers between devices: 155 us -> 0.01 us  [the longest x1 0.01 us: on_device(): lax.psum_scatter(down_grad, 'dp', scatter_dimension=1, tiled=True)]
    pallas_call x0 -> x6, Pallas kernels: none -> 154 us  [the longest x1 56.2 us: expert_rows(): pl.pallas_call(lambda *refs: expert_kernel(*refs, parts=parts), grid=(f /...]
    unnamed x165 -> x33, local copies, waits for them, and re-layouts: 122 us -> 4.46 us
    all_to_all x2, blocking collectives: 157 us -> 48.4 us  [the longest x1 40.4 us: over_all(): half = lax.all_to_all(half, 'dp', split_axis=0, concat_axis=0, tiled=True)]
    all_to_all x2 -> x9, waiting for transfers between devices: 150 us -> 226 us  [the longest x5 198 us: exchange(): lax.all_to_all(rows.reshape((experts, capacity) + shape[1:]), 'expert', s...]
    another operation x6 -> x0, other arithmetic: 46.3 us -> none
    unnamed x1 -> x0, blocking collectives: 39.8 us -> none
  transfers between devices with their start and end apart: 8 -> 13, of which waited for: 3 -> 9; matrix products, arithmetic and copies ran while one was open for 31% -> 21% of each run, Pallas kernels for 0% -> 13%
where the time goes in v1:
time: 652 us; the launch traced here: 643 us
  waiting for transfers between devices  226 us (35%)
  Pallas kernels  154 us (24%)
  matrix products  86.9 us (13%)
  blocking collectives  48.4 us (7%)
  other arithmetic  44.5 us (7%)
  starting transfers between devices  40 us (6%)
  local copies, waits for them, and re-layouts  28.5 us (4%)
  between operations  14.7 us (2%)
    all_to_all x5, waiting for transfers between devices, exchange(): lax.all_to_all(rows.reshape((experts, capacity) + shape[1:]), 'expert', s...  198 us
    dot_general x19, matrix products, dot(): return lax.dot_general(a, b, dims, preferred_element_type=jnp.float32)  80.8 us
    pallas_call x1, Pallas kernels, expert_rows(): pl.pallas_call(lambda *refs: expert_kernel(*refs, parts=parts), grid=(f /...  56.2 us
    all_to_all x1, blocking collectives, over_all(): half = lax.all_to_all(half, 'dp', split_axis=0, concat_axis=0, tiled=True)  40.4 us
    pallas_call x1, Pallas kernels, gate_up_grads(): pl.pallas_call(gate_up_kernel, grid=(f // FT,), in_specs=[tile, tile, pl....  27 us
    all_to_all x5, starting transfers between devices, exchange(): lax.all_to_all(rows.reshape((experts, capacity) + shape[1:]), 'expert', s...  23.5 us
    pallas_call x1, Pallas kernels, attention_backward(): pl.pallas_call(attention_backward_kernel, grid=(pairs,), in_specs=[pl.Blo...  22.1 us
    pallas_call x1, Pallas kernels, down_grads(): pl.pallas_call(down_kernel, grid=(f // FT,), in_specs=[pl.BlockSpec((n, F...  16.7 us
  transfers between devices with their start and end apart: 13, of which 9 were waited for; matrix products, arithmetic and copies ran while one was open for 21% of the time, Pallas kernels for 13%

profile of v1, /device:TPU:0, one launch (start us, length us, event | category | flops | bytes accessed | tf_op | source)
XLA Modules:
  0.0 643.4 jit_solution(8240808444768513209)
XLA Ops:
  13.8 6.5 %all-to-all-start = ((bf16[8,200,1024]{2,1,0:T(8,128)(2,1)}), bf16[8,200,1024]{2,1,0:T(8,128)(2,1)}, u32[]{:S(2)}, u32[]{:S(2)}) async-start(bf16[8,200,1024]{2,1,0:T(8,128)(2,1)} %bitcast.92), calls=%async_computation | async-start | bytes 6553600 | tf_op jit(solution)/shard_map/all_to_all | solution.py:397
  21.6 8.7 %convolution_convert_fusion.q_ref.k_ref.v_ref = bf16[640,3072]{1,0:T(8,128)(2,1)} fusion(bf16[1024,3072]{1,0:T(8,128)(2,1)} %param.16, bf16[640,1024]{1,0:T(8,128)(2,1)S(1)} %copy-done.5, f32[1024]{0:T(1024)S(1)} %copy-done.12, f32[640]{0:T(1024)S(1)} %add_rsqrt_fusion.1), kind=kOutput, calls=%fused_computation.9 | convolution fusion | flops 4031119360 | bytes 11540992 | tf_op jit(solution)/shard_map/dot_general | solution.py:26
  30.3 16.1 %attention_forward.1 = (bf16[640,1024]{1,0:T(8,128)(2,1)}, f32[8,2,640]{2,1,0:T(2,128)}) custom-call(s32[1,2]{1,0:T(1,128)} %lengths_ref.3, f32[8,2,512]{2,1,0:T(2,128)} %reshape.254.bias_ref, bf16[640,3072]{1,0:T(8,128)(2,1)} %convolution_convert_fusion.q_ref.k_ref.v_ref, bf16[640,3072]{1,0:T(8,128)(2,1)} %convolution_convert_fusion.q_ref.k_ref.v_ref, ...), custom_call_target="tpu_custom_call" | custom-call | tf_op jit(solution)/shard_map/attention_forward/pallas_call | solution.py:105
  55.2 39.5 %all-to-all-done = bf16[8,200,1024]{2,1,0:T(8,128)(2,1)} async-done(((bf16[8,200,1024]{2,1,0:T(8,128)(2,1)}), bf16[8,200,1024]{2,1,0:T(8,128)(2,1)}, u32[]{:S(2)}, u32[]{:S(2)}) %all-to-all-start) | async-done | bytes 3276832 | tf_op jit(solution)/shard_map/all_to_all | solution.py:397
  100.1 16.2 %slope_rows.1.refs_1_ = bf16[1600,2816]{1,0:T(8,128)(2,1)} custom-call(bf16[1600,1024]{1,0:T(8,128)(2,1)} %bitcast.2.u_ref, bf16[2816,1024]{1,0:T(8,128)(2,1)} %bitcast.88), custom_call_target="tpu_custom_call" | custom-call | tf_op jit(solution)/shard_map/slope_rows/pallas_call | solution.py:307
  116.3 57.6 %all-to-all-done.1 = bf16[8,200,1024]{2,1,0:T(8,128)(2,1)} async-done(((bf16[8,200,1024]{2,1,0:T(8,128)(2,1)}), bf16[8,200,1024]{2,1,0:T(8,128)(2,1)}, u32[]{:S(2)}, u32[]{:S(2)}) %all-to-all-start.1) | async-done | bytes 3276832 | tf_op jit(solution)/shard_map/all_to_all | solution.py:397
  173.8 56.2 %expert_rows.1 = (bf16[1600,2816]{1,0:T(8,128)(2,1)}, bf16[1600,2816]{1,0:T(8,128)(2,1)}, bf16[1600,2816]{1,0:T(8,128)(2,1)}, bf16[1600,1024]{1,0:T(8,128)(2,1)}, f32[1600,128]{1,0:T(8,128)}) custom-call(bf16[1600,1024]{1,0:T(8,128)(2,1)} %bitcast.4.refs_0_, bf16[1600,2816]{1,0:T(8,128)(2,1)} %slope_rows.1.refs_1_, bf16[1024,2816]{1,0:T(8,128)(2,1)} %bitcast.86, ...), custom_call_target="tpu_custom_call" | custom-call | tf_op jit(solution)/shard_map/expert_rows/pallas_call | solution.py:288
  243.5 8.0 %all_to_all.67 = f32[8,1,200]{2,1,0:T(1,128)S(1)} all-to-all(f32[8,1,200]{2,1,0:T(1,128)S(1)} %all_to_all.45), channel_id=1, replica_groups=mesh['dp'=4,'expert'=8] {'expert'}, dimensions={0} | all-to-all | bytes 12800 | tf_op jit(solution)/shard_map/all_to_all | solution.py:397
  257.0 16.7 %down_grads.1 = bf16[2816,1024]{1,0:T(8,128)(2,1)} custom-call(bf16[1600,2816]{1,0:T(8,128)(2,1)} %get-tuple-element.32.h_ref, bf16[1600,1024]{1,0:T(8,128)(2,1)} %get-tuple-element.94.u_ref), custom_call_target="tpu_custom_call" | custom-call | tf_op jit(solution)/shard_map/down_grads/pallas_call | solution.py:324
  278.4 27.0 %gate_up_grads.1 = bf16[2816,2048]{1,0:T(8,128)(2,1)} custom-call(bf16[1600,2816]{1,0:T(8,128)(2,1)} %get-tuple-element.33.g_ref, bf16[1600,2816]{1,0:T(8,128)(2,1)} %get-tuple-element.34.p_ref, bf16[1600,1024]{1,0:T(8,128)(2,1)} %get-tuple-element.93.x_ref), custom_call_target="tpu_custom_call" | custom-call | tf_op jit(solution)/shard_map/gate_up_grads/pallas_call | solution.py:344
  305.5 14.8 %convolution_convert_fusion.1 = bf16[1600,1024]{1,0:T(8,128)(2,1)} fusion(bf16[1600,2816]{1,0:T(8,128)(2,1)} %get-tuple-element.32.h_ref, bf16[1,2816,1024]{2,1,0:T(8,128)(2,1)} %param.24), kind=kOutput, calls=%fused_computation.25 | convolution fusion | flops 9229107200 | bytes 18055168 | tf_op jit(solution)/shard_map/dot_general | solution.py:26
  320.3 32.1 %all-to-all-done.2 = bf16[8,200,1024]{2,1,0:T(8,128)(2,1)} async-done(((bf16[8,200,1024]{2,1,0:T(8,128)(2,1)}), bf16[8,200,1024]{2,1,0:T(8,128)(2,1)}, u32[]{:S(2)}, u32[]{:S(2)}) %all-to-all-start.2) | async-done | bytes 3276832 | tf_op jit(solution)/shard_map/all_to_all | solution.py:397
  361.9 22.1 %attention_backward.1 = (bf16[3,640,1024]{2,1,0:T(8,128)(2,1)}, f32[8,2,136,384]{3,2,1,0:T(8,128)}) custom-call(s32[1,2]{1,0:T(1,128)} %lengths_ref.3, f32[8,2,512]{2,1,0:T(2,128)} %reshape.254.bias_ref, f32[8,2,640]{2,1,0:T(2,128)} %get-tuple-element.38.stat_ref, bf16[640,3072]{1,0:T(8,128)(2,1)} %convolution_convert_fusion.q_ref.k_ref.v_ref, ...), custom_call_target="tpu_custom_call" | custom-call | tf_op jit(solution)/shard_map/attention_backward/pallas_call | solution.py:194
  391.4 5.6 pad_maximum_fusion
  397.0 13.1 %copy.38 = f32[1024,3072]{1,0:T(8,128)} copy(f32[1024,3072]{0,1:T(8,128)} %pad_maximum_fusion) | data formatting | bytes 25165824 | tf_op jit(solution)/shard_map/concatenate | solution.py:474
  440.6 7.0 %fusion.21 = (f32[1024]{0:T(1024)S(1)}, f32[640]{0:T(1024)S(1)}, f32[640,1024]{1,0:T(8,128)}) fusion(bf16[640,1024]{1,0:T(8,128)(2,1)S(1)} %copy-done.6, f32[640]{0:T(1024)S(1)} %add_rsqrt_fusion.1, f32[1024]{0:T(1024)S(1)} %copy-done.12, f32[640,1024]{1,0:T(8,128)} %fusion.24, f32[640,1024]{1,0:T(8,128)} %fusion.26, bf16[1024,3072]{1,0:T(8,128)(2,1)} %param.16, ...), kind=kOutput, calls=%fused_computation.38 | convolution fusion | flops 1348073856 | bytes 12596224 | tf_op jit(solution)/shard_map/dot_general | solution.py:26
  447.7 5.8 fusion.59
  454.3 8.2 %all-to-all-done.8 = bf16[4,4,32,1024]{3,2,1,0:T(8,128)(2,1)S(1)} async-done(((bf16[4,4,32,1024]{3,2,1,0:T(8,128)(2,1)}), bf16[4,4,32,1024]{3,2,1,0:T(8,128)(2,1)S(1)}, u32[]{:S(2)}, u32[]{:S(2)}) %all-to-all-start.8) | async-done | bytes 1048608 | tf_op jit(solution)/shard_map/all_to_all | solution.py:449
  468.1 6.4 all-to-all-done.10
  478.1 6.4 fusion.3
  487.5 40.4 %all_to_all.68 = bf16[4,4,32,3072]{3,2,1,0:T(8,128)(2,1)} all-to-all(bf16[4,4,32,3072]{3,2,1,0:T(8,128)(2,1)} %fusion.3), channel_id=1, replica_groups=mesh['dp'=4,'expert'=8] {'dp'}, dimensions={0} | all-to-all | bytes 6291456 | tf_op jit(solution)/shard_map/all_to_all | solution.py:449
  543.4 63.4 %all-to-all-done.4 = bf16[8,200,1024]{2,1,0:T(8,128)(2,1)} async-done(((bf16[8,200,1024]{2,1,0:T(8,128)(2,1)}), bf16[8,200,1024]{2,1,0:T(8,128)(2,1)}, u32[]{:S(2)}, u32[]{:S(2)}) %all-to-all-start.4) | async-done | bytes 3276832 | tf_op jit(solution)/shard_map/all_to_all | solution.py:397
  610.3 6.5 %add_convert_fusion = bf16[640,1024]{1,0:T(8,128)(2,1)} fusion(f32[640,1024]{1,0:T(8,128)} %copy-done.2, bf16[1600,1024]{1,0:T(8,128)(2,1)} %bitcast.11, f32[640]{0:T(1024)S(1)} %get-tuple-element.88, f32[640]{0:T(1024)S(1)} %get-tuple-element.87, s32[640]{0:T(1024)S(1)} %convert_element_type.218, s32[640]{0:T(1024)S(1)} %convert_element_type.217), kind=kOutput, calls=%fused_computation.44 | convolution fusion | flops 2104606720 | bytes 7219200 | tf_op jit(solution)/shard_map/dot_general | solution.py:26
  620.0 10.5 %all-to-all-done.7 = bf16[4,32,3072]{2,1,0:T(8,128)(2,1)S(1)} async-done(((bf16[4,32,3072]{2,1,0:T(8,128)(2,1)}), bf16[4,32,3072]{2,1,0:T(8,128)(2,1)S(1)}, u32[]{:S(2)}, u32[]{:S(2)}) %all-to-all-start.7) | async-done | bytes 786464 | tf_op jit(solution)/shard_map/all_to_all | solution.py:452
  (123 shorter events, 133.8 us)
Async XLA Ops:
  7.2 39.2 %copy-start = (bf16[1024,1024]{1,0:T(8,128)(2,1)S(1)}, bf16[1024,1024]{1,0:T(8,128)(2,1)}, u32[]{:S(2)}) copy-start(bf16[1024,1024]{1,0:T(8,128)(2,1)} %param.17) | copy-start | bytes 6291460
  13.8 6.5 %copy-start.15 = (f32[32,16]{0,1:T(8,128)S(1)}, f32[32,16]{0,1:T(8,128)}, u32[]{:S(2)}) copy-start(f32[32,16]{0,1:T(8,128)} %param.18) | copy-start | bytes 6148
  13.8 7.5 %copy-start.5 = (bf16[640,1024]{1,0:T(8,128)(2,1)S(1)}, bf16[640,1024]{1,0:T(8,128)(2,1)}, u32[]{:S(2)}) copy-start(bf16[640,1024]{1,0:T(8,128)(2,1)} %param.13) | copy-start | bytes 3932164
  13.8 7.8 %copy-start.12 = (f32[1024]{0:T(1024)S(1)}, f32[1024]{0:T(1024)}, u32[]{:S(2)}) copy-start(f32[1024]{0:T(1024)} %param.19) | copy-start | bytes 12292
  13.8 80.9 %all-to-all-start = ((bf16[8,200,1024]{2,1,0:T(8,128)(2,1)}), bf16[8,200,1024]{2,1,0:T(8,128)(2,1)}, u32[]{:S(2)}, u32[]{:S(2)}) async-start(bf16[8,200,1024]{2,1,0:T(8,128)(2,1)} %bitcast.92), calls=%async_computation | async-start | bytes 6553600 | tf_op jit(solution)/shard_map/all_to_all | solution.py:397
  46.4 4.5 copy-start.11
  94.7 4.8 copy-start.10
  94.7 79.1 %all-to-all-start.1 = ((bf16[8,200,1024]{2,1,0:T(8,128)(2,1)}), bf16[8,200,1024]{2,1,0:T(8,128)(2,1)}, u32[]{:S(2)}, u32[]{:S(2)}) async-start(bf16[8,200,1024]{2,1,0:T(8,128)(2,1)} %bitcast.91), calls=%async_computation.1 | async-start | bytes 6553600 | tf_op jit(solution)/shard_map/all_to_all | solution.py:397
  232.2 8.9 %all-to-all-start.5 = ((f32[8,1,200]{2,1,0:T(1,128)}), f32[8,1,200]{2,1,0:T(1,128)S(1)}, u32[]{:S(2)}, u32[]{:S(2)}) async-start(f32[8,1,200]{2,1,0:T(1,128)} %all_to_all.48), calls=%async_computation.5 | async-start | bytes 16384 | tf_op jit(solution)/shard_map/all_to_all | solution.py:397
  235.5 381.3 %reduce-scatter.5.cloned.1.call-start = ((), (), s32[]{:S(2)}) async-start(), calls=%async_computation.14 | async-start | bytes 7208960 | tf_op jit(solution)/shard_map/reduce_scatter | solution.py:433
  273.6 78.8 %all-to-all-start.2 = ((bf16[8,200,1024]{2,1,0:T(8,128)(2,1)}), bf16[8,200,1024]{2,1,0:T(8,128)(2,1)}, u32[]{:S(2)}, u32[]{:S(2)}) async-start(bf16[8,200,1024]{2,1,0:T(8,128)(2,1)} %bitcast.90), calls=%async_computation.2 | async-start | bytes 6553600 | tf_op jit(solution)/shard_map/all_to_all | solution.py:397
  278.1 353.2 %reduce-scatter.3.cloned.1.call-start = ((), (), s32[]{:S(2)}) async-start(), calls=%async_computation.13 | async-start | bytes 14417920 | tf_op jit(solution)/shard_map/reduce_scatter | solution.py:435
  352.5 4.7 copy-start.3
  361.9 22.2 %copy-start.6 = (bf16[640,1024]{1,0:T(8,128)(2,1)S(1)}, bf16[640,1024]{1,0:T(8,128)(2,1)}, u32[]{:S(2)}) copy-start(bf16[640,1024]{1,0:T(8,128)(2,1)} %param.13) | copy-start | bytes 3932164
  415.0 63.1 %collective-permute-start = (bf16[4,4,32,3072]{3,2,1,0:T(8,128)(2,1)}, bf16[4,4,32,3072]{3,2,1,0:T(8,128)(2,1)}, u32[]{:S(2)}, u32[]{:S(2)}) collective-permute-start(bf16[4,4,32,3072]{3,2,1,0:T(8,128)(2,1)} %fusion.15), channel_id=1, source_target_pairs={{0,1},{1,0},{2,3},{3,2},{4,5},{5,4},{6,7},{7,6},{8,9},{9,8},{10,11... | collective-permute-start | bytes 9437192 | tf_op jit(solution)/shard_map/ppermute | solution.py:444
  422.3 11.7 %collective-permute-start.1 = (bf16[4,4,32,1024]{3,2,1,0:T(8,128)(2,1)}, bf16[4,4,32,1024]{3,2,1,0:T(8,128)(2,1)}, u32[]{:S(2)}, u32[]{:S(2)}) collective-permute-start(bf16[4,4,32,1024]{3,2,1,0:T(8,128)(2,1)} %fusion.64), channel_id=1, source_target_pairs={{0,1},{1,0},{2,3},{3,2},{4,5},{5,4},{6,7},{7,6},{8,9},{9,8},{10,11... | collective-permute-start | bytes 3145736 | tf_op jit(solution)/shard_map/ppermute | solution.py:444
  423.7 5.2 copy-start.14
  428.9 5.1 copy-start.8
  436.6 25.9 %all-to-all-start.8 = ((bf16[4,4,32,1024]{3,2,1,0:T(8,128)(2,1)}), bf16[4,4,32,1024]{3,2,1,0:T(8,128)(2,1)S(1)}, u32[]{:S(2)}, u32[]{:S(2)}) async-start(bf16[4,4,32,1024]{3,2,1,0:T(8,128)(2,1)} %fusion.23), calls=%async_computation.8 | async-start | bytes 2097152 | tf_op jit(solution)/shard_map/all_to_all | solution.py:449
  462.6 11.9 %all-to-all-start.10 = ((f32[32,1,336]{2,1,0:T(1,128)}), f32[32,1,336]{2,1,0:T(1,128)S(1)}, u32[]{:S(2)}, u32[]{:S(2)}) async-start(f32[32,1,336]{2,1,0:T(1,128)} %copy.43), calls=%async_computation.10 | async-start | bytes 98304 | tf_op jit(solution)/shard_map/all_to_all | solution.py:484
  474.5 13.0 %all-to-all-start.9 = ((bf16[4,32,1024]{2,1,0:T(8,128)(2,1)}), bf16[4,32,1024]{2,1,0:T(8,128)(2,1)S(1)}, u32[]{:S(2)}, u32[]{:S(2)}) async-start(bf16[4,32,1024]{2,1,0:T(8,128)(2,1)} %reduce_sum.207), calls=%async_computation.9 | async-start | bytes 524288 | tf_op jit(solution)/shard_map/all_to_all | solution.py:452
  528.0 78.8 %all-to-all-start.4 = ((bf16[8,200,1024]{2,1,0:T(8,128)(2,1)}), bf16[8,200,1024]{2,1,0:T(8,128)(2,1)}, u32[]{:S(2)}, u32[]{:S(2)}) async-start(bf16[8,200,1024]{2,1,0:T(8,128)(2,1)} %bitcast.89), calls=%async_computation.4 | async-start | bytes 6553600 | tf_op jit(solution)/shard_map/all_to_all | solution.py:397
  606.8 23.7 %all-to-all-start.7 = ((bf16[4,32,3072]{2,1,0:T(8,128)(2,1)}), bf16[4,32,3072]{2,1,0:T(8,128)(2,1)S(1)}, u32[]{:S(2)}, u32[]{:S(2)}) async-start(bf16[4,32,3072]{2,1,0:T(8,128)(2,1)} %reduce_sum.205), calls=%async_computation.7 | async-start | bytes 1572864 | tf_op jit(solution)/shard_map/all_to_all | solution.py:452
  630.5 5.9 copy-start.1
  (5 other events, 10.9 us)
Sparse Core Ops, SparseCore 0:
  273.8 64.0 reduce-scatter.4
  341.0 123.2 reduce-scatter.2

commit v2 on v1

--- a/solution.py
+++ b/solution.py
@@ -20,6 +20,10 @@
 TN = (((0,), (0,)), ((), ()))
 CURVE = 0.7978845608028654
 CUBE = 0.044715
+EXTRA = 8
+SMALL = pl.CostEstimate(flops=1 << 20, bytes_accessed=1 << 16, transcendentals=0)
+MEDIUM = pl.CostEstimate(flops=230 * 10**9, bytes_accessed=1 << 16, transcendentals=0)
+LARGE = pl.CostEstimate(flops=1 << 38, bytes_accessed=1 << 28, transcendentals=0)
 
 
 def dot(a, b, dims=NN):
@@ -121,14 +125,30 @@
             jax.ShapeDtypeStruct((pairs, 2, tokens), jnp.float32),
         ],
         scratch_shapes=[pltpu.VMEM((LONG_LEN, LONG_LEN), jnp.float32), pltpu.VMEM((LONG_LEN, LONG_LEN), jnp.bfloat16)],
+        cost_estimate=SMALL,
         name="attention_forward",
     )(lengths, bias, proj, proj, proj)
 
 
 def attention_backward_kernel(
     lengths_ref, bias_ref, stat_ref, q_ref, k_ref, v_ref, mixed_ref, grad_ref, proj_ref, table_ref,
-    score_ref, slope_ref, weight_ref, change_ref,
+    score_ref, slope_ref, weight_ref, change_ref, stage_ref, done_ref,
 ):
+    pair = pl.program_id(0)
+    pairs = pl.num_programs(0)
+    slot = pair % 2
+
+    def copy(part, step):
+        at = pl.multiple_of((part * pairs + step) * TILE, TILE)
+        return pltpu.make_async_copy(
+            stage_ref.at[step % 2, part], proj_ref.at[:, pl.ds(at, TILE)], done_ref.at[step % 2, part]
+        )
+
+    @pl.when(pair >= 2)
+    def _():
+        for part in range(3):
+            copy(part, pair - 2).wait()
+
     tokens, lanes = q_ref.shape
     size = lanes // 2
     lane = lax.broadcasted_iota(jnp.int32, (1, lanes), 1)
@@ -182,9 +202,17 @@
             value_grads.append(dot(weight_ref[0:length, 0:length], grad))
             key_grads.append(dot(change_ref[0:length, 0:length], query))
             query_grads.append(dot(keys_t[head * size : (head + 1) * size, start:stop], change_ref[0:length, 0:length]))
-        proj_ref[0, start:stop, :] = (jnp.concatenate(query_grads, axis=0).T * 0.125).astype(jnp.bfloat16)
-        proj_ref[1, start:stop, :] = (key_grads[0] + key_grads[1]).astype(jnp.bfloat16)
-        proj_ref[2, start:stop, :] = (value_grads[0] + value_grads[1]).astype(jnp.bfloat16)
+        stage_ref[slot, 0, start:stop, :] = (jnp.concatenate(query_grads, axis=0).T * 0.125).astype(jnp.bfloat16)
+        stage_ref[slot, 1, start:stop, :] = (key_grads[0] + key_grads[1]).astype(jnp.bfloat16)
+        stage_ref[slot, 2, start:stop, :] = (value_grads[0] + value_grads[1]).astype(jnp.bfloat16)
+    for part in range(3):
+        copy(part, pair).start()
+
+    @pl.when(pair == pairs - 1)
+    def _():
+        for part in range(3):
+            copy(part, pair - 1).wait()
+            copy(part, pair).wait()
 
 
 def attention_backward(lengths, bias, stat, proj, mixed, grad):
@@ -205,11 +233,11 @@
             pl.BlockSpec((tokens, lanes), lambda p: (0, p)),
         ],
         out_specs=[
-            pl.BlockSpec((3, tokens, lanes), lambda p: (0, 0, p)),
+            pl.BlockSpec(memory_space=pl.ANY),
             pl.BlockSpec((1, 2, TILE + 8, 3 * TILE), lambda p: (p, 0, 0, 0)),
         ],
         out_shape=[
-            jax.ShapeDtypeStruct((3, tokens, width), jnp.bfloat16),
+            jax.ShapeDtypeStruct((tokens, 3 * width), jnp.bfloat16),
             jax.ShapeDtypeStruct((pairs, 2, TILE + 8, 3 * TILE), jnp.float32),
         ],
         scratch_shapes=[
@@ -217,7 +245,10 @@
             pltpu.VMEM((LONG_LEN, LONG_LEN), jnp.float32),
             pltpu.VMEM((LONG_LEN, LONG_LEN), jnp.bfloat16),
             pltpu.VMEM((LONG_LEN, LONG_LEN), jnp.bfloat16),
-        ],
+            pltpu.VMEM((2, 3, tokens, lanes), jnp.bfloat16),
+            pltpu.SemaphoreType.DMA((2, 3)),
+        ],
+        cost_estimate=SMALL,
         name="attention_backward",
     )(lengths, bias, stat, proj, proj, proj, mixed, grad)
 
@@ -244,7 +275,135 @@
     return jnp.einsum("ghrc,rcb->bgh", tiles, onehot, precision=HIGHEST).reshape(buckets, -1)
 
 
-def expert_kernel(x_ref, slope_ref, wg_ref, wu_ref, hidden_ref, gate_ref, up_ref, pair_ref, dots_ref, acc_ref, *, parts):
+def pack_first_kernel(place_ref, routes_ref, rows_ref, *out_refs, experts, capacity):
+    target_ref = out_refs[-1]
+    tokens = routes_ref.shape[1]
+    routes = [routes_ref[rank : rank + 1, :] for rank in range(TOP)]
+    label = lax.broadcasted_iota(jnp.int32, (experts, 1), 0)
+    picks = [label == route for route in routes]
+    named = jnp.where(picks[0] | picks[1], 1.0, 0.0).astype(jnp.bfloat16)
+    later = lax.broadcasted_iota(jnp.int32, (1, tokens), 1)
+    earlier = lax.broadcasted_iota(jnp.int32, (tokens, 1), 0)
+    count = dot(named, jnp.where(earlier < later, 1.0, 0.0).astype(jnp.bfloat16))
+    for rank in range(TOP):
+        position = jnp.sum(jnp.where(picks[rank], count, 0.0), axis=0, keepdims=True).astype(jnp.int32)
+        apart = routes[rank] ^ place_ref[0]
+        apart = jnp.where(apart < experts // 2, routes[rank] & (experts // 2 - 1), apart)
+        target_ref[rank : rank + 1, :] = apart * capacity + position
+    other = jnp.concatenate([routes[1], routes[0]], axis=0).astype(jnp.float32) + 1.0
+    pack_kernel(target_ref, rows_ref, *out_refs[:-1], other=other, capacity=capacity)
+
+
+def pack_kernel(target_ref, rows_ref, *out_refs, other=None, capacity):
+    rows = rows_ref[...]
+    base = 0
+    for out_ref in out_refs:
+        stride = capacity + (0 if other is None else EXTRA)
+        for at in range(0, out_ref.shape[0], stride):
+            slot = lax.broadcasted_iota(jnp.int32, (capacity, 1), 0) + base
+            hits = [slot == target_ref[rank : rank + 1, :] for rank in range(TOP)]
+            hit = jnp.where(hits[0] | hits[1], 1.0, 0.0).astype(jnp.bfloat16)
+            out_ref[at : at + capacity, :] = dot(hit, rows).astype(jnp.bfloat16)
+            if other is not None:
+                named = sum(jnp.where(hits[rank], other[rank : rank + 1, :], 0.0) for rank in range(TOP))
+                ones = jnp.ones((EXTRA, named.shape[1]), jnp.bfloat16)
+                out_ref[at + capacity : at + stride, :] = jnp.zeros((EXTRA, out_ref.shape[1]), jnp.bfloat16)
+                out_ref[at + capacity : at + stride, 0:capacity] = dot(ones, named.astype(jnp.bfloat16), NT).astype(jnp.bfloat16)
+            base += capacity
+
+
+def block_shapes(experts, rows, width):
+    half = experts // 2
+    return [jax.ShapeDtypeStruct((n * rows, width), jnp.bfloat16) for n in [half] + [1] * half]
+
+
+def pack_first(place, routes, rows, experts, capacity):
+    blocks = block_shapes(experts, capacity + EXTRA, rows.shape[1])
+    *blocks, target = pl.pallas_call(
+        lambda *refs: pack_first_kernel(*refs, experts=experts, capacity=capacity),
+        in_specs=[pl.BlockSpec(memory_space=pltpu.SMEM), pl.BlockSpec(), pl.BlockSpec()],
+        out_shape=blocks + [jax.ShapeDtypeStruct(routes.shape, jnp.int32)],
+        cost_estimate=SMALL,
+        name="pack_first",
+    )(place, routes, rows)
+    return blocks, target
+
+
+def pack(target, rows, experts, capacity):
+    return pl.pallas_call(
+        lambda *refs: pack_kernel(*refs, capacity=capacity),
+        out_shape=block_shapes(experts, capacity, rows.shape[1]),
+        cost_estimate=SMALL,
+        name="pack_rows",
+    )(target, rows)
+
+
+def gather_rows(target_ref, gates_ref, blocks):
+    total = None
+    base = 0
+    for block in blocks:
+        slot = lax.broadcasted_iota(jnp.int32, (1, block.shape[0]), 1) + base
+        share = sum(
+            jnp.where(target_ref[:, rank : rank + 1] == slot, gates_ref[:, rank : rank + 1], 0.0) for rank in range(TOP)
+        )
+        part = dot(share.astype(jnp.bfloat16), block[...])
+        total = part if total is None else total + part
+        base += block.shape[0]
+    return total
+
+
+def output_kernel(target_ref, gates_ref, resid_ref, *refs):
+    refs[-1][...] = (resid_ref[...] + gather_rows(target_ref, gates_ref, refs[:-1])).astype(jnp.bfloat16)
+
+
+def combine_output(target, gates, resid, blocks):
+    return pl.pallas_call(
+        output_kernel,
+        out_shape=jax.ShapeDtypeStruct(resid.shape, jnp.bfloat16),
+        cost_estimate=MEDIUM,
+        name="combine_output",
+    )(target, gates, resid, *blocks)
+
+
+def combine_kernel(target_ref, gates_ref, resid_ref, scale_ref, gain_ref, upstream_ref, *refs):
+    blocks, (grad_ref, low_ref, gain_grad_ref) = refs[:-3], refs[-3:]
+    total = gather_rows(target_ref, gates_ref, blocks)
+    scale = scale_ref[...]
+    unit = resid_ref[...] * scale
+    gain_grad_ref[...] = jnp.sum(total * unit, axis=0, keepdims=True)
+    along = total * gain_ref[...]
+    inner = jnp.mean(along * unit, axis=1, keepdims=True)
+    grad = upstream_ref[...].astype(jnp.float32) + scale * (along - unit * inner)
+    grad_ref[...] = grad
+    low_ref[...] = grad.astype(jnp.bfloat16)
+
+
+def combine(target, gates, resid, scale, gain, upstream, blocks):
+    tokens, width = resid.shape
+    return pl.pallas_call(
+        combine_kernel,
+        out_shape=[
+            jax.ShapeDtypeStruct((tokens, width), jnp.float32),
+            jax.ShapeDtypeStruct((tokens, width), jnp.bfloat16),
+            jax.ShapeDtypeStruct((1, width), jnp.float32),
+        ],
+        cost_estimate=SMALL,
+        name="combine_back",
+    )(target, gates, resid, scale, gain, upstream, *blocks)
+
+
+def spans(blocks, capacity, extra=0):
+    base = 0
+    for block in blocks:
+        for at in range(0, block.shape[0], capacity + extra):
+            yield block, at, base
+            base += capacity
+
+
+def expert_kernel(own_ref, slope_ref, wg_ref, wu_ref, wr_ref, other_ref, *refs, ways, parts):
+    blocks, refs = refs[:ways], refs[-(8 + ways) :]
+    hidden_ref, gate_ref, up_ref, share_ref, router_ref = refs[:5]
+    pairs, (x_ref, acc_ref, dots_ref) = refs[5 : 5 + ways], refs[5 + ways :]
     step = pl.program_id(0)
     rows = x_ref.shape[0] // parts
 
@@ -252,6 +411,10 @@
     def _():
         acc_ref[...] = jnp.zeros_like(acc_ref)
         dots_ref[...] = jnp.zeros_like(dots_ref)
+        base = 0
+        for block in blocks:
+            x_ref[base : base + block.shape[0], :] = block[...]
+            base += block.shape[0]
 
     for part in range(parts):
         span = slice(part * rows, (part + 1) * rows)
@@ -276,79 +439,262 @@
 
     @pl.when(step == pl.num_programs(0) - 1)
     def _():
-        pair_ref[...] = acc_ref[...].astype(jnp.bfloat16)
-
-
-def expert_rows(x, slope, wg, wu, parts=4):
-    n, d = x.shape
-    f = wg.shape[1]
-    tile = pl.BlockSpec((n, FT), lambda i: (0, i))
+        logits = dot(x_ref[...], wr_ref[...], NT)
+        label = lax.broadcasted_iota(jnp.int32, (1, TILE), 1)
+        mine = label == own_ref[0]
+        theirs = label == other_ref[...].astype(jnp.int32) - 1
+        first = jnp.sum(jnp.where(mine, logits, 0.0), axis=1, keepdims=True)
+        second = jnp.sum(jnp.where(theirs, logits, 0.0), axis=1, keepdims=True)
+        top = jnp.maximum(first, second)
+        first = jnp.exp(first - top)
+        second = jnp.exp(second - top)
+        total = first + second
+        first = first / total
+        second = second / total
+        inner = jnp.sum(dots_ref[...], axis=1, keepdims=True)
+        coef = inner * second * (jnp.where(mine, 1.0, 0.0) - jnp.where(theirs, 1.0, 0.0))
+        share_ref[...] = jnp.broadcast_to(first, share_ref.shape)
+        router_ref[...] = dot((first * coef).astype(jnp.bfloat16), x_ref[...], TN)
+        acc_ref[...] += dot(coef.astype(jnp.bfloat16), wr_ref[...])
+        base = 0
+        for pair in pairs:
+            pair[...] = acc_ref[base : base + pair.shape[0], :].astype(jnp.bfloat16)
+            base += pair.shape[0]
+
+
+def once(shape):
+    return pl.BlockSpec(shape, lambda i: (0, 0), pipeline_mode=pl.Buffered(1))
+
+
+def expert_rows(own, blocks, slope, wg, wu, wr, other, chunk, kept, parts=2):
+    n = slope.shape[0] // 2
+    d, f = wg.shape
+    ways = len(blocks)
+    tile = pl.BlockSpec((n, FT), lambda i: (chunk, i))
     weight = pl.BlockSpec((d, FT), lambda i: (0, i))
-    whole = pl.BlockSpec((n, d), lambda i: (0, 0))
+    fixed = lambda shape: pl.BlockSpec(shape, lambda i: (0, 0))
+    hidden, gate, up, share, router, *pairs = pl.pallas_call(
+        lambda *refs: expert_kernel(*refs, ways=ways, parts=parts),
+        grid=(f // FT,),
+        in_specs=[
+            pl.BlockSpec(memory_space=pltpu.SMEM),
+            tile,
+            weight,
+            weight,
+            once((TILE, d)),
+            pl.BlockSpec((n, 1), lambda i: (chunk, 0), pipeline_mode=pl.Buffered(1)),
+        ]
+        + [once(block.shape) for block in blocks]
+        + [pl.BlockSpec(memory_space=pl.ANY) for _ in kept],
+        out_specs=[tile, tile, tile, fixed((n, TILE)), fixed((TILE, d))] + [fixed(block.shape) for block in blocks],
+        out_shape=[jax.ShapeDtypeStruct((2 * n, f), jnp.bfloat16)] * 3
+        + [jax.ShapeDtypeStruct((n, TILE), jnp.float32), jax.ShapeDtypeStruct((TILE, d), jnp.float32)]
+        + [jax.ShapeDtypeStruct(block.shape, jnp.bfloat16) for block in blocks],
+        scratch_shapes=[
+            pltpu.VMEM((n, d), jnp.bfloat16),
+            pltpu.VMEM((n, d), jnp.float32),
+            pltpu.VMEM((n, TILE), jnp.float32),
+        ],
+        input_output_aliases={6 + ways + k: k for k in range(len(kept))},
+        cost_estimate=LARGE if chunk else SMALL,
+        name="expert_rows",
+    )(own, slope, wg, wu, wr, other, *blocks, *kept)
+    return (hidden, gate, up), share, router, pairs
+
+
+def slope_kernel(wd_ref, *refs, capacity):
+    blocks, (out_ref, u_ref) = refs[:-2], refs[-2:]
+
+    @pl.when(pl.program_id(0) == 0)
+    def _():
+        for block, at, base in spans(blocks, capacity, EXTRA):
+            u_ref[base : base + capacity, :] = block[at : at + capacity, :]
+
+    out_ref[...] = dot(u_ref[...], wd_ref[...], NT).astype(jnp.bfloat16)
+
+
+def slope_rows(blocks, wd, experts, capacity):
+    f, d = wd.shape
+    n = experts * capacity
     return pl.pallas_call(
-        lambda *refs: expert_kernel(*refs, parts=parts),
+        lambda *refs: slope_kernel(*refs, capacity=capacity),
         grid=(f // FT,),
-        in_specs=[whole, tile, weight, weight],
-        out_specs=[tile, tile, tile, whole, pl.BlockSpec((n, TILE), lambda i: (0, 0))],
-        out_shape=[jax.ShapeDtypeStruct((n, f), jnp.bfloat16)] * 3
-        + [jax.ShapeDtypeStruct((n, d), jnp.bfloat16), jax.ShapeDtypeStruct((n, TILE), jnp.float32)],
-        scratch_shapes=[pltpu.VMEM((n, d), jnp.float32)],
-        name="expert_rows",
-    )(x, slope, wg, wu)
-
-
-def slope_kernel(u_ref, wd_ref, out_ref):
-    out_ref[...] = dot(u_ref[...], wd_ref[...], NT).astype(jnp.bfloat16)
-
-
-def slope_rows(u, wd):
-    n, d = u.shape
-    f = wd.shape[0]
-    return pl.pallas_call(
-        slope_kernel,
-        grid=(f // FT,),
-        in_specs=[pl.BlockSpec((n, d), lambda i: (0, 0)), pl.BlockSpec((FT, d), lambda i: (i, 0))],
+        in_specs=[pl.BlockSpec((FT, d), lambda i: (i, 0))] + [once(block.shape) for block in blocks],
         out_specs=pl.BlockSpec((n, FT), lambda i: (0, i)),
         out_shape=jax.ShapeDtypeStruct((n, f), jnp.bfloat16),
+        scratch_shapes=[pltpu.VMEM((n, d), jnp.bfloat16)],
+        cost_estimate=LARGE,
         name="slope_rows",
-    )(u, wd)
-
-
-def down_kernel(h_ref, u_ref, out_ref):
-    out_ref[...] = dot(h_ref[...], u_ref[...], TN).astype(jnp.bfloat16)
-
-
-def down_grads(h, u):
-    n, f = h.shape
-    d = u.shape[1]
+    )(wd, *blocks)
+
+
+def weight_kernel(hidden, gate, up, wd_ref, near_ref, far_ref, *refs, ways, copies, capacity):
+    rows, raw, refs = refs[:ways], refs[ways : 2 * ways], refs[2 * ways :]
+    out_ref, results, refs = refs[0], refs[1 : 1 + ways], refs[1 + ways :]
+    rows_ref, raw_ref, acc_ref, stage_ref, down_ref, done_ref, sent_ref = refs
+    step = pl.program_id(0)
+    steps = pl.num_programs(0)
+    d = stage_ref.shape[2] // 2
+    piece = d // copies
+    part_of = out_ref.shape[0] // copies
+
+    def whole(at):
+        return pltpu.make_async_copy(
+            stage_ref.at[at % 2], out_ref.at[pl.ds(pl.multiple_of(at * FT, FT), FT), 0 : 2 * d], done_ref.at[at % 2]
+        )
+
+    def small(at, part, copy):
+        row = at * FT + part * 64
+        column = pl.multiple_of(2 * d + row // part_of * piece, piece)
+        return pltpu.make_async_copy(
+            down_ref.at[at % 2, part * 64 : (part + 1) * 64, copy * piece : (copy + 1) * piece],
+            out_ref.at[pl.ds(pl.multiple_of(copy * part_of + row % part_of, 64), 64), pl.ds(column, piece)],
+            sent_ref.at[at % 2, part, copy],
+        )
+
+    def finish(at):
+        whole(at).wait()
+        for part in range(FT // 64):
+            for copy in range(copies):
+                small(at, part, copy).wait()
+
+    @pl.when(step == 0)
+    def _():
+        acc_ref[...] = jnp.zeros_like(acc_ref)
+        for target_ref, blocks, extra in ((rows_ref, rows, 0), (raw_ref, raw, EXTRA)):
+            for block, at, base in spans(blocks, capacity, extra):
+                share_ref, start = (near_ref, base) if base < near_ref.shape[0] else (far_ref, base - near_ref.shape[0])
+                share = share_ref[start : start + capacity, 0:1]
+                value = block[at : at + capacity, :].astype(jnp.float32) * share
+                target_ref[base : base + capacity, :] = value.astype(jnp.bfloat16)
+
+    @pl.when(step >= 2)
+    def _():
+        finish(step - 2)
+
+    slot = step % 2
+    stage_ref[slot, :, 0:d] = dot(gate[...], rows_ref[...], TN).astype(jnp.bfloat16)
+    stage_ref[slot, :, d : 2 * d] = dot(up[...], rows_ref[...], TN).astype(jnp.bfloat16)
+    down_ref[slot] = dot(hidden[...], raw_ref[...], TN).astype(jnp.bfloat16)
+    acc_ref[...] += dot(hidden[...], wd_ref[...])
+    whole(step).start()
+    for part in range(FT // 64):
+        for copy in range(copies):
+            small(step, part, copy).start()
+
+    @pl.when(step == steps - 1)
+    def _():
+        base = 0
+        for result in results:
+            result[...] = acc_ref[base : base + result.shape[0], :].astype(jnp.bfloat16)
+            base += result.shape[0]
+        finish(step - 1)
+        finish(step)
+
+
+def weight_grads(hidden, gate, up, wd, shares, rows, raw, copies, capacity):
+    n, f = hidden.shape
+    d = wd.shape[1]
+    ways = len(rows)
+    narrow = pl.BlockSpec((n, FT), lambda i: (0, i))
+    grad, *results = pl.pallas_call(
+        lambda *refs: weight_kernel(*refs, ways=ways, copies=copies, capacity=capacity),
+        grid=(f // FT,),
+        in_specs=[narrow] * 3
+        + [pl.BlockSpec((FT, d), lambda i: (i, 0))]
+        + [once(part.shape) for part in (*shares, *rows, *raw)],
+        out_specs=[pl.BlockSpec(memory_space=pl.ANY)] + [pl.BlockSpec(part.shape, lambda i: (0, 0)) for part in rows],
+        out_shape=[jax.ShapeDtypeStruct((f, 3 * d), jnp.bfloat16)]
+        + [jax.ShapeDtypeStruct(part.shape, jnp.bfloat16) for part in rows],
+        scratch_shapes=[
+            pltpu.VMEM((n, d), jnp.bfloat16),
+            pltpu.VMEM((n, d), jnp.bfloat16),
+            pltpu.VMEM((n, d), jnp.float32),
+            pltpu.VMEM((2, FT, 2 * d), jnp.bfloat16),
+            pltpu.VMEM((2, FT, d), jnp.bfloat16),
+            pltpu.SemaphoreType.DMA((2,)),
+            pltpu.SemaphoreType.DMA((2, FT // 64, copies)),
+        ],
+        cost_estimate=SMALL,
+        name="weight_grads",
+    )(hidden, gate, up, wd, *shares, *rows, *raw)
+    return grad, results
+
+
+def shared_kernel(core_ref, first_ref, wide_ref, second_ref, narrow_ref, mine_ref, away_ref, *, steps, unit):
+    step = pl.program_id(0)
+
+    def store(value):
+        own = core_ref[0] == 0
+        for group in range(mine_ref.shape[0] // unit):
+            low = value[2 * group * unit : (2 * group + 1) * unit, :]
+            high = value[(2 * group + 1) * unit : (2 * group + 2) * unit, :]
+            span = slice(group * unit, (group + 1) * unit)
+            mine_ref[span, :] = jnp.where(own, low, high).astype(jnp.bfloat16)
+            away_ref[span, :] = jnp.where(own, high, low).astype(jnp.bfloat16)
+
+    @pl.when(step < steps)
+    def _():
+        store(dot(first_ref[...], wide_ref[...], TN))
+
+    @pl.when(step >= steps)
+    def _():
+        store(dot(second_ref[...], narrow_ref[...], TN))
+
+
+def shared_grads(core, first, wide, second, narrow, unit):
+    tokens, rows = first.shape
+    tile = 512
+    steps, more = wide.shape[1] // tile, narrow.shape[1] // tile
+    whole = once((tokens, rows))
+    out = pl.BlockSpec((rows // 2, tile), lambda i: (0, i))
+    shape = jax.ShapeDtypeStruct((rows // 2, wide.shape[1] + narrow.shape[1]), jnp.bfloat16)
     return pl.pallas_call(
-        down_kernel,
-        grid=(f // FT,),
-        in_specs=[pl.BlockSpec((n, FT), lambda i: (0, i)), pl.BlockSpec((n, d), lambda i: (0, 0))],
-        out_specs=pl.BlockSpec((FT, d), lambda i: (i, 0)),
-        out_shape=jax.ShapeDtypeStruct((f, d), jnp.bfloat16),
-        name="down_grads",
-    )(h, u)
-
-
-def gate_up_kernel(g_ref, p_ref, x_ref, out_ref):
-    d = x_ref.shape[1]
-    out_ref[:, 0:d] = dot(g_ref[...], x_ref[...], TN).astype(jnp.bfloat16)
-    out_ref[:, d : 2 * d] = dot(p_ref[...], x_ref[...], TN).astype(jnp.bfloat16)
-
-
-def gate_up_grads(g, p, x):
-    n, f = g.shape
-    d = x.shape[1]
-    tile = pl.BlockSpec((n, FT), lambda i: (0, i))
-    return pl.pallas_call(
-        gate_up_kernel,
-        grid=(f // FT,),
-        in_specs=[tile, tile, pl.BlockSpec((n, d), lambda i: (0, 0))],
-        out_specs=pl.BlockSpec((FT, 2 * d), lambda i: (i, 0)),
-        out_shape=jax.ShapeDtypeStruct((f, 2 * d), jnp.bfloat16),
-        name="gate_up_grads",
-    )(g, p, x)
+        lambda *refs: shared_kernel(*refs, steps=steps, unit=unit),
+        grid=(steps + more,),
+        in_specs=[
+            pl.BlockSpec(memory_space=pltpu.SMEM),
+            whole,
+            pl.BlockSpec((tokens, tile), lambda i: (0, jnp.minimum(i, steps - 1))),
+            whole,
+            pl.BlockSpec((tokens, tile), lambda i: (0, jnp.maximum(i - steps, 0))),
+        ],
+        out_specs=[out, out],
+        out_shape=[shape, shape],
+        cost_estimate=SMALL,
+        name="shared_grads",
+    )(core, first, wide, second, narrow)
+
+
+def after(value, *before):
+    return lax.optimization_barrier((value,) + before)[0]
+
+
+def swap(value, axis, step):
+    size = lax.axis_size(axis)
+    return lax.ppermute(value, axis, [(k, k ^ step) for k in range(size)])
+
+
+def direct_sum(pieces, axis, stride):
+    total = pieces[0].astype(jnp.float32)
+    for step, piece in enumerate(pieces[1:], 1):
+        total = total + swap(piece, axis, step * stride).astype(jnp.float32)
+    return total
+
+
+def over_all(mine, away, unit, *wait):
+    copies, chips = lax.axis_size("dp"), lax.axis_size("expert") // 2
+    other = swap(after(away, *wait), "expert", 1)
+    parts = [array.reshape(copies, chips * unit, -1) for array in (mine, other)]
+    place = lax.axis_index("dp")
+    pieces = []
+    for step in range(copies):
+        both = [lax.dynamic_index_in_dim(part, place ^ step, 0, keepdims=False) for part in parts]
+        pieces.append((both[0].astype(jnp.float32) + both[1].astype(jnp.float32)).astype(jnp.bfloat16))
+    half = direct_sum(pieces, "dp", 1).astype(jnp.bfloat16).reshape(chips, unit, -1)
+    place = lax.axis_index("expert") // 2
+    half = [lax.dynamic_index_in_dim(half, place ^ step, 0, keepdims=False) for step in range(chips)]
+    return pieces, half, direct_sum(half, "expert", 2)
 
 
 def on_device(
@@ -369,38 +715,33 @@
     tokens, width = block_input.shape
     experts = w_router.shape[1]
     capacity = TOK_DEV * TOP * 5 // (4 * experts)
+    slots = experts * capacity
     buckets = rel_table.shape[0]
-    slots = experts * capacity
-    ways = lax.axis_size("expert")
-    copies = lax.axis_size("dp")
-    core = lax.axis_index("expert") % 2
+    copies, ways = lax.axis_size("dp"), lax.axis_size("expert")
+    place = lax.axis_index("expert").astype(jnp.int32)
+    own = place.reshape(1)
     labels = jnp.arange(experts, dtype=jnp.int32)
     picks = [routes[:, rank : rank + 1] == labels[None, :] for rank in range(TOP)]
-    named = (picks[0] | picks[1]).astype(jnp.bfloat16)
-    ticks = jnp.arange(tokens, dtype=jnp.int32)
-    earlier = (ticks[:, None] > ticks[None, :]).astype(jnp.bfloat16)
-    count = dot(earlier, named)
-    starts = (labels * capacity).astype(jnp.float32)
-    target = [
-        jnp.sum(jnp.where(pick, count + starts[None, :], 0.0), axis=1, keepdims=True).astype(jnp.int32)
-        for pick in picks
-    ]
     places = jnp.arange(slots, dtype=jnp.int32)
-    routing = [(target[rank] == places[None, :]) for rank in range(TOP)]
-    either = (routing[0] | routing[1]).astype(jnp.bfloat16)
-
-    def pack(rows):
-        return dot(either, rows, TN).astype(jnp.bfloat16)
-
-    def exchange(rows):
-        shape = rows.shape
-        return lax.all_to_all(
-            rows.reshape((experts, capacity) + shape[1:]), "expert", split_axis=0, concat_axis=0, tiled=True
-        ).reshape(shape)
-
-    packed = pack(cotangent)
-    packed, block_input = lax.optimization_barrier((packed, block_input))
+
+    half = ways // 2
+    groups = [list(range(k * half, (k + 1) * half)) for k in range(2)]
+
+    def near(block):
+        parts = block.reshape(half, -1, block.shape[1])
+        parts = lax.all_to_all(parts, "expert", split_axis=0, concat_axis=0, axis_index_groups=groups, tiled=True)
+        return parts.reshape(block.shape)
+
+    def exchange(blocks):
+        far = [swap(block, "expert", half + step) for step, block in enumerate(blocks[1:])]
+        return [near(blocks[0])] + far
+
+    packed, target_rows = pack_first(own, routes.T, cotangent, experts, capacity)
+    target = target_rows.T
     raw = exchange(packed)
+    block_input = after(block_input, *packed)
+    other = [block[at + capacity, :capacity] for block, at, _ in spans(raw, capacity, EXTRA)]
+    other = jnp.stack(other).astype(jnp.float32).reshape(slots, 1)
     inputs = block_input.astype(jnp.float32)
     normed, unit_one, scale_one = normalize_forward(inputs, gain_attn)
     attn_in = normed.astype(jnp.bfloat16)
@@ -411,76 +752,59 @@
     resid = inputs + attn
     second, unit_two, scale_two = normalize_forward(resid, gain_moe)
     moe_in = second.astype(jnp.bfloat16)
-    packed = pack(moe_in)
-    packed, raw = lax.optimization_barrier((packed, raw))
-    rows = exchange(packed)
+    rows = exchange(pack(target_rows, after(moe_in, *raw), experts, capacity))
     logits = dot(moe_in, w_router)
     chosen = jnp.stack([jnp.sum(jnp.where(pick, logits, 0.0), axis=1) for pick in picks], axis=1)
     highest = jnp.max(chosen, axis=1, keepdims=True)
     exps = jnp.exp(chosen - highest)
     gates = exps / jnp.sum(exps, axis=1, keepdims=True)
-    gated = jnp.where(routing[0], gates[:, 0:1], 0.0) + jnp.where(routing[1], gates[:, 1:2], 0.0)
-    slot_gates = exchange(jnp.sum(gated, axis=0))[:, None]
-    gated = gated.astype(jnp.bfloat16)
     gate_weight, up_weight, down_weight = w_gate[0], w_up[0], w_down[0]
-    slope = slope_rows(raw, down_weight)
-    hidden, gate_pre_grad, up_pre_grad, pair_grad, dots = expert_rows(rows, slope, gate_weight, up_weight)
-    back = exchange(pair_grad)
-    slot_dots = exchange(jnp.sum(dots, axis=1))[None, :]
-    gated_raw = (raw.astype(jnp.float32) * slot_gates).astype(jnp.bfloat16)
-    gated_rows = (rows.astype(jnp.float32) * slot_gates).astype(jnp.bfloat16)
-    down_grad = down_grads(hidden, gated_raw)
-    down_sum = lax.psum_scatter(down_grad, "dp", scatter_dimension=1, tiled=True)
-    gate_up_grad = gate_up_grads(gate_pre_grad, up_pre_grad, gated_rows)
-    gate_up_sum = lax.psum_scatter(gate_up_grad, "dp", scatter_dimension=0, tiled=True)
-    result = dot(hidden, down_weight).astype(jnp.bfloat16)
-    back, result, down_grad, gate_up_grad = lax.optimization_barrier((back, result, down_grad, gate_up_grad))
+    router_rows = jnp.pad(w_router.T, ((0, TILE - experts), (0, 0)))
+    slope = slope_rows(raw, down_weight, experts, capacity)
+    weights = (gate_weight, up_weight, router_rows, other)
+    kept, near_share, near_router, near_pairs = expert_rows(own, rows[:1], slope, *weights, 0, ())
+    back = [near(near_pairs[0])]
+    rows[1:] = [after(block, near_pairs[0]) for block in rows[1:]]
+    kept, far_share, far_router, far_pairs = expert_rows(own, rows[1:], slope, *weights, 1, kept)
+    back += [swap(block, "expert", half + step) for step, block in enumerate(far_pairs)]
+    hidden, gate_pre_grad, up_pre_grad = kept
+    weight_grad, result = weight_grads(
+        after(hidden, back[0]),
+        gate_pre_grad,
+        up_pre_grad,
+        down_weight,
+        (near_share, far_share),
+        rows,
+        raw,
+        copies,
+        capacity,
+    )
+    weight_sum = lax.psum_scatter(weight_grad, "dp", scatter_dimension=0, tiled=True)
+    *back, held = lax.optimization_barrier((*back, result[0]))
+    result = [after(block, *back) for block in (held, *result[1:])]
     returned = exchange(result)
-
-    def halve(grad):
-        parts = grad.reshape(copies, ways // 2, 2, -1, grad.shape[1])
-        away = lax.dynamic_index_in_dim(parts, 1 - core, 2, keepdims=False).astype(jnp.bfloat16)
-        mine = lax.dynamic_index_in_dim(parts, core, 2, keepdims=False)
-        other = lax.ppermute(away, "expert", [(k, k ^ 1) for k in range(ways)])
-        return (mine + other.astype(jnp.float32)).astype(jnp.bfloat16)
-
-    def over_all(grad):
-        half = halve(grad)
-        half = lax.all_to_all(half, "dp", split_axis=0, concat_axis=0, tiled=True)
-        part = jnp.sum(half.astype(jnp.float32), axis=0).astype(jnp.bfloat16)
-        groups = [list(range(0, ways, 2)), list(range(1, ways, 2))]
-        part = lax.all_to_all(
-            part, "expert", split_axis=0, concat_axis=0, axis_index_groups=groups, tiled=True
-        )
-        return jnp.sum(part.astype(jnp.float32), axis=0)
-
-    gate_grads = [jnp.sum(jnp.where(routing[rank], slot_dots, 0.0), axis=1) for rank in range(TOP)]
-    average = gates[:, 0] * gate_grads[0] + gates[:, 1] * gate_grads[1]
-    dlogits = jnp.zeros_like(logits)
-    for rank in range(TOP):
-        logit_grad = gates[:, rank] * (gate_grads[rank] - average)
-        dlogits = dlogits + jnp.where(picks[rank], logit_grad[:, None], 0.0)
-    dlogits = dlogits.astype(jnp.bfloat16)
-    router_grad = dot(moe_in, dlogits, TN)
-    moe_in_grad = dot(dlogits, w_router, NT) + dot(gated, back)
-    upstream = cotangent.astype(jnp.float32)
-    resid_norm_grad, gain_moe_grad = normalize_backward(moe_in_grad, unit_two, scale_two, gain_moe)
-    resid_grad = upstream + resid_norm_grad
-    attn_grad = resid_grad.astype(jnp.bfloat16)
-    out_weight_sum = over_all(dot(mixed, attn_grad, TN))
+    resid_grad, attn_grad, gain_moe_grad = combine(
+        target, gates, resid, scale_two, gain_moe.reshape(1, width), cotangent, back
+    )
     mixed_grad = dot(attn_grad, w_attn_out, NT).astype(jnp.bfloat16)
     proj_grad, tiles = attention_backward(item_lengths, bias, stat, proj, mixed, mixed_grad)
+    unit = width // (copies * ways)
+    mine, away = shared_grads(own % 2, attn_in, proj_grad, mixed, attn_grad, unit)
+    mine, half_sums, sums = over_all(mine, away, unit, *returned)
+    proj_grad = after(proj_grad, *mine)
     table_grad = table_sums(tiles, buckets)
-    qkv_grad = jnp.concatenate([dot(attn_in, proj_grad[k], TN) for k in range(3)], axis=1)
-    qkv_sum = over_all(qkv_grad)
-    attn_in_grad = sum(dot(proj_grad[k], w_qkv[:, k * width : (k + 1) * width], NT) for k in range(3))
+    router_grad = (near_router + far_router)[:experts].T
+    attn_in_grad = dot(proj_grad, w_qkv, NT)
     input_norm_grad, gain_attn_grad = normalize_backward(attn_in_grad, unit_one, scale_one, gain_attn)
     input_grad = resid_grad + input_norm_grad
-    output = (resid + dot(gated, returned)).astype(jnp.bfloat16)
-    devices = copies * ways
+    output = combine_output(target, gates, after(resid, *half_sums), returned)
+    piece = width // copies
+    down_sum = jnp.concatenate(
+        [weight_sum[:, 2 * width + k * piece : 2 * width + (k + 1) * piece] for k in range(copies)], axis=0
+    )
     small = (table_grad.reshape(-1), gain_attn_grad, gain_moe_grad, router_grad)
-    sizes = [part.size // devices for part in small]
-    together = jnp.concatenate([part.reshape(devices, -1) for part in small], axis=1)
+    sizes = [part.size // (copies * ways) for part in small]
+    together = jnp.concatenate([part.reshape(copies * ways, -1) for part in small], axis=1)
     together = lax.all_to_all(together, ("dp", "expert"), split_axis=0, concat_axis=0, tiled=True)
     together = jnp.sum(together, axis=0)
     at = [sum(sizes[:k]) for k in range(5)]
@@ -488,14 +812,14 @@
     return (
         output,
         input_grad,
-        qkv_sum,
-        out_weight_sum,
+        sums[:, : 3 * width],
+        sums[:, 3 * width :],
         table_sum,
         attn_sum,
         moe_sum,
         router_sum.reshape(-1, experts),
-        gate_up_sum[:, :width].astype(jnp.float32).T[None],
-        gate_up_sum[:, width:].astype(jnp.float32).T[None],
+        weight_sum[:, :width].astype(jnp.float32).T[None],
+        weight_sum[:, width : 2 * width].astype(jnp.float32).T[None],
         down_sum.astype(jnp.float32)[None],
     )
 

time: 652 us -> 517 us (0.79)
  waiting for transfers between devices: 226 us -> 89.5 us
  starting transfers between devices: 40 us -> 112 us
  Pallas kernels: 154 us -> 217 us
  matrix products: 86.9 us -> 31 us
  blocking collectives: 48.4 us -> 0 us
  other arithmetic: 44.5 us -> 24.8 us
    all_to_all x8 -> x4, waiting for transfers between devices: 220 us -> 12.2 us  [near(): lax.all_to_all(parts, 'expert', split_axis=0, concat_axis=0, axis_index_g...]
    ppermute x2 -> x23, waiting for transfers between devices: 0.01 us -> 74.7 us  [swap(): return lax.ppermute(value, axis, [(k, k ^ step) for k in range(size)])]
    pallas_call x4 -> x9, Pallas kernels: 116 us -> 178 us  [the longest x2 67.5 us: expert_rows(): pl.pallas_call(lambda *refs: expert_kernel(*refs, ways=ways, parts=parts)...]
    ppermute x2 -> x23, starting transfers between devices: 0.51 us -> 60.5 us  [swap(): return lax.ppermute(value, axis, [(k, k ^ step) for k in range(size)])]
    dot_general x19 -> x5, matrix products: 80.8 us -> 24.9 us  [dot(): return lax.dot_general(a, b, dims, preferred_element_type=jnp.float32)]
    all_to_all x2 -> x0, blocking collectives: 48.4 us -> none  [the longest x1 40.4 us: over_all(): half = lax.all_to_all(half, 'dp', split_axis=0, concat_axis=0, tiled=True)]
    all_to_all x8 -> x4, starting transfers between devices: 34.5 us -> 46.5 us  [near(): lax.all_to_all(parts, 'expert', split_axis=0, concat_axis=0, axis_index_g...]
    concatenate x1, local copies, waits for them, and re-layouts: 13.1 us -> 1.42 us  [on_device(): jnp.concatenate([weight_sum[:, 2 * width + k * piece:2 * width + (k + 1)...]
  transfers between devices with their start and end apart: 13 -> 29, of which waited for: 9 -> 8; matrix products, arithmetic and copies ran while one was open for 21% -> 13% of each run, Pallas kernels for 13% -> 40%
where the time goes in v2:
time: 517 us; the launch traced here: 512 us
  Pallas kernels  217 us (42%)
  starting transfers between devices  112 us (22%)
  waiting for transfers between devices  89.5 us (17%)
  matrix products  31 us (6%)
  other arithmetic  24.8 us (5%)
  local copies, waits for them, and re-layouts  22.8 us (4%)
  between operations  15.1 us (3%)
    ppermute x23, waiting for transfers between devices, swap(): return lax.ppermute(value, axis, [(k, k ^ step) for k in range(size)])  74.7 us
    pallas_call x2, Pallas kernels, expert_rows(): pl.pallas_call(lambda *refs: expert_kernel(*refs, ways=ways, parts=parts)...  67.5 us
    ppermute x23, starting transfers between devices, swap(): return lax.ppermute(value, axis, [(k, k ^ step) for k in range(size)])  60.5 us
    pallas_call x1, Pallas kernels, weight_grads(): pl.pallas_call(lambda *refs: weight_kernel(*refs, ways=ways, copies=copie...  53 us
    all_to_all x4, starting transfers between devices, near(): lax.all_to_all(parts, 'expert', split_axis=0, concat_axis=0, axis_index_g...  46.5 us
    dot_general x5, matrix products, dot(): return lax.dot_general(a, b, dims, preferred_element_type=jnp.float32)  24.9 us
    pallas_call x1, Pallas kernels, attention_backward(): pl.pallas_call(attention_backward_kernel, grid=(pairs,), in_specs=[pl.Blo...  22.8 us
    pallas_call x1, Pallas kernels, slope_rows(): pl.pallas_call(lambda *refs: slope_kernel(*refs, capacity=capacity), grid...  16.4 us
  transfers between devices with their start and end apart: 29, of which 8 were waited for; matrix products, arithmetic and copies ran while one was open for 13% of the time, Pallas kernels for 40%

profile of v2, /device:TPU:0, one launch (start us, length us, event | category | flops | bytes accessed | tf_op | source)
XLA Modules:
  0.0 512.4 jit_solution(4477653616159944980)
XLA Ops:
  7.2 6.2 %pack_first.1 = (bf16[832,1024]{1,0:T(8,128)(2,1)}, bf16[208,1024]{1,0:T(8,128)(2,1)}, bf16[208,1024]{1,0:T(8,128)(2,1)}, bf16[208,1024]{1,0:T(8,128)(2,1)}, bf1...) custom-call(s32[1]{0:T(128)} %bitcast.refs_0_, s32[2,640]{1,0:T(2,128)} %bitcast.97, bf16[640,1024]{1,0:T(8,128)(2,1)} %upstream_ref.1), custom_call_target="tpu_custom_call" | custom-call | flops 1048576 | bytes 65536 | tf_op jit(solution)/shard_map/pack_first/pallas_call | solution.py:322
  29.8 8.5 %convolution_convert_fusion.q_ref.k_ref.v_ref = bf16[640,3072]{1,0:T(8,128)(2,1)} fusion(bf16[640,1024]{1,0:T(8,128)(2,1)S(1)} %fusion.9.refs_1_, bf16[1024,3072]{1,0:T(8,128)(2,1)} %param.16), kind=kOutput, calls=%fused_computation.3 | convolution fusion | flops 4028497920 | bytes 11534336 | tf_op jit(solution)/shard_map/dot_general | solution.py:30
  38.3 16.0 %attention_forward.1 = (bf16[640,1024]{1,0:T(8,128)(2,1)}, f32[8,2,640]{2,1,0:T(2,128)}) custom-call(s32[1,2]{1,0:T(1,128)} %lengths_ref.3, f32[8,2,512]{2,1,0:T(2,128)} %reshape.326.bias_ref, bf16[640,3072]{1,0:T(8,128)(2,1)} %convolution_convert_fusion.q_ref.k_ref.v_ref, bf16[640,3072]{1,0:T(8,128)(2,1)} %convolution_convert_fusion.q_ref.k_ref.v_ref, ...), custom_call_target="tpu_custom_call" | custom-call | flops 1048576 | bytes 65536 | tf_op jit(solution)/shard_map/attention_forward/pallas_call | solution.py:109
  62.8 8.4 %collective-permute-done.2.refs_4_.refs_14_ = bf16[208,1024]{1,0:T(8,128)(2,1)} collective-permute-done((bf16[208,1024]{1,0:T(8,128)(2,1)}, bf16[208,1024]{1,0:T(8,128)(2,1)}, u32[]{:S(2)}, u32[]{:S(2)}) %collective-permute-start.2) | collective-permute-done | bytes 426016 | tf_op jit(solution)/shard_map/ppermute | solution.py:675
  72.5 6.9 %collective-permute-done.3.refs_5_.refs_15_ = bf16[208,1024]{1,0:T(8,128)(2,1)} collective-permute-done((bf16[208,1024]{1,0:T(8,128)(2,1)}, bf16[208,1024]{1,0:T(8,128)(2,1)}, u32[]{:S(2)}, u32[]{:S(2)}) %collective-permute-start.3) | collective-permute-done | bytes 426016 | tf_op jit(solution)/shard_map/ppermute | solution.py:675
  85.5 20.5 %all-to-all-start.1 = ((bf16[4,200,1024]{2,1,0:T(8,128)(2,1)}), bf16[4,200,1024]{2,1,0:T(8,128)(2,1)}, u32[]{:S(2)}, u32[]{:S(2)}) async-start(bf16[4,200,1024]{2,1,0:T(8,128)(2,1)} %bitcast.92), calls=%async_computation.1 | async-start | bytes 3276800 | tf_op jit(solution)/shard_map/all_to_all | solution.py:732
  114.4 16.4 %slope_rows.1.refs_1_ = bf16[1600,2816]{1,0:T(8,128)(2,1)} custom-call(bf16[2816,1024]{1,0:T(8,128)(2,1)} %bitcast.79, bf16[832,1024]{1,0:T(8,128)(2,1)} %bitcast.7.refs_1_.refs_11_, bf16[208,1024]{1,0:T(8,128)(2,1)} %collective-permute-done.refs_2_.refs_12_, bf16[208,1024]{1,0:T(8,128)(2,1)} %collective-permute-done.1.refs_3_.refs_13_, ...), custom_call_target="tpu_custom_call" | custom-call | flops 274877906944 | bytes 268435456 | tf_op jit(solution)/shard_map/slope_rows/pallas_call | solution.py:519
  132.7 12.1 %all-to-all-done.1 = bf16[4,200,1024]{2,1,0:T(8,128)(2,1)} async-done(((bf16[4,200,1024]{2,1,0:T(8,128)(2,1)}), bf16[4,200,1024]{2,1,0:T(8,128)(2,1)}, u32[]{:S(2)}, u32[]{:S(2)}) %all-to-all-start.1) | async-done | bytes 1638432 | tf_op jit(solution)/shard_map/all_to_all | solution.py:732
  144.9 33.6 %expert_rows.2 = (bf16[1600,2816]{1,0:T(8,128)(2,1)}, bf16[1600,2816]{1,0:T(8,128)(2,1)}, bf16[1600,2816]{1,0:T(8,128)(2,1)}, f32[800,128]{1,0:T(8,128)}, f32[12...) custom-call(s32[1]{0:T(128)} %bitcast.refs_0_, bf16[1600,2816]{1,0:T(8,128)(2,1)} %slope_rows.1.refs_1_, ...), custom_call_target="tpu_custom_call" | custom-call | flops 1048576 | bytes 65536 | tf_op jit(solution)/shard_map/expert_rows/pallas_call | solution.py:476
  183.1 33.8 %expert_rows.3 = (bf16[1600,2816]{1,0:T(8,128)(2,1)}, bf16[1600,2816]{1,0:T(8,128)(2,1)}, bf16[1600,2816]{1,0:T(8,128)(2,1)}, f32[800,128]{1,0:T(8,128)}, f32[12...) custom-call(s32[1]{0:T(128)} %bitcast.refs_0_, ...), custom_call_target="tpu_custom_call", output_to_operand_aliasing={{0}: (10, {}), {1}: (11, {}), {2}: (12, {})} | custom-call | flops 274877906944 | bytes 268435456 | tf_op jit(solution)/shard_map/expert_rows/pallas_call | solution.py:476
  223.3 53.0 %weight_grads.1 = (bf16[2816,3072]{1,0:T(8,128)(2,1)}, bf16[800,1024]{1,0:T(8,128)(2,1)}, bf16[200,1024]{1,0:T(8,128)(2,1)}, bf16[200,1024]{1,0:T(8,128)(2,1)}, ...) custom-call(bf16[1600,2816]{1,0:T(8,128)(2,1)} %get-tuple-element.101.refs_0_, ...), custom_call_target="tpu_custom_call" | custom-call | flops 1048576 | bytes 65536 | tf_op jit(solution)/shard_map/weight_grads/pallas_call | solution.py:600
  276.4 16.8 %all-to-all-start.3 = ((bf16[4,200,1024]{2,1,0:T(8,128)(2,1)}), bf16[4,200,1024]{2,1,0:T(8,128)(2,1)}, u32[]{:S(2)}, u32[]{:S(2)}) async-start(bf16[4,200,1024]{2,1,0:T(8,128)(2,1)} %bitcast.90), calls=%async_computation.3 | async-start | bytes 3276800 | tf_op jit(solution)/shard_map/all_to_all | solution.py:732
  303.8 9.7 %combine_back.1 = (f32[640,1024]{1,0:T(8,128)}, bf16[640,1024]{1,0:T(8,128)(2,1)}, f32[1,1024]{1,0:T(1,128)}) custom-call(s32[640,2]{1,0:T(8,128)} %bitcast.93, f32[640,2]{1,0:T(8,128)} %exponential_divide_fusion.gates_ref, f32[640,1024]{1,0:T(8,128)} %copy-done.4, f32[640,1]{1,0:T(8,128)} %rsqrt.16.scale_ref, f32[1,1024]{1,0:T(1,128)} %bitcast.98, ...), custom_call_target="tpu_custom_call" | custom-call | flops 1048576 | bytes 65536 | tf_op jit(solution)/shard_map/combine_back/pallas_call | solution.py:383
  317.4 22.8 %attention_backward.1 = (bf16[640,3072]{1,0:T(8,128)(2,1)}, f32[8,2,136,384]{3,2,1,0:T(8,128)}) custom-call(s32[1,2]{1,0:T(1,128)} %lengths_ref.3, f32[8,2,512]{2,1,0:T(2,128)} %reshape.326.bias_ref, f32[8,2,640]{2,1,0:T(2,128)} %get-tuple-element.81.stat_ref, bf16[640,3072]{1,0:T(8,128)(2,1)} %convolution_convert_fusion.q_ref.k_ref.v_ref, ...), custom_call_target="tpu_custom_call" | custom-call | flops 1048576 | bytes 65536 | tf_op jit(solution)/shard_map/attention_backward/pallas_call | solution.py:222
  340.2 13.4 %shared_grads.1 = (bf16[512,4096]{1,0:T(8,128)(2,1)}, bf16[512,4096]{1,0:T(8,128)(2,1)}) custom-call(s32[1]{0:T(128)S(6)} %select_n.84.refs_0_, bf16[640,1024]{1,0:T(8,128)(2,1)} %copy-done.5, bf16[640,3072]{1,0:T(8,128)(2,1)} %get-tuple-element.129.refs_2_, bf16[640,1024]{1,0:T(8,128)(2,1)} %get-tuple-element.80.mixed_ref.refs_3_, ...), custom_call_target="tpu_custom_call" | custom-call | flops 1048576 | bytes 65536 | tf_op jit(solution)/shard_map/shared_grads/pallas_call | solution.py:652
  354.2 7.2 %collective-permute-done.16 = bf16[512,4096]{1,0:T(8,128)(2,1)} collective-permute-done((bf16[512,4096]{1,0:T(8,128)(2,1)}, bf16[512,4096]{1,0:T(8,128)(2,1)}, u32[]{:S(2)}, u32[]{:S(2)}) %collective-permute-start.16) | collective-permute-done | bytes 4194336 | tf_op jit(solution)/shard_map/ppermute | solution.py:675
  361.5 5.2 %fusion.22 = (bf16[128,4096]{1,0:T(8,128)(2,1)}, bf16[128,4096]{1,0:T(8,128)(2,1)}, bf16[128,4096]{1,0:T(8,128)(2,1)}) fusion(bf16[4,128,4096]{2,1,0:T(8,128)(2,1)} %bitcast.18, s32[]{:T(128)S(6)} %select_n.86, bf16[4,128,4096]{2,1,0:T(8,128)(2,1)} %bitcast.85, s32[]{:T(128)S(6)} %select_n.88, s32[]{:T(128)S(6)} %select_n.87), kind=kLoop, calls=%fused_computation.34 | loop fusion | flops 6291456 | bytes 9437196 | tf_op jit(solution)/shard_map/convert_element_type | solution.py:693
  372.9 5.8 %fusion.16 = f32[32,8,2]{0,1,2:T(8,128)S(1)} fusion(f32[8,2,136,384]{3,2,1,0:T(8,128)} %get-tuple-element.130, s32[136,384]{1,0:T(8,128)S(1)} %fusion.26), kind=kOutput, calls=%fused_computation.32 | convolution fusion | flops 322535424 | bytes 3553280 | tf_op jit(solution)/shard_map/ghrc,rcb->bgh/dot_general | solution.py:275
  378.8 21.8 %collective-permute-done.19 = bf16[128,4096]{1,0:T(8,128)(2,1)} collective-permute-done((bf16[128,4096]{1,0:T(8,128)(2,1)}, bf16[128,4096]{1,0:T(8,128)(2,1)}, u32[]{:S(2)}, u32[]{:S(2)}) %collective-permute-start.19) | collective-permute-done | bytes 1048608 | tf_op jit(solution)/shard_map/ppermute | solution.py:675
  400.6 30.1 %collective-permute-done.18 = bf16[128,4096]{1,0:T(8,128)(2,1)} collective-permute-done((bf16[128,4096]{1,0:T(8,128)(2,1)}, bf16[128,4096]{1,0:T(8,128)(2,1)}, u32[]{:S(2)}, u32[]{:S(2)}) %collective-permute-start.18) | collective-permute-done | bytes 1048608 | tf_op jit(solution)/shard_map/ppermute | solution.py:675
  439.5 22.8 %collective-permute-start.21 = (bf16[32,4096]{1,0:T(8,128)(2,1)}, bf16[32,4096]{1,0:T(8,128)(2,1)}, u32[]{:S(2)}, u32[]{:S(2)}) collective-permute-start(bf16[32,4096]{1,0:T(8,128)(2,1)} %get-tuple-element.193), channel_id=1, source_target_pairs={{0,4},{1,5},{2,6},{3,7},{4,0},{5,1},{6,2},{7,3},{8,12},{9,13},{10,... | collective-permute-start | bytes 786440 | tf_op jit(solution)/shard_map/ppermute | solution.py:675
  462.9 9.0 %fusion.14 = (f32[1024]{0:T(1024)S(1)}, f32[640]{0:T(1024)S(1)}, f32[640,1024]{1,0:T(8,128)}) fusion(bf16[640,1024]{1,0:T(8,128)(2,1)S(1)} %copy-done.2, f32[640]{0:T(1024)S(1)} %copy-done.12, f32[1024]{0:T(1024)S(1)} %copy-done.18, bf16[640,3072]{1,0:T(8,128)(2,1)S(1)} %copy-done.8, bf16[1024,3072]{1,0:T(8,128)(2,1)} %param.16), kind=kOutput, calls=%fused_computation.20 | convolution fusion | flops 4031117824 | bytes 14169088 | tf_op jit(solution)/shard_map/dot_general | solution.py:30
  472.8 5.0 all-to-all-start.4
  489.9 7.2 %combine_output.1 = bf16[640,1024]{1,0:T(8,128)(2,1)} custom-call(s32[640,2]{1,0:T(8,128)} %bitcast.94, f32[640,2]{1,0:T(8,128)} %exponential_divide_fusion.gates_ref, f32[640,1024]{1,0:T(8,128)} %copy-done.4, bf16[800,1024]{1,0:T(8,128)(2,1)} %bitcast.17.refs_0_, bf16[200,1024]{1,0:T(8,128)(2,1)} %copy-done.25, bf16[200,1024]{1,0:T(8,128)(2,1)} %copy-done.26, ...), custom_call_target="tpu_custom_call" | custom-call | flops 230000001024 | bytes 65536 | tf_op jit(solution)/shard_map/combine_output/pallas_call | solution.py:360
  (167 shorter events, 104.9 us)
Async XLA Ops:
  13.4 67.2 %all-to-all-start = ((bf16[4,208,1024]{2,1,0:T(8,128)(2,1)}), bf16[4,208,1024]{2,1,0:T(8,128)(2,1)}, u32[]{:S(2)}, u32[]{:S(2)}) async-start(bf16[4,208,1024]{2,1,0:T(8,128)(2,1)} %bitcast.89), calls=%async_computation | async-start | bytes 3407872 | tf_op jit(solution)/shard_map/all_to_all | solution.py:732
  18.3 42.0 %collective-permute-start = (bf16[208,1024]{1,0:T(8,128)(2,1)}, bf16[208,1024]{1,0:T(8,128)(2,1)}, u32[]{:S(2)}, u32[]{:S(2)}) collective-permute-start(bf16[208,1024]{1,0:T(8,128)(2,1)} %get-tuple-element.75), channel_id=1, source_target_pairs={{0,4},{1,5},{2,6},{3,7},{4,0},{5,1},{6,2},{7,3},{8,12},{9,13},{10,... | collective-permute-start | bytes 1277960 | tf_op jit(solution)/shard_map/ppermute | solution.py:675
  22.5 48.7 %collective-permute-start.2 = (bf16[208,1024]{1,0:T(8,128)(2,1)}, bf16[208,1024]{1,0:T(8,128)(2,1)}, u32[]{:S(2)}, u32[]{:S(2)}) collective-permute-start(bf16[208,1024]{1,0:T(8,128)(2,1)} %get-tuple-element.77), channel_id=1, source_target_pairs={{0,6},{1,7},{2,4},{3,5},{4,2},{5,3},{6,0},{7,1},{8,14},{9,15},{10,... | collective-permute-start | bytes 1277960 | tf_op jit(solution)/shard_map/ppermute | solution.py:675
  26.2 53.2 %collective-permute-start.3 = (bf16[208,1024]{1,0:T(8,128)(2,1)}, bf16[208,1024]{1,0:T(8,128)(2,1)}, u32[]{:S(2)}, u32[]{:S(2)}) collective-permute-start(bf16[208,1024]{1,0:T(8,128)(2,1)} %get-tuple-element.78), channel_id=1, source_target_pairs={{0,7},{1,6},{2,5},{3,4},{4,3},{5,2},{6,1},{7,0},{8,15},{9,14},{10,... | collective-permute-start | bytes 1277960 | tf_op jit(solution)/shard_map/ppermute | solution.py:675
  85.5 59.3 %all-to-all-start.1 = ((bf16[4,200,1024]{2,1,0:T(8,128)(2,1)}), bf16[4,200,1024]{2,1,0:T(8,128)(2,1)}, u32[]{:S(2)}, u32[]{:S(2)}) async-start(bf16[4,200,1024]{2,1,0:T(8,128)(2,1)} %bitcast.92), calls=%async_computation.1 | async-start | bytes 3276800 | tf_op jit(solution)/shard_map/all_to_all | solution.py:732
  106.0 77.1 %collective-permute-start.4 = (bf16[200,1024]{1,0:T(8,128)(2,1)}, bf16[200,1024]{1,0:T(8,128)(2,1)}, u32[]{:S(2)}, u32[]{:S(2)}) collective-permute-start(bf16[200,1024]{1,0:T(8,128)(2,1)} %get-tuple-element.85), channel_id=1, source_target_pairs={{0,4},{1,5},{2,6},{3,7},{4,0},{5,1},{6,2},{7,3},{8,12},{9,13},{10,... | collective-permute-start | bytes 1228808 | tf_op jit(solution)/shard_map/ppermute | solution.py:675
  110.3 72.8 %collective-permute-start.5 = (bf16[200,1024]{1,0:T(8,128)(2,1)}, bf16[200,1024]{1,0:T(8,128)(2,1)}, u32[]{:S(2)}, u32[]{:S(2)}) collective-permute-start(bf16[200,1024]{1,0:T(8,128)(2,1)} %get-tuple-element.87), channel_id=1, source_target_pairs={{0,5},{1,4},{2,7},{3,6},{4,1},{5,0},{6,3},{7,2},{8,13},{9,12},{10,... | collective-permute-start | bytes 1228808 | tf_op jit(solution)/shard_map/ppermute | solution.py:675
  110.6 72.5 %collective-permute-start.6 = (bf16[200,1024]{1,0:T(8,128)(2,1)}, bf16[200,1024]{1,0:T(8,128)(2,1)}, u32[]{:S(2)}, u32[]{:S(2)}) collective-permute-start(bf16[200,1024]{1,0:T(8,128)(2,1)} %get-tuple-element.89), channel_id=1, source_target_pairs={{0,6},{1,7},{2,4},{3,5},{4,2},{5,3},{6,0},{7,1},{8,14},{9,15},{10,... | collective-permute-start | bytes 1228808 | tf_op jit(solution)/shard_map/ppermute | solution.py:675
  114.1 69.0 %collective-permute-start.7 = (bf16[200,1024]{1,0:T(8,128)(2,1)}, bf16[200,1024]{1,0:T(8,128)(2,1)}, u32[]{:S(2)}, u32[]{:S(2)}) collective-permute-start(bf16[200,1024]{1,0:T(8,128)(2,1)} %get-tuple-element.91), channel_id=1, source_target_pairs={{0,7},{1,6},{2,5},{3,4},{4,3},{5,2},{6,1},{7,0},{8,15},{9,14},{10,... | collective-permute-start | bytes 1228808 | tf_op jit(solution)/shard_map/ppermute | solution.py:675
  178.5 44.8 %all-to-all-start.2 = ((bf16[4,200,1024]{2,1,0:T(8,128)(2,1)}), bf16[4,200,1024]{2,1,0:T(8,128)(2,1)}, u32[]{:S(2)}, u32[]{:S(2)}) async-start(bf16[4,200,1024]{2,1,0:T(8,128)(2,1)} %bitcast.91), calls=%async_computation.2 | async-start | bytes 3276800 | tf_op jit(solution)/shard_map/all_to_all | solution.py:732
  182.8 314.2 %reduce-scatter.2.cloned.1.call-start = ((), (), s32[]{:S(2)}) async-start(), calls=%async_computation.6 | async-start | bytes 21626880 | tf_op jit(solution)/shard_map/reduce_scatter | solution.py:782
  217.0 59.4 %collective-permute-start.8 = (bf16[200,1024]{1,0:T(8,128)(2,1)}, bf16[200,1024]{1,0:T(8,128)(2,1)}, u32[]{:S(2)}, u32[]{:S(2)}) collective-permute-start(bf16[200,1024]{1,0:T(8,128)(2,1)} %get-tuple-element.96), channel_id=1, source_target_pairs={{0,4},{1,5},{2,6},{3,7},{4,0},{5,1},{6,2},{7,3},{8,12},{9,13},{10,... | collective-permute-start | bytes 1228808 | tf_op jit(solution)/shard_map/ppermute | solution.py:675
  218.2 58.2 %collective-permute-start.9 = (bf16[200,1024]{1,0:T(8,128)(2,1)}, bf16[200,1024]{1,0:T(8,128)(2,1)}, u32[]{:S(2)}, u32[]{:S(2)}) collective-permute-start(bf16[200,1024]{1,0:T(8,128)(2,1)} %get-tuple-element.97), channel_id=1, source_target_pairs={{0,5},{1,4},{2,7},{3,6},{4,1},{5,0},{6,3},{7,2},{8,13},{9,12},{10,... | collective-permute-start | bytes 1228808 | tf_op jit(solution)/shard_map/ppermute | solution.py:675
  219.7 56.7 %collective-permute-start.10 = (bf16[200,1024]{1,0:T(8,128)(2,1)}, bf16[200,1024]{1,0:T(8,128)(2,1)}, u32[]{:S(2)}, u32[]{:S(2)}) collective-permute-start(bf16[200,1024]{1,0:T(8,128)(2,1)} %get-tuple-element.98), channel_id=1, source_target_pairs={{0,6},{1,7},{2,4},{3,5},{4,2},{5,3},{6,0},{7,1},{8,14},{9,15},{10,... | collective-permute-start | bytes 1228808 | tf_op jit(solution)/shard_map/ppermute | solution.py:675
  221.3 55.1 %collective-permute-start.11 = (bf16[200,1024]{1,0:T(8,128)(2,1)}, bf16[200,1024]{1,0:T(8,128)(2,1)}, u32[]{:S(2)}, u32[]{:S(2)}) collective-permute-start(bf16[200,1024]{1,0:T(8,128)(2,1)} %get-tuple-element.99), channel_id=1, source_target_pairs={{0,7},{1,6},{2,5},{3,4},{4,3},{5,2},{6,1},{7,0},{8,15},{9,14},{10,... | collective-permute-start | bytes 1228808 | tf_op jit(solution)/shard_map/ppermute | solution.py:675
  276.4 77.5 %all-to-all-start.3 = ((bf16[4,200,1024]{2,1,0:T(8,128)(2,1)}), bf16[4,200,1024]{2,1,0:T(8,128)(2,1)}, u32[]{:S(2)}, u32[]{:S(2)}) async-start(bf16[4,200,1024]{2,1,0:T(8,128)(2,1)} %bitcast.90), calls=%async_computation.3 | async-start | bytes 3276800 | tf_op jit(solution)/shard_map/all_to_all | solution.py:732
  296.9 56.7 %collective-permute-start.12 = (bf16[200,1024]{1,0:T(8,128)(2,1)}, bf16[200,1024]{1,0:T(8,128)(2,1)S(1)}, u32[]{:S(2)}, u32[]{:S(2)}) collective-permute-start(bf16[200,1024]{1,0:T(8,128)(2,1)} %get-tuple-element.119), channel_id=1, source_target_pairs={{0,4},{1,5},{2,6},{3,7},{4,0},{5,1},{6,2},{7,3},{8,12},{9,13},{10,... | collective-permute-start | bytes 1228808 | tf_op jit(solution)/shard_map/ppermute | solution.py:675
  299.7 54.2 %collective-permute-start.13 = (bf16[200,1024]{1,0:T(8,128)(2,1)}, bf16[200,1024]{1,0:T(8,128)(2,1)S(1)}, u32[]{:S(2)}, u32[]{:S(2)}) collective-permute-start(bf16[200,1024]{1,0:T(8,128)(2,1)} %get-tuple-element.121), channel_id=1, source_target_pairs={{0,5},{1,4},{2,7},{3,6},{4,1},{5,0},{6,3},{7,2},{8,13},{9,12},{10,... | collective-permute-start | bytes 1228808 | tf_op jit(solution)/shard_map/ppermute | solution.py:675
  299.9 53.9 %collective-permute-start.14 = (bf16[200,1024]{1,0:T(8,128)(2,1)}, bf16[200,1024]{1,0:T(8,128)(2,1)S(1)}, u32[]{:S(2)}, u32[]{:S(2)}) collective-permute-start(bf16[200,1024]{1,0:T(8,128)(2,1)} %get-tuple-element.123), channel_id=1, source_target_pairs={{0,6},{1,7},{2,4},{3,5},{4,2},{5,3},{6,0},{7,1},{8,14},{9,15},{10,... | collective-permute-start | bytes 1228808 | tf_op jit(solution)/shard_map/ppermute | solution.py:675
  303.5 50.3 %collective-permute-start.15 = (bf16[200,1024]{1,0:T(8,128)(2,1)}, bf16[200,1024]{1,0:T(8,128)(2,1)}, u32[]{:S(2)}, u32[]{:S(2)}) collective-permute-start(bf16[200,1024]{1,0:T(8,128)(2,1)} %get-tuple-element.125), channel_id=1, source_target_pairs={{0,7},{1,6},{2,5},{3,4},{4,3},{5,2},{6,1},{7,0},{8,15},{9,14},{10,... | collective-permute-start | bytes 1228808 | tf_op jit(solution)/shard_map/ppermute | solution.py:675
  369.4 61.3 %collective-permute-start.18 = (bf16[128,4096]{1,0:T(8,128)(2,1)}, bf16[128,4096]{1,0:T(8,128)(2,1)}, u32[]{:S(2)}, u32[]{:S(2)}) collective-permute-start(bf16[128,4096]{1,0:T(8,128)(2,1)} %get-tuple-element.180), channel_id=1, source_target_pairs={{0,16},{8,24},{16,0},{24,8},{1,17},{9,25},{17,1},{25,9},{2,18},{10... | collective-permute-start | bytes 3145736 | tf_op jit(solution)/shard_map/ppermute | solution.py:675
  369.6 61.0 %collective-permute-start.17 = (bf16[128,4096]{1,0:T(8,128)(2,1)}, bf16[128,4096]{1,0:T(8,128)(2,1)}, u32[]{:S(2)}, u32[]{:S(2)}) collective-permute-start(bf16[128,4096]{1,0:T(8,128)(2,1)} %get-tuple-element.178), channel_id=1, source_target_pairs={{0,8},{8,0},{16,24},{24,16},{1,9},{9,1},{17,25},{25,17},{2,10},{10... | collective-permute-start | bytes 3145736 | tf_op jit(solution)/shard_map/ppermute | solution.py:675
  436.2 50.9 %collective-permute-start.22 = (bf16[32,4096]{1,0:T(8,128)(2,1)}, bf16[32,4096]{1,0:T(8,128)(2,1)}, u32[]{:S(2)}, u32[]{:S(2)}) collective-permute-start(bf16[32,4096]{1,0:T(8,128)(2,1)} %get-tuple-element.192), channel_id=1, source_target_pairs={{0,6},{1,7},{2,4},{3,5},{4,2},{5,3},{6,0},{7,1},{8,14},{9,15},{10,... | collective-permute-start | bytes 786440 | tf_op jit(solution)/shard_map/ppermute | solution.py:675
  439.5 47.6 %collective-permute-start.21 = (bf16[32,4096]{1,0:T(8,128)(2,1)}, bf16[32,4096]{1,0:T(8,128)(2,1)}, u32[]{:S(2)}, u32[]{:S(2)}) collective-permute-start(bf16[32,4096]{1,0:T(8,128)(2,1)} %get-tuple-element.193), channel_id=1, source_target_pairs={{0,4},{1,5},{2,6},{3,7},{4,0},{5,1},{6,2},{7,3},{8,12},{9,13},{10,... | collective-permute-start | bytes 786440 | tf_op jit(solution)/shard_map/ppermute | solution.py:675
  (34 other events, 774.6 us)
Sparse Core Ops, SparseCore 0:
  276.4 193.3 reduce-scatter.1

commit v3 on v2

--- a/solution.py
+++ b/solution.py
@@ -22,7 +22,7 @@
 CUBE = 0.044715
 EXTRA = 8
 SMALL = pl.CostEstimate(flops=1 << 20, bytes_accessed=1 << 16, transcendentals=0)
-MEDIUM = pl.CostEstimate(flops=230 * 10**9, bytes_accessed=1 << 16, transcendentals=0)
+MEDIUM = pl.CostEstimate(flops=250_700_000_000, bytes_accessed=1 << 16, transcendentals=0)
 LARGE = pl.CostEstimate(flops=1 << 38, bytes_accessed=1 << 28, transcendentals=0)
 
 
@@ -442,7 +442,7 @@
         logits = dot(x_ref[...], wr_ref[...], NT)
         label = lax.broadcasted_iota(jnp.int32, (1, TILE), 1)
         mine = label == own_ref[0]
-        theirs = label == other_ref[...].astype(jnp.int32) - 1
+        theirs = label == other_ref[:, 0:1].astype(jnp.int32) - 1
         first = jnp.sum(jnp.where(mine, logits, 0.0), axis=1, keepdims=True)
         second = jnp.sum(jnp.where(theirs, logits, 0.0), axis=1, keepdims=True)
         top = jnp.maximum(first, second)
@@ -482,7 +482,7 @@
             weight,
             weight,
             once((TILE, d)),
-            pl.BlockSpec((n, 1), lambda i: (chunk, 0), pipeline_mode=pl.Buffered(1)),
+            pl.BlockSpec((n, TILE), lambda i: (chunk, 0), pipeline_mode=pl.Buffered(1)),
         ]
         + [once(block.shape) for block in blocks]
         + [pl.BlockSpec(memory_space=pl.ANY) for _ in kept],
@@ -503,12 +503,15 @@
 
 
 def slope_kernel(wd_ref, *refs, capacity):
-    blocks, (out_ref, u_ref) = refs[:-2], refs[-2:]
+    blocks, (out_ref, other_ref, u_ref) = refs[:-3], refs[-3:]
 
     @pl.when(pl.program_id(0) == 0)
     def _():
+        reach = -(-capacity // TILE) * TILE
         for block, at, base in spans(blocks, capacity, EXTRA):
             u_ref[base : base + capacity, :] = block[at : at + capacity, :]
+            named = block[at + capacity : at + capacity + EXTRA, 0:reach].astype(jnp.float32).T
+            other_ref[base : base + capacity, :] = jnp.broadcast_to(named[0:capacity, 0:1], (capacity, TILE))
 
     out_ref[...] = dot(u_ref[...], wd_ref[...], NT).astype(jnp.bfloat16)
 
@@ -520,18 +523,24 @@
         lambda *refs: slope_kernel(*refs, capacity=capacity),
         grid=(f // FT,),
         in_specs=[pl.BlockSpec((FT, d), lambda i: (i, 0))] + [once(block.shape) for block in blocks],
-        out_specs=pl.BlockSpec((n, FT), lambda i: (0, i)),
-        out_shape=jax.ShapeDtypeStruct((n, f), jnp.bfloat16),
+        out_specs=[pl.BlockSpec((n, FT), lambda i: (0, i)), pl.BlockSpec((n, TILE), lambda i: (0, 0))],
+        out_shape=[jax.ShapeDtypeStruct((n, f), jnp.bfloat16), jax.ShapeDtypeStruct((n, TILE), jnp.float32)],
         scratch_shapes=[pltpu.VMEM((n, d), jnp.bfloat16)],
         cost_estimate=LARGE,
         name="slope_rows",
     )(wd, *blocks)
 
 
-def weight_kernel(hidden, gate, up, wd_ref, near_ref, far_ref, *refs, ways, copies, capacity):
+def gate_slots(target_ref, blocks, near_ref, far_ref, capacity, extra):
+    for block, at, base in spans(blocks, capacity, extra):
+        share_ref, start = (near_ref, base) if base < near_ref.shape[0] else (far_ref, base - near_ref.shape[0])
+        value = block[at : at + capacity, :].astype(jnp.float32) * share_ref[start : start + capacity, 0:1]
+        target_ref[base : base + capacity, :] = value.astype(jnp.bfloat16)
+
+
+def weight_kernel(hidden, gate, up, near_ref, far_ref, *refs, ways, copies, capacity):
     rows, raw, refs = refs[:ways], refs[ways : 2 * ways], refs[2 * ways :]
-    out_ref, results, refs = refs[0], refs[1 : 1 + ways], refs[1 + ways :]
-    rows_ref, raw_ref, acc_ref, stage_ref, down_ref, done_ref, sent_ref = refs
+    out_ref, rows_ref, raw_ref, stage_ref, down_ref, done_ref, sent_ref = refs
     step = pl.program_id(0)
     steps = pl.num_programs(0)
     d = stage_ref.shape[2] // 2
@@ -560,13 +569,8 @@
 
     @pl.when(step == 0)
     def _():
-        acc_ref[...] = jnp.zeros_like(acc_ref)
-        for target_ref, blocks, extra in ((rows_ref, rows, 0), (raw_ref, raw, EXTRA)):
-            for block, at, base in spans(blocks, capacity, extra):
-                share_ref, start = (near_ref, base) if base < near_ref.shape[0] else (far_ref, base - near_ref.shape[0])
-                share = share_ref[start : start + capacity, 0:1]
-                value = block[at : at + capacity, :].astype(jnp.float32) * share
-                target_ref[base : base + capacity, :] = value.astype(jnp.bfloat16)
+        gate_slots(rows_ref, rows, near_ref, far_ref, capacity, 0)
+        gate_slots(raw_ref, raw, near_ref, far_ref, capacity, EXTRA)
 
     @pl.when(step >= 2)
     def _():
@@ -576,7 +580,6 @@
     stage_ref[slot, :, 0:d] = dot(gate[...], rows_ref[...], TN).astype(jnp.bfloat16)
     stage_ref[slot, :, d : 2 * d] = dot(up[...], rows_ref[...], TN).astype(jnp.bfloat16)
     down_ref[slot] = dot(hidden[...], raw_ref[...], TN).astype(jnp.bfloat16)
-    acc_ref[...] += dot(hidden[...], wd_ref[...])
     whole(step).start()
     for part in range(FT // 64):
         for copy in range(copies):
@@ -584,44 +587,74 @@
 
     @pl.when(step == steps - 1)
     def _():
+        finish(step - 1)
+        finish(step)
+
+
+def weight_grads(hidden, gate, up, shares, rows, raw, copies, capacity):
+    n, f = hidden.shape
+    d = rows[0].shape[1]
+    ways = len(rows)
+    narrow = pl.BlockSpec((n, FT), lambda i: (0, i))
+    return pl.pallas_call(
+        lambda *refs: weight_kernel(*refs, ways=ways, copies=copies, capacity=capacity),
+        grid=(f // FT,),
+        in_specs=[narrow] * 3 + [once(part.shape) for part in (*shares, *rows, *raw)],
+        out_specs=pl.BlockSpec(memory_space=pl.ANY),
+        out_shape=jax.ShapeDtypeStruct((f, 3 * d), jnp.bfloat16),
+        scratch_shapes=[
+            pltpu.VMEM((n, d), jnp.bfloat16),
+            pltpu.VMEM((n, d), jnp.bfloat16),
+            pltpu.VMEM((2, FT, 2 * d), jnp.bfloat16),
+            pltpu.VMEM((2, FT, d), jnp.bfloat16),
+            pltpu.SemaphoreType.DMA((2,)),
+            pltpu.SemaphoreType.DMA((2, FT // 64, copies)),
+        ],
+        cost_estimate=SMALL,
+        name="weight_grads",
+    )(hidden, gate, up, *shares, *rows, *raw)
+
+
+def result_kernel(hidden_ref, wd_ref, *refs):
+    results, acc_ref = refs[:-1], refs[-1]
+    step = pl.program_id(0)
+    part = dot(hidden_ref[...], wd_ref[...])
+
+    @pl.when(step == 0)
+    def _():
+        acc_ref[...] = part
+
+    @pl.when(step > 0)
+    def _():
+        acc_ref[...] += part
+
+    @pl.when(step == pl.num_programs(0) - 1)
+    def _():
         base = 0
         for result in results:
             result[...] = acc_ref[base : base + result.shape[0], :].astype(jnp.bfloat16)
             base += result.shape[0]
-        finish(step - 1)
-        finish(step)
-
-
-def weight_grads(hidden, gate, up, wd, shares, rows, raw, copies, capacity):
+
+
+def result_rows(hidden, wd, shapes):
     n, f = hidden.shape
     d = wd.shape[1]
-    ways = len(rows)
-    narrow = pl.BlockSpec((n, FT), lambda i: (0, i))
-    grad, *results = pl.pallas_call(
-        lambda *refs: weight_kernel(*refs, ways=ways, copies=copies, capacity=capacity),
-        grid=(f // FT,),
-        in_specs=[narrow] * 3
-        + [pl.BlockSpec((FT, d), lambda i: (i, 0))]
-        + [once(part.shape) for part in (*shares, *rows, *raw)],
-        out_specs=[pl.BlockSpec(memory_space=pl.ANY)] + [pl.BlockSpec(part.shape, lambda i: (0, 0)) for part in rows],
-        out_shape=[jax.ShapeDtypeStruct((f, 3 * d), jnp.bfloat16)]
-        + [jax.ShapeDtypeStruct(part.shape, jnp.bfloat16) for part in rows],
-        scratch_shapes=[
-            pltpu.VMEM((n, d), jnp.bfloat16),
-            pltpu.VMEM((n, d), jnp.bfloat16),
-            pltpu.VMEM((n, d), jnp.float32),
-            pltpu.VMEM((2, FT, 2 * d), jnp.bfloat16),
-            pltpu.VMEM((2, FT, d), jnp.bfloat16),
-            pltpu.SemaphoreType.DMA((2,)),
-            pltpu.SemaphoreType.DMA((2, FT // 64, copies)),
-        ],
+    tile = FT * 2 if f % (FT * 2) == 0 else FT
+    return pl.pallas_call(
+        result_kernel,
+        grid=(f // tile,),
+        in_specs=[pl.BlockSpec((n, tile), lambda i: (0, i)), pl.BlockSpec((tile, d), lambda i: (i, 0))],
+        out_specs=[pl.BlockSpec(shape, lambda i: (0, 0)) for shape in shapes],
+        out_shape=[jax.ShapeDtypeStruct(shape, jnp.bfloat16) for shape in shapes],
+        scratch_shapes=[pltpu.VMEM((n, d), jnp.float32)],
         cost_estimate=SMALL,
-        name="weight_grads",
-    )(hidden, gate, up, wd, *shares, *rows, *raw)
-    return grad, results
-
-
-def shared_kernel(core_ref, first_ref, wide_ref, second_ref, narrow_ref, mine_ref, away_ref, *, steps, unit):
+        name="result_rows",
+    )(hidden, wd)
+
+
+def shared_kernel(
+    core_ref, first_ref, wide_ref, second_ref, narrow_ref, mine_ref, away_ref, left_ref, *, steps, unit
+):
     step = pl.program_id(0)
 
     def store(value):
@@ -633,13 +666,21 @@
             mine_ref[span, :] = jnp.where(own, low, high).astype(jnp.bfloat16)
             away_ref[span, :] = jnp.where(own, high, low).astype(jnp.bfloat16)
 
+    @pl.when(step == 0)
+    def _():
+        left_ref[...] = first_ref[...].T
+
+    @pl.when(step == steps)
+    def _():
+        left_ref[...] = second_ref[...].T
+
     @pl.when(step < steps)
     def _():
-        store(dot(first_ref[...], wide_ref[...], TN))
+        store(dot(left_ref[...], wide_ref[...]))
 
     @pl.when(step >= steps)
     def _():
-        store(dot(second_ref[...], narrow_ref[...], TN))
+        store(dot(left_ref[...], narrow_ref[...]))
 
 
 def shared_grads(core, first, wide, second, narrow, unit):
@@ -661,6 +702,7 @@
         ],
         out_specs=[out, out],
         out_shape=[shape, shape],
+        scratch_shapes=[pltpu.VMEM((rows, tokens), jnp.bfloat16)],
         cost_estimate=SMALL,
         name="shared_grads",
     )(core, first, wide, second, narrow)
@@ -675,26 +717,24 @@
     return lax.ppermute(value, axis, [(k, k ^ step) for k in range(size)])
 
 
-def direct_sum(pieces, axis, stride):
-    total = pieces[0].astype(jnp.float32)
-    for step, piece in enumerate(pieces[1:], 1):
-        total = total + swap(piece, axis, step * stride).astype(jnp.float32)
-    return total
-
-
-def over_all(mine, away, unit, *wait):
+def chip_sums(mine, away, unit):
     copies, chips = lax.axis_size("dp"), lax.axis_size("expert") // 2
-    other = swap(after(away, *wait), "expert", 1)
-    parts = [array.reshape(copies, chips * unit, -1) for array in (mine, other)]
+    parts = [array.reshape(copies, chips * unit, -1) for array in (mine, swap(away, "expert", 1))]
     place = lax.axis_index("dp")
     pieces = []
     for step in range(copies):
         both = [lax.dynamic_index_in_dim(part, place ^ step, 0, keepdims=False) for part in parts]
         pieces.append((both[0].astype(jnp.float32) + both[1].astype(jnp.float32)).astype(jnp.bfloat16))
-    half = direct_sum(pieces, "dp", 1).astype(jnp.bfloat16).reshape(chips, unit, -1)
+    return pieces
+
+
+def device_sums(pieces, unit, *work):
+    arrived = [swap(piece, "dp", step) if step else piece for step, piece in enumerate(pieces)]
+    *arrived, _ = lax.optimization_barrier((*arrived, work))
+    chips = lax.axis_size("expert") // 2
+    total = sum(piece.astype(jnp.float32) for piece in arrived).astype(jnp.bfloat16).reshape(chips, unit, -1)
     place = lax.axis_index("expert") // 2
-    half = [lax.dynamic_index_in_dim(half, place ^ step, 0, keepdims=False) for step in range(chips)]
-    return pieces, half, direct_sum(half, "expert", 2)
+    return [lax.dynamic_index_in_dim(total, place ^ step, 0, keepdims=False) for step in range(chips)]
 
 
 def on_device(
@@ -740,8 +780,6 @@
     target = target_rows.T
     raw = exchange(packed)
     block_input = after(block_input, *packed)
-    other = [block[at + capacity, :capacity] for block, at, _ in spans(raw, capacity, EXTRA)]
-    other = jnp.stack(other).astype(jnp.float32).reshape(slots, 1)
     inputs = block_input.astype(jnp.float32)
     normed, unit_one, scale_one = normalize_forward(inputs, gain_attn)
     attn_in = normed.astype(jnp.bfloat16)
@@ -752,7 +790,8 @@
     resid = inputs + attn
     second, unit_two, scale_two = normalize_forward(resid, gain_moe)
     moe_in = second.astype(jnp.bfloat16)
-    rows = exchange(pack(target_rows, after(moe_in, *raw), experts, capacity))
+    *packed, _ = lax.optimization_barrier((*pack(target_rows, moe_in, experts, capacity), raw))
+    rows = exchange(packed)
     logits = dot(moe_in, w_router)
     chosen = jnp.stack([jnp.sum(jnp.where(pick, logits, 0.0), axis=1) for pick in picks], axis=1)
     highest = jnp.max(chosen, axis=1, keepdims=True)
@@ -760,7 +799,7 @@
     gates = exps / jnp.sum(exps, axis=1, keepdims=True)
     gate_weight, up_weight, down_weight = w_gate[0], w_up[0], w_down[0]
     router_rows = jnp.pad(w_router.T, ((0, TILE - experts), (0, 0)))
-    slope = slope_rows(raw, down_weight, experts, capacity)
+    slope, other = slope_rows(raw, down_weight, experts, capacity)
     weights = (gate_weight, up_weight, router_rows, other)
     kept, near_share, near_router, near_pairs = expert_rows(own, rows[:1], slope, *weights, 0, ())
     back = [near(near_pairs[0])]
@@ -768,18 +807,11 @@
     kept, far_share, far_router, far_pairs = expert_rows(own, rows[1:], slope, *weights, 1, kept)
     back += [swap(block, "expert", half + step) for step, block in enumerate(far_pairs)]
     hidden, gate_pre_grad, up_pre_grad = kept
-    weight_grad, result = weight_grads(
-        after(hidden, back[0]),
-        gate_pre_grad,
-        up_pre_grad,
-        down_weight,
-        (near_share, far_share),
-        rows,
-        raw,
-        copies,
-        capacity,
-    )
+    shares = (near_share, far_share)
+    hidden = after(hidden, back[0])
+    weight_grad = weight_grads(hidden, gate_pre_grad, up_pre_grad, shares, rows, raw, copies, capacity)
     weight_sum = lax.psum_scatter(weight_grad, "dp", scatter_dimension=0, tiled=True)
+    result = result_rows(after(hidden, weight_grad), down_weight, [block.shape for block in rows])
     *back, held = lax.optimization_barrier((*back, result[0]))
     result = [after(block, *back) for block in (held, *result[1:])]
     returned = exchange(result)
@@ -790,25 +822,34 @@
     proj_grad, tiles = attention_backward(item_lengths, bias, stat, proj, mixed, mixed_grad)
     unit = width // (copies * ways)
     mine, away = shared_grads(own % 2, attn_in, proj_grad, mixed, attn_grad, unit)
-    mine, half_sums, sums = over_all(mine, away, unit, *returned)
-    proj_grad = after(proj_grad, *mine)
+    pieces = chip_sums(mine, after(away, *returned), unit)
+    proj_grad = after(proj_grad, *pieces)
     table_grad = table_sums(tiles, buckets)
     router_grad = (near_router + far_router)[:experts].T
     attn_in_grad = dot(proj_grad, w_qkv, NT)
     input_norm_grad, gain_attn_grad = normalize_backward(attn_in_grad, unit_one, scale_one, gain_attn)
     input_grad = resid_grad + input_norm_grad
-    output = combine_output(target, gates, after(resid, *half_sums), returned)
+    output = combine_output(target, gates, after(resid, *pieces), returned)
+    small = (table_grad.reshape(-1), gain_attn_grad, gain_moe_grad, router_grad)
+    sizes = [part.size // (copies * ways) for part in small]
+    together = jnp.concatenate([part.reshape(copies * ways, -1) for part in small], axis=1)
+    halves = device_sums(pieces, unit, input_grad, output, together)
+    together = lax.all_to_all(together, ("dp", "expert"), split_axis=0, concat_axis=0, tiled=True)
+    together = jnp.sum(together, axis=0)
+    at = [sum(sizes[:k]) for k in range(5)]
+    table_sum, attn_sum, moe_sum, router_sum = [together[at[k] : at[k + 1]] for k in range(4)]
     piece = width // copies
     down_sum = jnp.concatenate(
         [weight_sum[:, 2 * width + k * piece : 2 * width + (k + 1) * piece] for k in range(copies)], axis=0
     )
-    small = (table_grad.reshape(-1), gain_attn_grad, gain_moe_grad, router_grad)
-    sizes = [part.size // (copies * ways) for part in small]
-    together = jnp.concatenate([part.reshape(copies * ways, -1) for part in small], axis=1)
-    together = lax.all_to_all(together, ("dp", "expert"), split_axis=0, concat_axis=0, tiled=True)
-    together = jnp.sum(together, axis=0)
-    at = [sum(sizes[:k]) for k in range(5)]
-    table_sum, attn_sum, moe_sum, router_sum = [together[at[k] : at[k + 1]] for k in range(4)]
+    experts_out = (
+        weight_sum[:, :width].astype(jnp.float32).T[None],
+        weight_sum[:, width : 2 * width].astype(jnp.float32).T[None],
+        down_sum.astype(jnp.float32)[None],
+    )
+    arrived = [swap(part, "expert", 2 * step) if step else part for step, part in enumerate(halves)]
+    *arrived, _ = lax.optimization_barrier((*arrived, experts_out))
+    sums = sum(part.astype(jnp.float32) for part in arrived)
     return (
         output,
         input_grad,
@@ -818,9 +859,7 @@
         attn_sum,
         moe_sum,
         router_sum.reshape(-1, experts),
-        weight_sum[:, :width].astype(jnp.float32).T[None],
-        weight_sum[:, width : 2 * width].astype(jnp.float32).T[None],
-        down_sum.astype(jnp.float32)[None],
+        *experts_out,
     )
 
 

time: 517 us -> 506 us (0.979)
  starting transfers between devices: 112 us -> 101 us
  Pallas kernels: 217 us -> 227 us
  local copies, waits for them, and re-layouts: 22.8 us -> 14.2 us
  waiting for transfers between devices: 89.5 us -> 84 us
    ppermute x23, waiting for transfers between devices: 74.7 us -> 25.3 us  [swap(): return lax.ppermute(value, axis, [(k, k ^ step) for k in range(size)])]
    all_to_all x1, waiting for transfers between devices: 2.6 us -> 45 us  [on_device(): lax.all_to_all(together, ('dp', 'expert'), split_axis=0, concat_axis=0, t...]
    pallas_call x0 -> x1, Pallas kernels: none -> 21.3 us  [result_rows(): pl.pallas_call(result_kernel, grid=(f // tile,), in_specs=[pl.BlockSpec((...]
    ppermute x23, starting transfers between devices: 60.5 us -> 40.7 us  [swap(): return lax.ppermute(value, axis, [(k, k ^ step) for k in range(size)])]
    all_to_all x1, starting transfers between devices: 5.03 us -> 23.1 us  [on_device(): lax.all_to_all(together, ('dp', 'expert'), split_axis=0, concat_axis=0, t...]
    pallas_call x1, Pallas kernels: 53 us -> 41.2 us  [weight_grads(): pl.pallas_call(lambda *refs: weight_kernel(*refs, ways=ways, copies=copie...]
    all_to_all x4, starting transfers between devices: 46.5 us -> 37.1 us  [near(): lax.all_to_all(parts, 'expert', split_axis=0, concat_axis=0, axis_index_g...]
    slice x5 -> x0, local copies, waits for them, and re-layouts: 5.71 us -> none  [on_device(): block[at + capacity, :capacity]]
  transfers between devices with their start and end apart: 29 -> 29, of which waited for: 8 -> 6; matrix products, arithmetic and copies ran while one was open for 13% -> 13% of each run, Pallas kernels for 40% -> 44%
where the time goes in v3:
time: 506 us; the launch traced here: 499 us
  Pallas kernels  227 us (45%)
  starting transfers between devices  101 us (20%)
  waiting for transfers between devices  84 us (17%)
  matrix products  31.5 us (6%)
  other arithmetic  26.4 us (5%)
  between operations  14.8 us (3%)
  local copies, waits for them, and re-layouts  14.2 us (3%)
    pallas_call x2, Pallas kernels, expert_rows(): pl.pallas_call(lambda *refs: expert_kernel(*refs, ways=ways, parts=parts)...  67.4 us
    all_to_all x1, waiting for transfers between devices, on_device(): lax.all_to_all(together, ('dp', 'expert'), split_axis=0, concat_axis=0, t...  45 us
    pallas_call x1, Pallas kernels, weight_grads(): pl.pallas_call(lambda *refs: weight_kernel(*refs, ways=ways, copies=copie...  41.2 us
    ppermute x23, starting transfers between devices, swap(): return lax.ppermute(value, axis, [(k, k ^ step) for k in range(size)])  40.7 us
    all_to_all x4, starting transfers between devices, near(): lax.all_to_all(parts, 'expert', split_axis=0, concat_axis=0, axis_index_g...  37.1 us
    dot_general x5, matrix products, dot(): return lax.dot_general(a, b, dims, preferred_element_type=jnp.float32)  25.3 us
    ppermute x23, waiting for transfers between devices, swap(): return lax.ppermute(value, axis, [(k, k ^ step) for k in range(size)])  25.3 us
    all_to_all x1, starting transfers between devices, on_device(): lax.all_to_all(together, ('dp', 'expert'), split_axis=0, concat_axis=0, t...  23.1 us
  transfers between devices with their start and end apart: 29, of which 6 were waited for; matrix products, arithmetic and copies ran while one was open for 13% of the time, Pallas kernels for 44%

profile of v3, /device:TPU:0, one launch (start us, length us, event | category | flops | bytes accessed | tf_op | source)
XLA Modules:
  0.0 498.9 jit_solution(5829616359823446511)
XLA Ops:
  7.2 6.2 %pack_first.1 = (bf16[832,1024]{1,0:T(8,128)(2,1)}, bf16[208,1024]{1,0:T(8,128)(2,1)}, bf16[208,1024]{1,0:T(8,128)(2,1)}, bf16[208,1024]{1,0:T(8,128)(2,1)}, bf1...) custom-call(s32[1]{0:T(128)} %bitcast.refs_0_, s32[2,640]{1,0:T(2,128)} %bitcast.93, bf16[640,1024]{1,0:T(8,128)(2,1)} %upstream_ref.1), custom_call_target="tpu_custom_call" | custom-call | flops 1048576 | bytes 65536 | tf_op jit(solution)/shard_map/pack_first/pallas_call | solution.py:322
  29.8 8.6 %convolution_convert_fusion.q_ref.k_ref.v_ref = bf16[640,3072]{1,0:T(8,128)(2,1)} fusion(bf16[640,1024]{1,0:T(8,128)(2,1)S(1)} %fusion.9.refs_1_, bf16[1024,3072]{1,0:T(8,128)(2,1)} %param.16), kind=kOutput, calls=%fused_computation.3 | convolution fusion | flops 4028497920 | bytes 11534336 | tf_op jit(solution)/shard_map/dot_general | solution.py:30
  38.4 16.0 %attention_forward.1 = (bf16[640,1024]{1,0:T(8,128)(2,1)}, f32[8,2,640]{2,1,0:T(2,128)}) custom-call(s32[1,2]{1,0:T(1,128)} %lengths_ref.3, f32[8,2,512]{2,1,0:T(2,128)} %reshape.313.bias_ref, bf16[640,3072]{1,0:T(8,128)(2,1)} %convolution_convert_fusion.q_ref.k_ref.v_ref, bf16[640,3072]{1,0:T(8,128)(2,1)} %convolution_convert_fusion.q_ref.k_ref.v_ref, ...), custom_call_target="tpu_custom_call" | custom-call | flops 1048576 | bytes 65536 | tf_op jit(solution)/shard_map/attention_forward/pallas_call | solution.py:109
  60.3 4.9 pack_rows.1
  65.2 6.0 %collective-permute-done.2.refs_4_.refs_13_ = bf16[208,1024]{1,0:T(8,128)(2,1)} collective-permute-done((bf16[208,1024]{1,0:T(8,128)(2,1)}, bf16[208,1024]{1,0:T(8,128)(2,1)}, u32[]{:S(2)}, u32[]{:S(2)}) %collective-permute-start.2) | collective-permute-done | bytes 426016 | tf_op jit(solution)/shard_map/ppermute | solution.py:717
  71.2 8.2 %collective-permute-done.3.refs_5_.refs_14_ = bf16[208,1024]{1,0:T(8,128)(2,1)} collective-permute-done((bf16[208,1024]{1,0:T(8,128)(2,1)}, bf16[208,1024]{1,0:T(8,128)(2,1)}, u32[]{:S(2)}, u32[]{:S(2)}) %collective-permute-start.3) | collective-permute-done | bytes 426016 | tf_op jit(solution)/shard_map/ppermute | solution.py:717
  79.4 20.5 %all-to-all-start.1 = ((bf16[4,200,1024]{2,1,0:T(8,128)(2,1)}), bf16[4,200,1024]{2,1,0:T(8,128)(2,1)}, u32[]{:S(2)}, u32[]{:S(2)}) async-start(bf16[4,200,1024]{2,1,0:T(8,128)(2,1)} %bitcast.88), calls=%async_computation.1 | async-start | bytes 3276800 | tf_op jit(solution)/shard_map/all_to_all | solution.py:772
  108.3 16.7 %slope_rows.1 = (bf16[1600,2816]{1,0:T(8,128)(2,1)}, f32[1600,128]{1,0:T(8,128)}) custom-call(bf16[2816,1024]{1,0:T(8,128)(2,1)} %bitcast.77, bf16[832,1024]{1,0:T(8,128)(2,1)} %bitcast.7.refs_1_.refs_10_, bf16[208,1024]{1,0:T(8,128)(2,1)} %collective-permute-done.refs_2_.refs_11_, bf16[208,1024]{1,0:T(8,128)(2,1)} %collective-permute-done.1.refs_3_.refs_12_, ...), custom_call_target="tpu_custom_call" | custom-call | flops 274877906944 | bytes 268435456 | tf_op jit(solution)/shard_map/slope_rows/pallas_call | solution.py:522
  124.9 13.8 %all-to-all-done.1 = bf16[4,200,1024]{2,1,0:T(8,128)(2,1)} async-done(((bf16[4,200,1024]{2,1,0:T(8,128)(2,1)}), bf16[4,200,1024]{2,1,0:T(8,128)(2,1)}, u32[]{:S(2)}, u32[]{:S(2)}) %all-to-all-start.1) | async-done | bytes 1638432 | tf_op jit(solution)/shard_map/all_to_all | solution.py:772
  138.7 33.6 %expert_rows.2 = (bf16[1600,2816]{1,0:T(8,128)(2,1)}, bf16[1600,2816]{1,0:T(8,128)(2,1)}, bf16[1600,2816]{1,0:T(8,128)(2,1)}, f32[800,128]{1,0:T(8,128)}, f32[12...) custom-call(s32[1]{0:T(128)} %bitcast.refs_0_, bf16[1600,2816]{1,0:T(8,128)(2,1)} %get-tuple-element.96.refs_1_, ...), custom_call_target="tpu_custom_call" | custom-call | flops 1048576 | bytes 65536 | tf_op jit(solution)/shard_map/expert_rows/pallas_call | solution.py:476
  177.0 33.7 %expert_rows.3 = (bf16[1600,2816]{1,0:T(8,128)(2,1)}, bf16[1600,2816]{1,0:T(8,128)(2,1)}, bf16[1600,2816]{1,0:T(8,128)(2,1)}, f32[800,128]{1,0:T(8,128)}, f32[12...) custom-call(s32[1]{0:T(128)} %bitcast.refs_0_, ...), custom_call_target="tpu_custom_call", output_to_operand_aliasing={{0}: (10, {}), {1}: (11, {}), {2}: (12, {})} | custom-call | flops 274877906944 | bytes 268435456 | tf_op jit(solution)/shard_map/expert_rows/pallas_call | solution.py:476
  217.0 41.2 %weight_grads.1 = bf16[2816,3072]{1,0:T(8,128)(2,1)} custom-call(bf16[1600,2816]{1,0:T(8,128)(2,1)} %get-tuple-element.126.refs_0_.hidden_ref, bf16[1600,2816]{1,0:T(8,128)(2,1)} %get-tuple-element.122.refs_1_, bf16[1600,2816]{1,0:T(8,128)(2,1)} %get-tuple-element.123.refs_2_, f32[800,128]{1,0:T(8,128)} %get-tuple-element.124.refs_3_, ...), custom_call_target="tpu_custom_call" | custom-call | flops 1048576 | bytes 65536 | tf_op jit(solution)/shard_map/weight_grads/pallas_call | solution.py:599
  258.2 21.3 %result_rows.1 = (bf16[800,1024]{1,0:T(8,128)(2,1)}, bf16[200,1024]{1,0:T(8,128)(2,1)}, bf16[200,1024]{1,0:T(8,128)(2,1)}, bf16[200,1024]{1,0:T(8,128)(2,1)}, bf16[200,1024]{1,0:T(8,128)(2,1)}) custom-call(bf16[1600,2816]{1,0:T(8,128)(2,1)} %get-tuple-element.126.refs_0_.hidden_ref, bf16[2816,1024]{1,0:T(8,128)(2,1)} %bitcast.78), custom_call_target="tpu_custom_call" | custom-call | flops 1048576 | bytes 65536 | tf_op jit(solution)/shard_map/result_rows/pallas_call | solution.py:643
  279.6 7.4 %all-to-all-start.3 = ((bf16[4,200,1024]{2,1,0:T(8,128)(2,1)}), bf16[4,200,1024]{2,1,0:T(8,128)(2,1)}, u32[]{:S(2)}, u32[]{:S(2)}) async-start(bf16[4,200,1024]{2,1,0:T(8,128)(2,1)} %bitcast.86), calls=%async_computation.3 | async-start | bytes 3276800 | tf_op jit(solution)/shard_map/all_to_all | solution.py:772
  297.6 9.7 %combine_back.1 = (f32[640,1024]{1,0:T(8,128)}, bf16[640,1024]{1,0:T(8,128)(2,1)}, f32[1,1024]{1,0:T(1,128)}) custom-call(s32[640,2]{1,0:T(8,128)} %bitcast.89, f32[640,2]{1,0:T(8,128)} %exponential_divide_fusion.gates_ref, f32[640,1024]{1,0:T(8,128)} %copy-done.5, f32[640,1]{1,0:T(8,128)} %rsqrt.16.scale_ref, f32[1,1024]{1,0:T(1,128)} %bitcast.94, ...), custom_call_target="tpu_custom_call" | custom-call | flops 1048576 | bytes 65536 | tf_op jit(solution)/shard_map/combine_back/pallas_call | solution.py:383
  311.3 22.6 %attention_backward.1 = (bf16[640,3072]{1,0:T(8,128)(2,1)}, f32[8,2,136,384]{3,2,1,0:T(8,128)}) custom-call(s32[1,2]{1,0:T(1,128)} %lengths_ref.3, f32[8,2,512]{2,1,0:T(2,128)} %reshape.313.bias_ref, f32[8,2,640]{2,1,0:T(2,128)} %get-tuple-element.95.stat_ref, bf16[640,3072]{1,0:T(8,128)(2,1)} %convolution_convert_fusion.q_ref.k_ref.v_ref, ...), custom_call_target="tpu_custom_call" | custom-call | flops 1048576 | bytes 65536 | tf_op jit(solution)/shard_map/attention_backward/pallas_call | solution.py:222
  333.9 13.6 %shared_grads.1 = (bf16[512,4096]{1,0:T(8,128)(2,1)}, bf16[512,4096]{1,0:T(8,128)(2,1)}) custom-call(s32[1]{0:T(128)S(6)} %select_n.84.refs_0_, bf16[640,1024]{1,0:T(8,128)(2,1)} %copy-done.6, bf16[640,3072]{1,0:T(8,128)(2,1)} %get-tuple-element.150.refs_2_, bf16[640,1024]{1,0:T(8,128)(2,1)} %get-tuple-element.94.mixed_ref.refs_3_, ...), custom_call_target="tpu_custom_call" | custom-call | flops 1048576 | bytes 65536 | tf_op jit(solution)/shard_map/shared_grads/pallas_call | solution.py:693
  350.8 5.9 %fusion.16 = f32[32,8,2]{0,1,2:T(8,128)S(1)} fusion(f32[8,2,136,384]{3,2,1,0:T(8,128)} %get-tuple-element.151, s32[136,384]{1,0:T(8,128)S(1)} %fusion.26), kind=kOutput, calls=%fused_computation.32 | convolution fusion | flops 322535424 | bytes 3553280 | tf_op jit(solution)/shard_map/ghrc,rcb->bgh/dot_general | solution.py:275
  356.8 6.9 %fusion.24 = (bf16[128,4096]{1,0:T(8,128)(2,1)}, bf16[128,4096]{1,0:T(8,128)(2,1)}, bf16[128,4096]{1,0:T(8,128)(2,1)}, bf16[128,4096]{1,0:T(8,128)(2,1)}) fusion(bf16[4,128,4096]{2,1,0:T(8,128)(2,1)} %bitcast.18, s32[]{:T(128)S(6)} %select_n.88, bf16[4,128,4096]{2,1,0:T(8,128)(2,1)} %bitcast.84, s32[]{:T(128)S(6)} %select_n.87, s32[]{:T(128)S(6)} %select_n.86, ...), kind=kLoop, calls=%fused_computation.36 | loop fusion | flops 8388608 | bytes 12582928 | tf_op jit(solution)/shard_map/convert_element_type | solution.py:727
  367.2 9.4 %fusion.14 = (f32[1024]{0:T(1024)S(1)}, f32[640]{0:T(1024)}, f32[640,1024]{1,0:T(8,128)}) fusion(bf16[640,1024]{1,0:T(8,128)(2,1)S(1)} %copy-done.2, f32[640]{0:T(1024)S(1)} %copy-done.12, f32[1024]{0:T(1024)S(1)} %copy-done.19, bf16[640,3072]{1,0:T(8,128)(2,1)S(1)} %copy-done.8, bf16[1024,3072]{1,0:T(8,128)(2,1)} %param.16), kind=kOutput, calls=%fused_computation.20 | convolution fusion | flops 4031117824 | bytes 14169088 | tf_op jit(solution)/shard_map/dot_general | solution.py:30
  377.4 23.1 %all-to-all-start.4 = ((f32[32,1,336]{2,1,0:T(1,128)}), f32[32,1,336]{2,1,0:T(1,128)}, u32[]{:S(2)}, u32[]{:S(2)}) async-start(f32[32,1,336]{2,1,0:T(1,128)} %copy.55), calls=%async_computation.5 | async-start | bytes 98304 | tf_op jit(solution)/shard_map/all_to_all | solution.py:837
  400.5 7.3 %combine_output.1 = bf16[640,1024]{1,0:T(8,128)(2,1)} custom-call(s32[640,2]{1,0:T(8,128)} %bitcast.90, f32[640,2]{1,0:T(8,128)} %exponential_divide_fusion.gates_ref, f32[640,1024]{1,0:T(8,128)} %copy-done.5, bf16[800,1024]{1,0:T(8,128)(2,1)} %bitcast.17.refs_0_, bf16[200,1024]{1,0:T(8,128)(2,1)} %copy-done.24, bf16[200,1024]{1,0:T(8,128)(2,1)} %copy-done.25, ...), custom_call_target="tpu_custom_call" | custom-call | flops 250700005376 | bytes 65536 | tf_op jit(solution)/shard_map/combine_output/pallas_call | solution.py:360
  412.6 45.0 %all-to-all-done.4 = f32[32,1,336]{2,1,0:T(1,128)} async-done(((f32[32,1,336]{2,1,0:T(1,128)}), f32[32,1,336]{2,1,0:T(1,128)}, u32[]{:S(2)}, u32[]{:S(2)}) %all-to-all-start.4) | async-done | bytes 43040 | tf_op jit(solution)/shard_map/all_to_all | solution.py:837
  479.4 9.9 %collective-permute-done.21 = bf16[32,4096]{1,0:T(8,128)(2,1)} collective-permute-done((bf16[32,4096]{1,0:T(8,128)(2,1)S(1)}, bf16[32,4096]{1,0:T(8,128)(2,1)}, u32[]{:S(2)}, u32[]{:S(2)}) %collective-permute-start.21) | collective-permute-done | bytes 262176 | tf_op jit(solution)/shard_map/ppermute | solution.py:717
  (157 shorter events, 92.8 us)
Async XLA Ops:
  13.4 66.0 %all-to-all-start = ((bf16[4,208,1024]{2,1,0:T(8,128)(2,1)}), bf16[4,208,1024]{2,1,0:T(8,128)(2,1)}, u32[]{:S(2)}, u32[]{:S(2)}) async-start(bf16[4,208,1024]{2,1,0:T(8,128)(2,1)} %bitcast.85), calls=%async_computation | async-start | bytes 3407872 | tf_op jit(solution)/shard_map/all_to_all | solution.py:772
  18.3 47.0 %collective-permute-start = (bf16[208,1024]{1,0:T(8,128)(2,1)}, bf16[208,1024]{1,0:T(8,128)(2,1)}, u32[]{:S(2)}, u32[]{:S(2)}) collective-permute-start(bf16[208,1024]{1,0:T(8,128)(2,1)} %get-tuple-element.89), channel_id=1, source_target_pairs={{0,4},{1,5},{2,6},{3,7},{4,0},{5,1},{6,2},{7,3},{8,12},{9,13},{10,... | collective-permute-start | bytes 1277960 | tf_op jit(solution)/shard_map/ppermute | solution.py:717
  22.5 48.7 %collective-permute-start.2 = (bf16[208,1024]{1,0:T(8,128)(2,1)}, bf16[208,1024]{1,0:T(8,128)(2,1)}, u32[]{:S(2)}, u32[]{:S(2)}) collective-permute-start(bf16[208,1024]{1,0:T(8,128)(2,1)} %get-tuple-element.91), channel_id=1, source_target_pairs={{0,6},{1,7},{2,4},{3,5},{4,2},{5,3},{6,0},{7,1},{8,14},{9,15},{10,... | collective-permute-start | bytes 1277960 | tf_op jit(solution)/shard_map/ppermute | solution.py:717
  26.2 53.2 %collective-permute-start.3 = (bf16[208,1024]{1,0:T(8,128)(2,1)}, bf16[208,1024]{1,0:T(8,128)(2,1)}, u32[]{:S(2)}, u32[]{:S(2)}) collective-permute-start(bf16[208,1024]{1,0:T(8,128)(2,1)} %get-tuple-element.92), channel_id=1, source_target_pairs={{0,7},{1,6},{2,5},{3,4},{4,3},{5,2},{6,1},{7,0},{8,15},{9,14},{10,... | collective-permute-start | bytes 1277960 | tf_op jit(solution)/shard_map/ppermute | solution.py:717
  79.4 59.3 %all-to-all-start.1 = ((bf16[4,200,1024]{2,1,0:T(8,128)(2,1)}), bf16[4,200,1024]{2,1,0:T(8,128)(2,1)}, u32[]{:S(2)}, u32[]{:S(2)}) async-start(bf16[4,200,1024]{2,1,0:T(8,128)(2,1)} %bitcast.88), calls=%async_computation.1 | async-start | bytes 3276800 | tf_op jit(solution)/shard_map/all_to_all | solution.py:772
  99.9 77.1 %collective-permute-start.4 = (bf16[200,1024]{1,0:T(8,128)(2,1)}, bf16[200,1024]{1,0:T(8,128)(2,1)}, u32[]{:S(2)}, u32[]{:S(2)}) collective-permute-start(bf16[200,1024]{1,0:T(8,128)(2,1)} %get-tuple-element.105), channel_id=1, source_target_pairs={{0,4},{1,5},{2,6},{3,7},{4,0},{5,1},{6,2},{7,3},{8,12},{9,13},{10,... | collective-permute-start | bytes 1228808 | tf_op jit(solution)/shard_map/ppermute | solution.py:717
  104.2 72.8 %collective-permute-start.5 = (bf16[200,1024]{1,0:T(8,128)(2,1)}, bf16[200,1024]{1,0:T(8,128)(2,1)}, u32[]{:S(2)}, u32[]{:S(2)}) collective-permute-start(bf16[200,1024]{1,0:T(8,128)(2,1)} %get-tuple-element.107), channel_id=1, source_target_pairs={{0,5},{1,4},{2,7},{3,6},{4,1},{5,0},{6,3},{7,2},{8,13},{9,12},{10,... | collective-permute-start | bytes 1228808 | tf_op jit(solution)/shard_map/ppermute | solution.py:717
  104.5 72.5 %collective-permute-start.6 = (bf16[200,1024]{1,0:T(8,128)(2,1)}, bf16[200,1024]{1,0:T(8,128)(2,1)}, u32[]{:S(2)}, u32[]{:S(2)}) collective-permute-start(bf16[200,1024]{1,0:T(8,128)(2,1)} %get-tuple-element.109), channel_id=1, source_target_pairs={{0,6},{1,7},{2,4},{3,5},{4,2},{5,3},{6,0},{7,1},{8,14},{9,15},{10,... | collective-permute-start | bytes 1228808 | tf_op jit(solution)/shard_map/ppermute | solution.py:717
  108.0 69.0 %collective-permute-start.7 = (bf16[200,1024]{1,0:T(8,128)(2,1)}, bf16[200,1024]{1,0:T(8,128)(2,1)}, u32[]{:S(2)}, u32[]{:S(2)}) collective-permute-start(bf16[200,1024]{1,0:T(8,128)(2,1)} %get-tuple-element.111), channel_id=1, source_target_pairs={{0,7},{1,6},{2,5},{3,4},{4,3},{5,2},{6,1},{7,0},{8,15},{9,14},{10,... | collective-permute-start | bytes 1228808 | tf_op jit(solution)/shard_map/ppermute | solution.py:717
  172.3 44.6 %all-to-all-start.2 = ((bf16[4,200,1024]{2,1,0:T(8,128)(2,1)}), bf16[4,200,1024]{2,1,0:T(8,128)(2,1)}, u32[]{:S(2)}, u32[]{:S(2)}) async-start(bf16[4,200,1024]{2,1,0:T(8,128)(2,1)} %bitcast.87), calls=%async_computation.2 | async-start | bytes 3276800 | tf_op jit(solution)/shard_map/all_to_all | solution.py:772
  176.7 293.6 %reduce-scatter.2.cloned.1.call-start = ((), (), s32[]{:S(2)}) async-start(), calls=%async_computation.6 | async-start | bytes 21626880 | tf_op jit(solution)/shard_map/reduce_scatter | solution.py:813
  210.7 68.9 %collective-permute-start.8 = (bf16[200,1024]{1,0:T(8,128)(2,1)}, bf16[200,1024]{1,0:T(8,128)(2,1)}, u32[]{:S(2)}, u32[]{:S(2)}) collective-permute-start(bf16[200,1024]{1,0:T(8,128)(2,1)} %get-tuple-element.116), channel_id=1, source_target_pairs={{0,4},{1,5},{2,6},{3,7},{4,0},{5,1},{6,2},{7,3},{8,12},{9,13},{10,... | collective-permute-start | bytes 1228808 | tf_op jit(solution)/shard_map/ppermute | solution.py:717
  211.9 67.7 %collective-permute-start.9 = (bf16[200,1024]{1,0:T(8,128)(2,1)}, bf16[200,1024]{1,0:T(8,128)(2,1)}, u32[]{:S(2)}, u32[]{:S(2)}) collective-permute-start(bf16[200,1024]{1,0:T(8,128)(2,1)} %get-tuple-element.117), channel_id=1, source_target_pairs={{0,5},{1,4},{2,7},{3,6},{4,1},{5,0},{6,3},{7,2},{8,13},{9,12},{10,... | collective-permute-start | bytes 1228808 | tf_op jit(solution)/shard_map/ppermute | solution.py:717
  213.5 66.1 %collective-permute-start.10 = (bf16[200,1024]{1,0:T(8,128)(2,1)}, bf16[200,1024]{1,0:T(8,128)(2,1)}, u32[]{:S(2)}, u32[]{:S(2)}) collective-permute-start(bf16[200,1024]{1,0:T(8,128)(2,1)} %get-tuple-element.118), channel_id=1, source_target_pairs={{0,6},{1,7},{2,4},{3,5},{4,2},{5,3},{6,0},{7,1},{8,14},{9,15},{10,... | collective-permute-start | bytes 1228808 | tf_op jit(solution)/shard_map/ppermute | solution.py:717
  215.1 64.6 %collective-permute-start.11 = (bf16[200,1024]{1,0:T(8,128)(2,1)}, bf16[200,1024]{1,0:T(8,128)(2,1)}, u32[]{:S(2)}, u32[]{:S(2)}) collective-permute-start(bf16[200,1024]{1,0:T(8,128)(2,1)} %get-tuple-element.119), channel_id=1, source_target_pairs={{0,7},{1,6},{2,5},{3,4},{4,3},{5,2},{6,1},{7,0},{8,15},{9,14},{10,... | collective-permute-start | bytes 1228808 | tf_op jit(solution)/shard_map/ppermute | solution.py:717
  279.6 67.9 %all-to-all-start.3 = ((bf16[4,200,1024]{2,1,0:T(8,128)(2,1)}), bf16[4,200,1024]{2,1,0:T(8,128)(2,1)}, u32[]{:S(2)}, u32[]{:S(2)}) async-start(bf16[4,200,1024]{2,1,0:T(8,128)(2,1)} %bitcast.86), calls=%async_computation.3 | async-start | bytes 3276800 | tf_op jit(solution)/shard_map/all_to_all | solution.py:772
  290.7 56.8 %collective-permute-start.12 = (bf16[200,1024]{1,0:T(8,128)(2,1)}, bf16[200,1024]{1,0:T(8,128)(2,1)S(1)}, u32[]{:S(2)}, u32[]{:S(2)}) collective-permute-start(bf16[200,1024]{1,0:T(8,128)(2,1)} %get-tuple-element.140), channel_id=1, source_target_pairs={{0,4},{1,5},{2,6},{3,7},{4,0},{5,1},{6,2},{7,3},{8,12},{9,13},{10,... | collective-permute-start | bytes 1228808 | tf_op jit(solution)/shard_map/ppermute | solution.py:717
  293.5 54.0 %collective-permute-start.13 = (bf16[200,1024]{1,0:T(8,128)(2,1)}, bf16[200,1024]{1,0:T(8,128)(2,1)S(1)}, u32[]{:S(2)}, u32[]{:S(2)}) collective-permute-start(bf16[200,1024]{1,0:T(8,128)(2,1)} %get-tuple-element.142), channel_id=1, source_target_pairs={{0,5},{1,4},{2,7},{3,6},{4,1},{5,0},{6,3},{7,2},{8,13},{9,12},{10,... | collective-permute-start | bytes 1228808 | tf_op jit(solution)/shard_map/ppermute | solution.py:717
  293.7 53.9 %collective-permute-start.14 = (bf16[200,1024]{1,0:T(8,128)(2,1)}, bf16[200,1024]{1,0:T(8,128)(2,1)}, u32[]{:S(2)}, u32[]{:S(2)}) collective-permute-start(bf16[200,1024]{1,0:T(8,128)(2,1)} %get-tuple-element.144), channel_id=1, source_target_pairs={{0,6},{1,7},{2,4},{3,5},{4,2},{5,3},{6,0},{7,1},{8,14},{9,15},{10,... | collective-permute-start | bytes 1228808 | tf_op jit(solution)/shard_map/ppermute | solution.py:717
  297.3 50.2 %collective-permute-start.15 = (bf16[200,1024]{1,0:T(8,128)(2,1)}, bf16[200,1024]{1,0:T(8,128)(2,1)}, u32[]{:S(2)}, u32[]{:S(2)}) collective-permute-start(bf16[200,1024]{1,0:T(8,128)(2,1)} %get-tuple-element.146), channel_id=1, source_target_pairs={{0,7},{1,6},{2,5},{3,4},{4,3},{5,2},{6,1},{7,0},{8,15},{9,14},{10,... | collective-permute-start | bytes 1228808 | tf_op jit(solution)/shard_map/ppermute | solution.py:717
  363.7 96.7 %collective-permute-start.17 = (bf16[128,4096]{1,0:T(8,128)(2,1)}, bf16[128,4096]{1,0:T(8,128)(2,1)}, u32[]{:S(2)}, u32[]{:S(2)}) collective-permute-start(bf16[128,4096]{1,0:T(8,128)(2,1)} %get-tuple-element.204), channel_id=1, source_target_pairs={{0,8},{8,0},{16,24},{24,16},{1,9},{9,1},{17,25},{25,17},{2,10},{10... | collective-permute-start | bytes 3145736 | tf_op jit(solution)/shard_map/ppermute | solution.py:717
  365.1 95.3 %collective-permute-start.18 = (bf16[128,4096]{1,0:T(8,128)(2,1)}, bf16[128,4096]{1,0:T(8,128)(2,1)}, u32[]{:S(2)}, u32[]{:S(2)}) collective-permute-start(bf16[128,4096]{1,0:T(8,128)(2,1)} %get-tuple-element.203), channel_id=1, source_target_pairs={{0,16},{8,24},{16,0},{24,8},{1,17},{9,25},{17,1},{25,9},{2,18},{10... | collective-permute-start | bytes 3145736 | tf_op jit(solution)/shard_map/ppermute | solution.py:717
  366.5 93.9 %collective-permute-start.19 = (bf16[128,4096]{1,0:T(8,128)(2,1)}, bf16[128,4096]{1,0:T(8,128)(2,1)}, u32[]{:S(2)}, u32[]{:S(2)}) collective-permute-start(bf16[128,4096]{1,0:T(8,128)(2,1)} %get-tuple-element.202), channel_id=1, source_target_pairs={{0,24},{8,16},{16,8},{24,0},{1,25},{9,17},{17,9},{25,1},{2,26},{10... | collective-permute-start | bytes 3145736 | tf_op jit(solution)/shard_map/ppermute | solution.py:717
  377.4 80.2 %all-to-all-start.4 = ((f32[32,1,336]{2,1,0:T(1,128)}), f32[32,1,336]{2,1,0:T(1,128)}, u32[]{:S(2)}, u32[]{:S(2)}) async-start(f32[32,1,336]{2,1,0:T(1,128)} %copy.55), calls=%async_computation.5 | async-start | bytes 98304 | tf_op jit(solution)/shard_map/all_to_all | solution.py:837
  (32 other events, 373.8 us)
Sparse Core Ops, SparseCore 0:
  258.4 202.5 reduce-scatter.1

commit v4 on v3

--- a/solution.py
+++ b/solution.py
@@ -22,7 +22,7 @@
 CUBE = 0.044715
 EXTRA = 8
 SMALL = pl.CostEstimate(flops=1 << 20, bytes_accessed=1 << 16, transcendentals=0)
-MEDIUM = pl.CostEstimate(flops=250_700_000_000, bytes_accessed=1 << 16, transcendentals=0)
+MEDIUM = pl.CostEstimate(flops=238_050_000_000, bytes_accessed=1 << 16, transcendentals=0)
 LARGE = pl.CostEstimate(flops=1 << 38, bytes_accessed=1 << 28, transcendentals=0)
 
 
@@ -423,10 +423,9 @@
         up = dot(x, wu_ref[...])
         slope = slope_ref[span, :].astype(jnp.float32)
         square = gate * gate
-        turn = jnp.tanh(gate * (CURVE + (CURVE * CUBE) * square))
-        rise = 0.5 + 0.5 * turn
+        rise = 0.5 + 0.5 * jnp.tanh(gate * (CURVE + (CURVE * CUBE) * square))
         unit = gate * rise
-        bend = rise + (0.5 * gate) * (1.0 - turn * turn) * (CURVE + (3 * CURVE * CUBE) * square)
+        bend = rise + (unit - unit * rise) * (2 * CURVE + (6 * CURVE * CUBE) * square)
         hidden = (unit * up).astype(jnp.bfloat16)
         hidden_ref[span, :] = hidden
         both = hidden.astype(jnp.float32) * slope
@@ -717,22 +716,39 @@
     return lax.ppermute(value, axis, [(k, k ^ step) for k in range(size)])
 
 
-def chip_sums(mine, away, unit):
+def parted(value, bit):
+    return [lax.dynamic_index_in_dim(value, place, 0, keepdims=False) for place in (bit, 1 - bit)]
+
+
+def added(first, second):
+    return (first.astype(jnp.float32) + second.astype(jnp.float32)).astype(jnp.bfloat16)
+
+
+def dp_halves(mine, away, unit):
     copies, chips = lax.axis_size("dp"), lax.axis_size("expert") // 2
-    parts = [array.reshape(copies, chips * unit, -1) for array in (mine, swap(away, "expert", 1))]
+    parts = [array.reshape(copies // 2, 2, chips * unit, -1) for array in (mine, swap(away, "expert", 1))]
     place = lax.axis_index("dp")
-    pieces = []
-    for step in range(copies):
-        both = [lax.dynamic_index_in_dim(part, place ^ step, 0, keepdims=False) for part in parts]
-        pieces.append((both[0].astype(jnp.float32) + both[1].astype(jnp.float32)).astype(jnp.bfloat16))
-    return pieces
-
-
-def device_sums(pieces, unit, *work):
-    arrived = [swap(piece, "dp", step) if step else piece for step, piece in enumerate(pieces)]
-    *arrived, _ = lax.optimization_barrier((*arrived, work))
+    cut = mine.shape[1] // 2
+    low = [jnp.swapaxes(part[..., :cut], 0, 1) for part in parts]
+    high = [part[..., cut:] for part in parts]
+    halves = []
+    for pair, bit in ((low, place % 2), (high, place // 2)):
+        stay, leave = zip(*(parted(part, bit) for part in pair))
+        halves.append((added(*stay), added(*leave)))
+    return halves
+
+
+def dp_sums(halves, unit, *work):
+    place = lax.axis_index("dp")
+    came = [swap(leave, "dp", step) for (_, leave), step in zip(halves, (1, 2))]
+    *came, _ = lax.optimization_barrier((*came, work))
+    total = []
+    for (stay, _), other, bit, step in zip(halves, came, (place // 2, place % 2), (2, 1)):
+        mine, mine_too = (parted(part, bit) for part in (stay, other))
+        leave = swap(added(mine[1], mine_too[1]), "dp", step)
+        total.append(mine[0].astype(jnp.float32) + mine_too[0].astype(jnp.float32) + leave.astype(jnp.float32))
     chips = lax.axis_size("expert") // 2
-    total = sum(piece.astype(jnp.float32) for piece in arrived).astype(jnp.bfloat16).reshape(chips, unit, -1)
+    total = jnp.concatenate(total, axis=1).astype(jnp.bfloat16).reshape(chips, unit, -1)
     place = lax.axis_index("expert") // 2
     return [lax.dynamic_index_in_dim(total, place ^ step, 0, keepdims=False) for step in range(chips)]
 
@@ -772,16 +788,16 @@
         parts = lax.all_to_all(parts, "expert", split_axis=0, concat_axis=0, axis_index_groups=groups, tiled=True)
         return parts.reshape(block.shape)
 
-    def exchange(blocks):
+    def exchange(blocks, *before):
         far = [swap(block, "expert", half + step) for step, block in enumerate(blocks[1:])]
-        return [near(blocks[0])] + far
+        return [near(after(blocks[0], *before))] + far
 
     packed, target_rows = pack_first(own, routes.T, cotangent, experts, capacity)
     target = target_rows.T
-    raw = exchange(packed)
     block_input = after(block_input, *packed)
     inputs = block_input.astype(jnp.float32)
     normed, unit_one, scale_one = normalize_forward(inputs, gain_attn)
+    raw = exchange(packed, scale_one)
     attn_in = normed.astype(jnp.bfloat16)
     bias = bias_rows(rel_table)
     proj = dot(attn_in, w_qkv).astype(jnp.bfloat16)
@@ -791,12 +807,12 @@
     second, unit_two, scale_two = normalize_forward(resid, gain_moe)
     moe_in = second.astype(jnp.bfloat16)
     *packed, _ = lax.optimization_barrier((*pack(target_rows, moe_in, experts, capacity), raw))
-    rows = exchange(packed)
     logits = dot(moe_in, w_router)
     chosen = jnp.stack([jnp.sum(jnp.where(pick, logits, 0.0), axis=1) for pick in picks], axis=1)
     highest = jnp.max(chosen, axis=1, keepdims=True)
     exps = jnp.exp(chosen - highest)
     gates = exps / jnp.sum(exps, axis=1, keepdims=True)
+    rows = exchange(packed, gates)
     gate_weight, up_weight, down_weight = w_gate[0], w_up[0], w_down[0]
     router_rows = jnp.pad(w_router.T, ((0, TILE - experts), (0, 0)))
     slope, other = slope_rows(raw, down_weight, experts, capacity)
@@ -822,18 +838,18 @@
     proj_grad, tiles = attention_backward(item_lengths, bias, stat, proj, mixed, mixed_grad)
     unit = width // (copies * ways)
     mine, away = shared_grads(own % 2, attn_in, proj_grad, mixed, attn_grad, unit)
-    pieces = chip_sums(mine, after(away, *returned), unit)
-    proj_grad = after(proj_grad, *pieces)
+    dp_parts = dp_halves(mine, after(away, *returned), unit)
+    proj_grad, _ = lax.optimization_barrier((proj_grad, dp_parts))
     table_grad = table_sums(tiles, buckets)
     router_grad = (near_router + far_router)[:experts].T
     attn_in_grad = dot(proj_grad, w_qkv, NT)
     input_norm_grad, gain_attn_grad = normalize_backward(attn_in_grad, unit_one, scale_one, gain_attn)
     input_grad = resid_grad + input_norm_grad
-    output = combine_output(target, gates, after(resid, *pieces), returned)
+    output = combine_output(target, gates, after(resid, dp_parts[0][1]), returned)
     small = (table_grad.reshape(-1), gain_attn_grad, gain_moe_grad, router_grad)
     sizes = [part.size // (copies * ways) for part in small]
     together = jnp.concatenate([part.reshape(copies * ways, -1) for part in small], axis=1)
-    halves = device_sums(pieces, unit, input_grad, output, together)
+    halves = dp_sums(dp_parts, unit, input_grad, output, together)
     together = lax.all_to_all(together, ("dp", "expert"), split_axis=0, concat_axis=0, tiled=True)
     together = jnp.sum(together, axis=0)
     at = [sum(sizes[:k]) for k in range(5)]

time: 506 us -> 491 us (0.970)
  starting transfers between devices: 101 us -> 67.3 us
  waiting for transfers between devices: 84 us -> 99.7 us
  local copies, waits for them, and re-layouts: 14.2 us -> 20.8 us
    ppermute x23 -> x24, waiting for transfers between devices: 25.3 us -> 89.4 us  [swap(): return lax.ppermute(value, axis, [(k, k ^ step) for k in range(size)])]
    all_to_all x1, waiting for transfers between devices: 45 us -> 0.01 us  [on_device(): lax.all_to_all(together, ('dp', 'expert'), split_axis=0, concat_axis=0, t...]
    all_to_all x1, starting transfers between devices: 23.1 us -> 3.43 us  [on_device(): lax.all_to_all(together, ('dp', 'expert'), split_axis=0, concat_axis=0, t...]
    all_to_all x4, starting transfers between devices: 37.1 us -> 25 us  [near(): lax.all_to_all(parts, 'expert', split_axis=0, concat_axis=0, axis_index_g...]
    slice x0 -> x2, local copies, waits for them, and re-layouts: none -> 6.7 us  [dp_halves(): high = [part[..., cut:] for part in parts]]
    ppermute x23 -> x24, starting transfers between devices: 40.7 us -> 38.6 us  [swap(): return lax.ppermute(value, axis, [(k, k ^ step) for k in range(size)])]
  transfers between devices with their start and end apart: 29 -> 30, of which waited for: 6 -> 12; matrix products, arithmetic and copies ran while one was open for 13% -> 15% of each run, Pallas kernels for 44% -> 45%
where the time goes in v4:
time: 491 us; the launch traced here: 486 us
  Pallas kernels  226 us (46%)
  waiting for transfers between devices  99.7 us (20%)
  starting transfers between devices  67.3 us (14%)
  other arithmetic  28.8 us (6%)
  matrix products  28.6 us (6%)
  local copies, waits for them, and re-layouts  20.8 us (4%)
  between operations  14.9 us (3%)
    ppermute x24, waiting for transfers between devices, swap(): return lax.ppermute(value, axis, [(k, k ^ step) for k in range(size)])  89.4 us
    pallas_call x2, Pallas kernels, expert_rows(): pl.pallas_call(lambda *refs: expert_kernel(*refs, ways=ways, parts=parts)...  65.9 us
    pallas_call x1, Pallas kernels, weight_grads(): pl.pallas_call(lambda *refs: weight_kernel(*refs, ways=ways, copies=copie...  41.3 us
    ppermute x24, starting transfers between devices, swap(): return lax.ppermute(value, axis, [(k, k ^ step) for k in range(size)])  38.6 us
    all_to_all x4, starting transfers between devices, near(): lax.all_to_all(parts, 'expert', split_axis=0, concat_axis=0, axis_index_g...  25 us
    pallas_call x1, Pallas kernels, attention_backward(): pl.pallas_call(attention_backward_kernel, grid=(pairs,), in_specs=[pl.Blo...  22.5 us
    dot_general x5, matrix products, dot(): return lax.dot_general(a, b, dims, preferred_element_type=jnp.float32)  22.5 us
    pallas_call x1, Pallas kernels, result_rows(): pl.pallas_call(result_kernel, grid=(f // tile,), in_specs=[pl.BlockSpec((...  21.3 us
  transfers between devices with their start and end apart: 30, of which 12 were waited for; matrix products, arithmetic and copies ran while one was open for 15% of the time, Pallas kernels for 45%

profile of v4, /device:TPU:0, one launch (start us, length us, event | category | flops | bytes accessed | tf_op | source)
XLA Modules:
  0.0 485.6 jit_solution(8648048929653341629)
XLA Ops:
  7.2 6.2 %pack_first.1 = (bf16[832,1024]{1,0:T(8,128)(2,1)}, bf16[208,1024]{1,0:T(8,128)(2,1)}, bf16[208,1024]{1,0:T(8,128)(2,1)}, bf16[208,1024]{1,0:T(8,128)(2,1)}, bf1...) custom-call(s32[1]{0:T(128)} %bitcast.refs_0_, s32[2,640]{1,0:T(2,128)} %bitcast.127, bf16[640,1024]{1,0:T(8,128)(2,1)} %upstream_ref.1), custom_call_target="tpu_custom_call" | custom-call | flops 1048576 | bytes 65536 | tf_op jit(solution)/shard_map/pack_first/pallas_call | solution.py:322
  28.7 8.5 %convolution_convert_fusion.q_ref.k_ref.v_ref = bf16[640,3072]{1,0:T(8,128)(2,1)} fusion(bf16[640,1024]{1,0:T(8,128)(2,1)S(1)} %fusion.9.refs_1_, bf16[1024,3072]{1,0:T(8,128)(2,1)} %param.16), kind=kOutput, calls=%fused_computation.3 | convolution fusion | flops 4028497920 | bytes 11534336 | tf_op jit(solution)/shard_map/dot_general | solution.py:30
  37.2 16.0 %attention_forward.1 = (bf16[640,1024]{1,0:T(8,128)(2,1)}, f32[8,2,640]{2,1,0:T(2,128)}) custom-call(s32[1,2]{1,0:T(1,128)} %lengths_ref.3, f32[8,2,512]{2,1,0:T(2,128)} %reshape.349.bias_ref, bf16[640,3072]{1,0:T(8,128)(2,1)} %convolution_convert_fusion.q_ref.k_ref.v_ref, bf16[640,3072]{1,0:T(8,128)(2,1)} %convolution_convert_fusion.q_ref.k_ref.v_ref, ...), custom_call_target="tpu_custom_call" | custom-call | flops 1048576 | bytes 65536 | tf_op jit(solution)/shard_map/attention_forward/pallas_call | solution.py:109
  72.5 10.3 %all-to-all-done = bf16[4,208,1024]{2,1,0:T(8,128)(2,1)} async-done(((bf16[4,208,1024]{2,1,0:T(8,128)(2,1)}), bf16[4,208,1024]{2,1,0:T(8,128)(2,1)}, u32[]{:S(2)}, u32[]{:S(2)}) %all-to-all-start) | async-done | bytes 1703968 | tf_op jit(solution)/shard_map/all_to_all | solution.py:788
  82.8 11.4 %all-to-all-start.1 = ((bf16[4,200,1024]{2,1,0:T(8,128)(2,1)}), bf16[4,200,1024]{2,1,0:T(8,128)(2,1)}, u32[]{:S(2)}, u32[]{:S(2)}) async-start(bf16[4,200,1024]{2,1,0:T(8,128)(2,1)} %bitcast.122), calls=%async_computation.1 | async-start | bytes 3276800 | tf_op jit(solution)/shard_map/all_to_all | solution.py:788
  94.2 6.2 %collective-permute-start.7 = (bf16[200,1024]{1,0:T(8,128)(2,1)}, bf16[200,1024]{1,0:T(8,128)(2,1)}, u32[]{:S(2)}, u32[]{:S(2)}) collective-permute-start(bf16[200,1024]{1,0:T(8,128)(2,1)} %get-tuple-element.111), channel_id=1, source_target_pairs={{0,7},{1,6},{2,5},{3,4},{4,3},{5,2},{6,1},{7,0},{8,15},{9,14},{10,... | collective-permute-start | bytes 1228808 | tf_op jit(solution)/shard_map/ppermute | solution.py:716
  103.2 16.7 %slope_rows.1 = (bf16[1600,2816]{1,0:T(8,128)(2,1)}, f32[1600,128]{1,0:T(8,128)}) custom-call(bf16[2816,1024]{1,0:T(8,128)(2,1)} %bitcast.110, bf16[832,1024]{1,0:T(8,128)(2,1)} %bitcast.7.refs_1_.refs_10_, bf16[208,1024]{1,0:T(8,128)(2,1)} %collective-permute-done.refs_2_.refs_11_, bf16[208,1024]{1,0:T(8,128)(2,1)} %collective-permute-done.1.refs_3_.refs_12_, ...), custom_call_target="tpu_custom_call" | custom-call | flops 274877906944 | bytes 268435456 | tf_op jit(solution)/shard_map/slope_rows/pallas_call | solution.py:521
  120.0 32.9 %expert_rows.2 = (bf16[1600,2816]{1,0:T(8,128)(2,1)}, bf16[1600,2816]{1,0:T(8,128)(2,1)}, bf16[1600,2816]{1,0:T(8,128)(2,1)}, f32[800,128]{1,0:T(8,128)}, f32[12...) custom-call(s32[1]{0:T(128)} %bitcast.refs_0_, bf16[1600,2816]{1,0:T(8,128)(2,1)} %get-tuple-element.95.refs_1_, ...), custom_call_target="tpu_custom_call" | custom-call | flops 1048576 | bytes 65536 | tf_op jit(solution)/shard_map/expert_rows/pallas_call | solution.py:475
  152.9 9.1 %collective-permute-done.5.refs_7_ = bf16[200,1024]{1,0:T(8,128)(2,1)} collective-permute-done((bf16[200,1024]{1,0:T(8,128)(2,1)}, bf16[200,1024]{1,0:T(8,128)(2,1)}, u32[]{:S(2)}, u32[]{:S(2)}) %collective-permute-start.5) | collective-permute-done | bytes 409632 | tf_op jit(solution)/shard_map/ppermute | solution.py:716
  162.0 9.0 %collective-permute-done.4.refs_6_ = bf16[200,1024]{1,0:T(8,128)(2,1)} collective-permute-done((bf16[200,1024]{1,0:T(8,128)(2,1)}, bf16[200,1024]{1,0:T(8,128)(2,1)}, u32[]{:S(2)}, u32[]{:S(2)}) %collective-permute-start.4) | collective-permute-done | bytes 409632 | tf_op jit(solution)/shard_map/ppermute | solution.py:716
  175.6 33.0 %expert_rows.3 = (bf16[1600,2816]{1,0:T(8,128)(2,1)}, bf16[1600,2816]{1,0:T(8,128)(2,1)}, bf16[1600,2816]{1,0:T(8,128)(2,1)}, f32[800,128]{1,0:T(8,128)}, f32[12...) custom-call(s32[1]{0:T(128)} %bitcast.refs_0_, ...), custom_call_target="tpu_custom_call", output_to_operand_aliasing={{0}: (10, {}), {1}: (11, {}), {2}: (12, {})} | custom-call | flops 274877906944 | bytes 268435456 | tf_op jit(solution)/shard_map/expert_rows/pallas_call | solution.py:475
  214.9 41.3 %weight_grads.1 = bf16[2816,3072]{1,0:T(8,128)(2,1)} custom-call(bf16[1600,2816]{1,0:T(8,128)(2,1)} %get-tuple-element.126.refs_0_.hidden_ref, bf16[1600,2816]{1,0:T(8,128)(2,1)} %get-tuple-element.122.refs_1_, bf16[1600,2816]{1,0:T(8,128)(2,1)} %get-tuple-element.123.refs_2_, f32[800,128]{1,0:T(8,128)} %get-tuple-element.124.refs_3_, ...), custom_call_target="tpu_custom_call" | custom-call | flops 1048576 | bytes 65536 | tf_op jit(solution)/shard_map/weight_grads/pallas_call | solution.py:598
  256.2 21.3 %result_rows.1 = (bf16[800,1024]{1,0:T(8,128)(2,1)}, bf16[200,1024]{1,0:T(8,128)(2,1)}, bf16[200,1024]{1,0:T(8,128)(2,1)}, bf16[200,1024]{1,0:T(8,128)(2,1)}, bf16[200,1024]{1,0:T(8,128)(2,1)}) custom-call(bf16[1600,2816]{1,0:T(8,128)(2,1)} %get-tuple-element.126.refs_0_.hidden_ref, bf16[2816,1024]{1,0:T(8,128)(2,1)} %bitcast.111), custom_call_target="tpu_custom_call" | custom-call | flops 1048576 | bytes 65536 | tf_op jit(solution)/shard_map/result_rows/pallas_call | solution.py:642
  295.2 9.6 %combine_back.1 = (f32[640,1024]{1,0:T(8,128)}, bf16[640,1024]{1,0:T(8,128)(2,1)}, f32[1,1024]{1,0:T(1,128)}) custom-call(s32[640,2]{1,0:T(8,128)} %bitcast.123, f32[640,2]{1,0:T(8,128)} %exponential_divide_fusion.gates_ref, f32[640,1024]{1,0:T(8,128)} %copy-done.5, f32[640,1]{1,0:T(8,128)} %rsqrt.16.scale_ref, f32[1,1024]{1,0:T(1,128)} %bitcast.128, ...), custom_call_target="tpu_custom_call" | custom-call | flops 1048576 | bytes 65536 | tf_op jit(solution)/shard_map/combine_back/pallas_call | solution.py:383
  308.8 22.5 %attention_backward.1 = (bf16[640,3072]{1,0:T(8,128)(2,1)}, f32[8,2,136,384]{3,2,1,0:T(8,128)}) custom-call(s32[1,2]{1,0:T(1,128)} %lengths_ref.3, f32[8,2,512]{2,1,0:T(2,128)} %reshape.349.bias_ref, f32[8,2,640]{2,1,0:T(2,128)} %get-tuple-element.94.stat_ref, bf16[640,3072]{1,0:T(8,128)(2,1)} %convolution_convert_fusion.q_ref.k_ref.v_ref, ...), custom_call_target="tpu_custom_call" | custom-call | flops 1048576 | bytes 65536 | tf_op jit(solution)/shard_map/attention_backward/pallas_call | solution.py:222
  331.3 13.7 %shared_grads.1 = (bf16[512,4096]{1,0:T(8,128)(2,1)}, bf16[512,4096]{1,0:T(8,128)(2,1)}) custom-call(s32[1]{0:T(128)S(6)} %select_n.105.refs_0_, bf16[640,1024]{1,0:T(8,128)(2,1)} %copy-done.10, bf16[640,3072]{1,0:T(8,128)(2,1)} %get-tuple-element.150.refs_2_, bf16[640,1024]{1,0:T(8,128)(2,1)} %get-tuple-element.93.mixed_ref.refs_3_, ...), custom_call_target="tpu_custom_call" | custom-call | flops 1048576 | bytes 65536 | tf_op jit(solution)/shard_map/shared_grads/pallas_call | solution.py:692
  345.1 9.7 %collective-permute-done.13.refs_2_ = bf16[200,1024]{1,0:T(8,128)(2,1)} collective-permute-done((bf16[200,1024]{1,0:T(8,128)(2,1)}, bf16[200,1024]{1,0:T(8,128)(2,1)}, u32[]{:S(2)}, u32[]{:S(2)}) %collective-permute-start.13) | collective-permute-done | bytes 409632 | tf_op jit(solution)/shard_map/ppermute | solution.py:716
  354.8 9.1 %collective-permute-done.12.refs_1_ = bf16[200,1024]{1,0:T(8,128)(2,1)} collective-permute-done((bf16[200,1024]{1,0:T(8,128)(2,1)}, bf16[200,1024]{1,0:T(8,128)(2,1)}, u32[]{:S(2)}, u32[]{:S(2)}) %collective-permute-start.12) | collective-permute-done | bytes 409632 | tf_op jit(solution)/shard_map/ppermute | solution.py:716
  365.4 5.8 %fusion.17 = f32[32,8,2]{0,1,2:T(8,128)S(1)} fusion(f32[8,2,136,384]{3,2,1,0:T(8,128)} %get-tuple-element.151, s32[136,384]{1,0:T(8,128)S(1)} %fusion.43), kind=kOutput, calls=%fused_computation.40 | convolution fusion | flops 322535424 | bytes 3553280 | tf_op jit(solution)/shard_map/ghrc,rcb->bgh/dot_general | solution.py:275
  385.8 6.6 %fusion.14 = (f32[1024]{0:T(1024)S(1)}, f32[640]{0:T(1024)}, f32[640,1024]{1,0:T(8,128)}) fusion(bf16[640,1024]{1,0:T(8,128)(2,1)S(1)} %copy-done.2, f32[640]{0:T(1024)S(1)} %copy-done.19, f32[1024]{0:T(1024)S(1)} %copy-done.26, bf16[640,3072]{1,0:T(8,128)(2,1)S(1)} %copy-done.13, bf16[1024,3072]{1,0:T(8,128)(2,1)S(1)} %bitcast.130), kind=kOutput, calls=%fused_computation.20 | convolution fusion | flops 4031117824 | bytes 14169088 | tf_op jit(solution)/shard_map/dot_general | solution.py:30
  396.7 7.3 %combine_output.1 = bf16[640,1024]{1,0:T(8,128)(2,1)} custom-call(s32[640,2]{1,0:T(8,128)} %bitcast.124, f32[640,2]{1,0:T(8,128)} %exponential_divide_fusion.gates_ref, f32[640,1024]{1,0:T(8,128)} %copy-done.5, bf16[800,1024]{1,0:T(8,128)(2,1)} %bitcast.17.refs_0_, bf16[200,1024]{1,0:T(8,128)(2,1)} %collective-permute-done.12.refs_1_, ...), custom_call_target="tpu_custom_call" | custom-call | flops 238050000896 | bytes 65536 | tf_op jit(solution)/shard_map/combine_output/pallas_call | solution.py:360
  408.9 21.5 %collective-permute-done.18 = bf16[2,128,2048]{2,1,0:T(8,128)(2,1)} collective-permute-done((bf16[2,128,2048]{2,1,0:T(8,128)(2,1)}, bf16[2,128,2048]{2,1,0:T(8,128)(2,1)}, u32[]{:S(2)}, u32[]{:S(2)}) %collective-permute-start.18) | collective-permute-done | bytes 1048608 | tf_op jit(solution)/shard_map/ppermute | solution.py:716
  442.6 6.0 %collective-permute-done.20 = bf16[128,2048]{1,0:T(8,128)(2,1)} collective-permute-done((bf16[128,2048]{1,0:T(8,128)(2,1)}, bf16[128,2048]{1,0:T(8,128)(2,1)}, u32[]{:S(2)}, u32[]{:S(2)}) %collective-permute-start.20) | collective-permute-done | bytes 524320 | tf_op jit(solution)/shard_map/ppermute | solution.py:716
  467.0 9.1 %collective-permute-done.22 = bf16[32,4096]{1,0:T(8,128)(2,1)} collective-permute-done((bf16[32,4096]{1,0:T(8,128)(2,1)S(1)}, bf16[32,4096]{1,0:T(8,128)(2,1)}, u32[]{:S(2)}, u32[]{:S(2)}) %collective-permute-start.22) | collective-permute-done | bytes 262176 | tf_op jit(solution)/shard_map/ppermute | solution.py:716
  (181 shorter events, 127.9 us)
Async XLA Ops:
  13.4 54.0 %collective-permute-start = (bf16[208,1024]{1,0:T(8,128)(2,1)}, bf16[208,1024]{1,0:T(8,128)(2,1)}, u32[]{:S(2)}, u32[]{:S(2)}) collective-permute-start(bf16[208,1024]{1,0:T(8,128)(2,1)} %get-tuple-element.88), channel_id=1, source_target_pairs={{0,4},{1,5},{2,6},{3,7},{4,0},{5,1},{6,2},{7,3},{8,12},{9,13},{10,... | collective-permute-start | bytes 1277960 | tf_op jit(solution)/shard_map/ppermute | solution.py:716
  17.5 55.0 %collective-permute-start.1 = (bf16[208,1024]{1,0:T(8,128)(2,1)}, bf16[208,1024]{1,0:T(8,128)(2,1)}, u32[]{:S(2)}, u32[]{:S(2)}) collective-permute-start(bf16[208,1024]{1,0:T(8,128)(2,1)} %get-tuple-element.89), channel_id=1, source_target_pairs={{0,5},{1,4},{2,7},{3,6},{4,1},{5,0},{6,3},{7,2},{8,13},{9,12},{10,... | collective-permute-start | bytes 1277960 | tf_op jit(solution)/shard_map/ppermute | solution.py:716
  17.5 55.0 %collective-permute-start.2 = (bf16[208,1024]{1,0:T(8,128)(2,1)}, bf16[208,1024]{1,0:T(8,128)(2,1)}, u32[]{:S(2)}, u32[]{:S(2)}) collective-permute-start(bf16[208,1024]{1,0:T(8,128)(2,1)} %get-tuple-element.90), channel_id=1, source_target_pairs={{0,6},{1,7},{2,4},{3,5},{4,2},{5,3},{6,0},{7,1},{8,14},{9,15},{10,... | collective-permute-start | bytes 1277960 | tf_op jit(solution)/shard_map/ppermute | solution.py:716
  20.6 51.9 %collective-permute-start.3 = (bf16[208,1024]{1,0:T(8,128)(2,1)}, bf16[208,1024]{1,0:T(8,128)(2,1)}, u32[]{:S(2)}, u32[]{:S(2)}) collective-permute-start(bf16[208,1024]{1,0:T(8,128)(2,1)} %get-tuple-element.91), channel_id=1, source_target_pairs={{0,7},{1,6},{2,5},{3,4},{4,3},{5,2},{6,1},{7,0},{8,15},{9,14},{10,... | collective-permute-start | bytes 1277960 | tf_op jit(solution)/shard_map/ppermute | solution.py:716
  21.2 61.6 %all-to-all-start = ((bf16[4,208,1024]{2,1,0:T(8,128)(2,1)}), bf16[4,208,1024]{2,1,0:T(8,128)(2,1)}, u32[]{:S(2)}, u32[]{:S(2)}) async-start(bf16[4,208,1024]{2,1,0:T(8,128)(2,1)} %bitcast.119), calls=%async_computation | async-start | bytes 3407872 | tf_op jit(solution)/shard_map/all_to_all | solution.py:788
  82.8 37.2 %all-to-all-start.1 = ((bf16[4,200,1024]{2,1,0:T(8,128)(2,1)}), bf16[4,200,1024]{2,1,0:T(8,128)(2,1)}, u32[]{:S(2)}, u32[]{:S(2)}) async-start(bf16[4,200,1024]{2,1,0:T(8,128)(2,1)} %bitcast.122), calls=%async_computation.1 | async-start | bytes 3276800 | tf_op jit(solution)/shard_map/all_to_all | solution.py:788
  94.2 58.7 %collective-permute-start.7 = (bf16[200,1024]{1,0:T(8,128)(2,1)}, bf16[200,1024]{1,0:T(8,128)(2,1)}, u32[]{:S(2)}, u32[]{:S(2)}) collective-permute-start(bf16[200,1024]{1,0:T(8,128)(2,1)} %get-tuple-element.111), channel_id=1, source_target_pairs={{0,7},{1,6},{2,5},{3,4},{4,3},{5,2},{6,1},{7,0},{8,15},{9,14},{10,... | collective-permute-start | bytes 1228808 | tf_op jit(solution)/shard_map/ppermute | solution.py:716
  100.3 52.6 %collective-permute-start.6 = (bf16[200,1024]{1,0:T(8,128)(2,1)}, bf16[200,1024]{1,0:T(8,128)(2,1)}, u32[]{:S(2)}, u32[]{:S(2)}) collective-permute-start(bf16[200,1024]{1,0:T(8,128)(2,1)} %get-tuple-element.109), channel_id=1, source_target_pairs={{0,6},{1,7},{2,4},{3,5},{4,2},{5,3},{6,0},{7,1},{8,14},{9,15},{10,... | collective-permute-start | bytes 1228808 | tf_op jit(solution)/shard_map/ppermute | solution.py:716
  100.7 61.4 %collective-permute-start.5 = (bf16[200,1024]{1,0:T(8,128)(2,1)}, bf16[200,1024]{1,0:T(8,128)(2,1)}, u32[]{:S(2)}, u32[]{:S(2)}) collective-permute-start(bf16[200,1024]{1,0:T(8,128)(2,1)} %get-tuple-element.107), channel_id=1, source_target_pairs={{0,5},{1,4},{2,7},{3,6},{4,1},{5,0},{6,3},{7,2},{8,13},{9,12},{10,... | collective-permute-start | bytes 1228808 | tf_op jit(solution)/shard_map/ppermute | solution.py:716
  100.7 70.4 %collective-permute-start.4 = (bf16[200,1024]{1,0:T(8,128)(2,1)}, bf16[200,1024]{1,0:T(8,128)(2,1)}, u32[]{:S(2)}, u32[]{:S(2)}) collective-permute-start(bf16[200,1024]{1,0:T(8,128)(2,1)} %get-tuple-element.105), channel_id=1, source_target_pairs={{0,4},{1,5},{2,6},{3,7},{4,0},{5,1},{6,2},{7,3},{8,12},{9,13},{10,... | collective-permute-start | bytes 1228808 | tf_op jit(solution)/shard_map/ppermute | solution.py:716
  171.0 43.9 %all-to-all-start.2 = ((bf16[4,200,1024]{2,1,0:T(8,128)(2,1)}), bf16[4,200,1024]{2,1,0:T(8,128)(2,1)}, u32[]{:S(2)}, u32[]{:S(2)}) async-start(bf16[4,200,1024]{2,1,0:T(8,128)(2,1)} %bitcast.121), calls=%async_computation.2 | async-start | bytes 3276800 | tf_op jit(solution)/shard_map/all_to_all | solution.py:788
  175.4 283.6 %reduce-scatter.2.cloned.1.call-start = ((), (), s32[]{:S(2)}) async-start(), calls=%async_computation.6 | async-start | bytes 21626880 | tf_op jit(solution)/shard_map/reduce_scatter | solution.py:829
  208.6 68.9 %collective-permute-start.10 = (bf16[200,1024]{1,0:T(8,128)(2,1)}, bf16[200,1024]{1,0:T(8,128)(2,1)S(1)}, u32[]{:S(2)}, u32[]{:S(2)}) collective-permute-start(bf16[200,1024]{1,0:T(8,128)(2,1)} %get-tuple-element.118), channel_id=1, source_target_pairs={{0,6},{1,7},{2,4},{3,5},{4,2},{5,3},{6,0},{7,1},{8,14},{9,15},{10,... | collective-permute-start | bytes 1228808 | tf_op jit(solution)/shard_map/ppermute | solution.py:716
  211.2 66.3 %collective-permute-start.11 = (bf16[200,1024]{1,0:T(8,128)(2,1)}, bf16[200,1024]{1,0:T(8,128)(2,1)S(1)}, u32[]{:S(2)}, u32[]{:S(2)}) collective-permute-start(bf16[200,1024]{1,0:T(8,128)(2,1)} %get-tuple-element.119), channel_id=1, source_target_pairs={{0,7},{1,6},{2,5},{3,4},{4,3},{5,2},{6,1},{7,0},{8,15},{9,14},{10,... | collective-permute-start | bytes 1228808 | tf_op jit(solution)/shard_map/ppermute | solution.py:716
  212.3 65.3 %collective-permute-start.8 = (bf16[200,1024]{1,0:T(8,128)(2,1)}, bf16[200,1024]{1,0:T(8,128)(2,1)S(1)}, u32[]{:S(2)}, u32[]{:S(2)}) collective-permute-start(bf16[200,1024]{1,0:T(8,128)(2,1)} %get-tuple-element.116), channel_id=1, source_target_pairs={{0,4},{1,5},{2,6},{3,7},{4,0},{5,1},{6,2},{7,3},{8,12},{9,13},{10,... | collective-permute-start | bytes 1228808 | tf_op jit(solution)/shard_map/ppermute | solution.py:716
  212.3 70.3 %collective-permute-start.9 = (bf16[200,1024]{1,0:T(8,128)(2,1)}, bf16[200,1024]{1,0:T(8,128)(2,1)}, u32[]{:S(2)}, u32[]{:S(2)}) collective-permute-start(bf16[200,1024]{1,0:T(8,128)(2,1)} %get-tuple-element.117), channel_id=1, source_target_pairs={{0,5},{1,4},{2,7},{3,6},{4,1},{5,0},{6,3},{7,2},{8,13},{9,12},{10,... | collective-permute-start | bytes 1228808 | tf_op jit(solution)/shard_map/ppermute | solution.py:716
  282.6 81.4 %all-to-all-start.3 = ((bf16[4,200,1024]{2,1,0:T(8,128)(2,1)}), bf16[4,200,1024]{2,1,0:T(8,128)(2,1)}, u32[]{:S(2)}, u32[]{:S(2)}) async-start(bf16[4,200,1024]{2,1,0:T(8,128)(2,1)} %bitcast.120), calls=%async_computation.3 | async-start | bytes 3276800 | tf_op jit(solution)/shard_map/all_to_all | solution.py:788
  289.0 56.1 %collective-permute-start.15 = (bf16[200,1024]{1,0:T(8,128)(2,1)}, bf16[200,1024]{1,0:T(8,128)(2,1)}, u32[]{:S(2)}, u32[]{:S(2)}) collective-permute-start(bf16[200,1024]{1,0:T(8,128)(2,1)} %get-tuple-element.146), channel_id=1, source_target_pairs={{0,7},{1,6},{2,5},{3,4},{4,3},{5,2},{6,1},{7,0},{8,15},{9,14},{10,... | collective-permute-start | bytes 1228808 | tf_op jit(solution)/shard_map/ppermute | solution.py:716
  290.5 54.6 %collective-permute-start.14 = (bf16[200,1024]{1,0:T(8,128)(2,1)}, bf16[200,1024]{1,0:T(8,128)(2,1)}, u32[]{:S(2)}, u32[]{:S(2)}) collective-permute-start(bf16[200,1024]{1,0:T(8,128)(2,1)} %get-tuple-element.144), channel_id=1, source_target_pairs={{0,6},{1,7},{2,4},{3,5},{4,2},{5,3},{6,0},{7,1},{8,14},{9,15},{10,... | collective-permute-start | bytes 1228808 | tf_op jit(solution)/shard_map/ppermute | solution.py:716
  293.0 61.8 %collective-permute-start.13 = (bf16[200,1024]{1,0:T(8,128)(2,1)}, bf16[200,1024]{1,0:T(8,128)(2,1)}, u32[]{:S(2)}, u32[]{:S(2)}) collective-permute-start(bf16[200,1024]{1,0:T(8,128)(2,1)} %get-tuple-element.142), channel_id=1, source_target_pairs={{0,5},{1,4},{2,7},{3,6},{4,1},{5,0},{6,3},{7,2},{8,13},{9,12},{10,... | collective-permute-start | bytes 1228808 | tf_op jit(solution)/shard_map/ppermute | solution.py:716
  293.0 70.9 %collective-permute-start.12 = (bf16[200,1024]{1,0:T(8,128)(2,1)}, bf16[200,1024]{1,0:T(8,128)(2,1)}, u32[]{:S(2)}, u32[]{:S(2)}) collective-permute-start(bf16[200,1024]{1,0:T(8,128)(2,1)} %get-tuple-element.140), channel_id=1, source_target_pairs={{0,4},{1,5},{2,6},{3,7},{4,0},{5,1},{6,2},{7,3},{8,12},{9,13},{10,... | collective-permute-start | bytes 1228808 | tf_op jit(solution)/shard_map/ppermute | solution.py:716
  381.5 49.0 %collective-permute-start.18 = (bf16[2,128,2048]{2,1,0:T(8,128)(2,1)}, bf16[2,128,2048]{2,1,0:T(8,128)(2,1)}, u32[]{:S(2)}, u32[]{:S(2)}) collective-permute-start(bf16[2,128,2048]{2,1,0:T(8,128)(2,1)} %get-tuple-element.207), channel_id=1, source_target_pairs={{0,16},{8,24},{16,0},{24,8},{1,17},{9,25},{17,1},{25,9},{2,18},{10... | collective-permute-start | bytes 3145736 | tf_op jit(solution)/shard_map/ppermute | solution.py:716
  384.4 48.9 %collective-permute-start.17 = (bf16[2,128,2048]{2,1,0:T(8,128)(2,1)}, bf16[2,128,2048]{2,1,0:T(8,128)(2,1)}, u32[]{:S(2)}, u32[]{:S(2)}) collective-permute-start(bf16[2,128,2048]{2,1,0:T(8,128)(2,1)} %fusion.22), channel_id=1, source_target_pairs={{0,8},{8,0},{16,24},{24,16},{1,9},{9,1},{17,25},{25,17},{2,10},{10... | collective-permute-start | bytes 3145736 | tf_op jit(solution)/shard_map/ppermute | solution.py:716
  393.2 43.9 %all-to-all-start.4 = ((f32[32,1,336]{2,1,0:T(1,128)}), f32[32,1,336]{2,1,0:T(1,128)}, u32[]{:S(2)}, u32[]{:S(2)}) async-start(f32[32,1,336]{2,1,0:T(1,128)} %copy.67), calls=%async_computation.5 | async-start | bytes 98304 | tf_op jit(solution)/shard_map/all_to_all | solution.py:853
  (40 other events, 500.8 us)
Sparse Core Ops, SparseCore 0:
  256.3 181.2 reduce-scatter.1

commit v5 on v4

--- a/solution.py
+++ b/solution.py
@@ -21,8 +21,9 @@
 CURVE = 0.7978845608028654
 CUBE = 0.044715
 EXTRA = 8
+SHORT = pl.CostEstimate(flops=23_000_000_000, bytes_accessed=1 << 16, transcendentals=0)
 SMALL = pl.CostEstimate(flops=1 << 20, bytes_accessed=1 << 16, transcendentals=0)
-MEDIUM = pl.CostEstimate(flops=238_050_000_000, bytes_accessed=1 << 16, transcendentals=0)
+MEDIUM = pl.CostEstimate(flops=233_450_000_000, bytes_accessed=1 << 16, transcendentals=0)
 LARGE = pl.CostEstimate(flops=1 << 38, bytes_accessed=1 << 28, transcendentals=0)
 
 
@@ -495,7 +496,7 @@
             pltpu.VMEM((n, TILE), jnp.float32),
         ],
         input_output_aliases={6 + ways + k: k for k in range(len(kept))},
-        cost_estimate=LARGE if chunk else SMALL,
+        cost_estimate=SHORT if chunk else SMALL,
         name="expert_rows",
     )(own, slope, wg, wu, wr, other, *blocks, *kept)
     return (hidden, gate, up), share, router, pairs
@@ -724,11 +725,11 @@
     return (first.astype(jnp.float32) + second.astype(jnp.float32)).astype(jnp.bfloat16)
 
 
-def dp_halves(mine, away, unit):
+def dp_halves(parts, unit):
     copies, chips = lax.axis_size("dp"), lax.axis_size("expert") // 2
-    parts = [array.reshape(copies // 2, 2, chips * unit, -1) for array in (mine, swap(away, "expert", 1))]
+    parts = [part.reshape(copies // 2, 2, chips * unit, -1) for part in parts]
     place = lax.axis_index("dp")
-    cut = mine.shape[1] // 2
+    cut = parts[0].shape[-1] // 2
     low = [jnp.swapaxes(part[..., :cut], 0, 1) for part in parts]
     high = [part[..., cut:] for part in parts]
     halves = []
@@ -751,6 +752,24 @@
     total = jnp.concatenate(total, axis=1).astype(jnp.bfloat16).reshape(chips, unit, -1)
     place = lax.axis_index("expert") // 2
     return [lax.dynamic_index_in_dim(total, place ^ step, 0, keepdims=False) for step in range(chips)]
+
+
+def total_of(parts):
+    return sum(part.astype(jnp.float32) for part in parts)
+
+
+def chip_parts(parts, unit):
+    copies, chips = lax.axis_size("dp"), lax.axis_size("expert") // 2
+    place = lax.axis_index("expert") // 2
+    parts = [part.reshape(copies, chips, unit, -1) for part in parts]
+    return [
+        added(*(lax.dynamic_index_in_dim(part, place ^ step, 1, keepdims=False) for part in parts))
+        for step in range(chips)
+    ]
+
+
+def sent(parts, axis, stride):
+    return [swap(part, axis, stride * step) if step else part for step, part in enumerate(parts)]
 
 
 def on_device(
@@ -838,8 +857,11 @@
     proj_grad, tiles = attention_backward(item_lengths, bias, stat, proj, mixed, mixed_grad)
     unit = width // (copies * ways)
     mine, away = shared_grads(own % 2, attn_in, proj_grad, mixed, attn_grad, unit)
-    dp_parts = dp_halves(mine, after(away, *returned), unit)
-    proj_grad, _ = lax.optimization_barrier((proj_grad, dp_parts))
+    both = (mine, swap(after(away, *returned), "expert", 1))
+    cut = mine.shape[1] // 2
+    dp_parts = dp_halves([part[:, :cut] for part in both], unit)
+    z_parts = chip_parts([part[:, cut:] for part in both], unit)
+    proj_grad, _ = lax.optimization_barrier((proj_grad, (dp_parts, z_parts)))
     table_grad = table_sums(tiles, buckets)
     router_grad = (near_router + far_router)[:experts].T
     attn_in_grad = dot(proj_grad, w_qkv, NT)
@@ -850,6 +872,10 @@
     sizes = [part.size // (copies * ways) for part in small]
     together = jnp.concatenate([part.reshape(copies * ways, -1) for part in small], axis=1)
     halves = dp_sums(dp_parts, unit, input_grad, output, together)
+    *z_came, _ = lax.optimization_barrier((*sent(z_parts, "expert", 2), halves))
+    z_sum = total_of(z_came).astype(jnp.bfloat16)
+    dp_place = lax.axis_index("dp")
+    z_sum = [lax.dynamic_index_in_dim(z_sum, dp_place ^ step, 0, keepdims=False) for step in range(copies)]
     together = lax.all_to_all(together, ("dp", "expert"), split_axis=0, concat_axis=0, tiled=True)
     together = jnp.sum(together, axis=0)
     at = [sum(sizes[:k]) for k in range(5)]
@@ -863,9 +889,9 @@
         weight_sum[:, width : 2 * width].astype(jnp.float32).T[None],
         down_sum.astype(jnp.float32)[None],
     )
-    arrived = [swap(part, "expert", 2 * step) if step else part for step, part in enumerate(halves)]
-    *arrived, _ = lax.optimization_barrier((*arrived, experts_out))
-    sums = sum(part.astype(jnp.float32) for part in arrived)
+    low, high = sent(halves, "expert", 2), sent(z_sum, "dp", 1)
+    (low, high), _ = lax.optimization_barrier(((low, high), experts_out))
+    sums = jnp.concatenate([total_of(low), total_of(high)], axis=1)
     return (
         output,
         input_grad,

time: 491 us -> 473 us (0.963)
  waiting for transfers between devices: 99.7 us -> 72.5 us
  starting transfers between devices: 67.3 us -> 77 us
    ppermute x24 -> x30, waiting for transfers between devices: 89.4 us -> 46.8 us  [swap(): return lax.ppermute(value, axis, [(k, k ^ step) for k in range(size)])]
    all_to_all x1, waiting for transfers between devices: 0.01 us -> 15.2 us  [on_device(): lax.all_to_all(together, ('dp', 'expert'), split_axis=0, concat_axis=0, t...]
    ppermute x24 -> x30, starting transfers between devices: 38.6 us -> 48.4 us  [swap(): return lax.ppermute(value, axis, [(k, k ^ step) for k in range(size)])]
    slice x2 -> x1, local copies, waits for them, and re-layouts: 6.7 us -> 0.5 us  [dp_halves(): high = [part[..., cut:] for part in parts]]
  transfers between devices with their start and end apart: 30 -> 36, of which waited for: 12 -> 11; matrix products, arithmetic and copies ran while one was open for 15% -> 16% of each run, Pallas kernels for 45% -> 47%
where the time goes in v5:
time: 473 us; the launch traced here: 467 us
  Pallas kernels  226 us (48%)
  starting transfers between devices  77 us (16%)
  waiting for transfers between devices  72.5 us (15%)
  other arithmetic  30.1 us (6%)
  matrix products  28.7 us (6%)
  local copies, waits for them, and re-layouts  18.7 us (4%)
  between operations  14.9 us (3%)
    pallas_call x2, Pallas kernels, expert_rows(): pl.pallas_call(lambda *refs: expert_kernel(*refs, ways=ways, parts=parts)...  65.8 us
    ppermute x30, starting transfers between devices, swap(): return lax.ppermute(value, axis, [(k, k ^ step) for k in range(size)])  48.4 us
    ppermute x30, waiting for transfers between devices, swap(): return lax.ppermute(value, axis, [(k, k ^ step) for k in range(size)])  46.8 us
    pallas_call x1, Pallas kernels, weight_grads(): pl.pallas_call(lambda *refs: weight_kernel(*refs, ways=ways, copies=copie...  41.3 us
    all_to_all x4, starting transfers between devices, near(): lax.all_to_all(parts, 'expert', split_axis=0, concat_axis=0, axis_index_g...  24.8 us
    pallas_call x1, Pallas kernels, attention_backward(): pl.pallas_call(attention_backward_kernel, grid=(pairs,), in_specs=[pl.Blo...  22.6 us
    dot_general x5, matrix products, dot(): return lax.dot_general(a, b, dims, preferred_element_type=jnp.float32)  21.9 us
    pallas_call x1, Pallas kernels, result_rows(): pl.pallas_call(result_kernel, grid=(f // tile,), in_specs=[pl.BlockSpec((...  21.4 us
  transfers between devices with their start and end apart: 36, of which 11 were waited for; matrix products, arithmetic and copies ran while one was open for 16% of the time, Pallas kernels for 47%

profile of v5, /device:TPU:0, one launch (start us, length us, event | category | flops | bytes accessed | tf_op | source)
XLA Modules:
  0.0 467.4 jit_solution(4443010284572549699)
XLA Ops:
  7.2 6.2 %pack_first.1 = (bf16[832,1024]{1,0:T(8,128)(2,1)}, bf16[208,1024]{1,0:T(8,128)(2,1)}, bf16[208,1024]{1,0:T(8,128)(2,1)}, bf16[208,1024]{1,0:T(8,128)(2,1)}, bf1...) custom-call(s32[1]{0:T(128)} %bitcast.refs_0_, s32[2,640]{1,0:T(2,128)} %bitcast.162, bf16[640,1024]{1,0:T(8,128)(2,1)} %upstream_ref.1), custom_call_target="tpu_custom_call" | custom-call | flops 1048576 | bytes 65536 | tf_op jit(solution)/shard_map/pack_first/pallas_call | solution.py:323
  28.9 8.5 %convolution_convert_fusion.q_ref.k_ref.v_ref = bf16[640,3072]{1,0:T(8,128)(2,1)} fusion(bf16[640,1024]{1,0:T(8,128)(2,1)S(1)} %fusion.9.refs_1_, bf16[1024,3072]{1,0:T(8,128)(2,1)} %param.16), kind=kOutput, calls=%fused_computation.3 | convolution fusion | flops 4028497920 | bytes 11534336 | tf_op jit(solution)/shard_map/dot_general | solution.py:31
  37.4 16.0 %attention_forward.1 = (bf16[640,1024]{1,0:T(8,128)(2,1)}, f32[8,2,640]{2,1,0:T(2,128)}) custom-call(s32[1,2]{1,0:T(1,128)} %lengths_ref.3, f32[8,2,512]{2,1,0:T(2,128)} %reshape.371.bias_ref, bf16[640,3072]{1,0:T(8,128)(2,1)} %convolution_convert_fusion.q_ref.k_ref.v_ref, bf16[640,3072]{1,0:T(8,128)(2,1)} %convolution_convert_fusion.q_ref.k_ref.v_ref, ...), custom_call_target="tpu_custom_call" | custom-call | flops 1048576 | bytes 65536 | tf_op jit(solution)/shard_map/attention_forward/pallas_call | solution.py:110
  59.6 4.9 %pack_rows.1 = (bf16[800,1024]{1,0:T(8,128)(2,1)}, bf16[200,1024]{1,0:T(8,128)(2,1)}, bf16[200,1024]{1,0:T(8,128)(2,1)}, bf16[200,1024]{1,0:T(8,128)(2,1)}, bf16[200,1024]{1,0:T(8,128)(2,1)}) custom-call(s32[2,640]{1,0:T(2,128)} %get-tuple-element.94.refs_0_, bf16[640,1024]{1,0:T(8,128)(2,1)} %copy-done.5), custom_call_target="tpu_custom_call" | custom-call | flops 1048576 | bytes 65536 | tf_op jit(solution)/shard_map/pack_rows/pallas_call | solution.py:334
  67.6 5.0 %collective-permute-done.1.refs_3_.refs_12_ = bf16[208,1024]{1,0:T(8,128)(2,1)} collective-permute-done((bf16[208,1024]{1,0:T(8,128)(2,1)}, bf16[208,1024]{1,0:T(8,128)(2,1)}, u32[]{:S(2)}, u32[]{:S(2)}) %collective-permute-start.1) | collective-permute-done | bytes 426016 | tf_op jit(solution)/shard_map/ppermute | solution.py:717
  72.5 10.4 %all-to-all-done = bf16[4,208,1024]{2,1,0:T(8,128)(2,1)} async-done(((bf16[4,208,1024]{2,1,0:T(8,128)(2,1)}), bf16[4,208,1024]{2,1,0:T(8,128)(2,1)}, u32[]{:S(2)}, u32[]{:S(2)}) %all-to-all-start) | async-done | bytes 1703968 | tf_op jit(solution)/shard_map/all_to_all | solution.py:807
  83.0 10.8 %all-to-all-start.1 = ((bf16[4,200,1024]{2,1,0:T(8,128)(2,1)}), bf16[4,200,1024]{2,1,0:T(8,128)(2,1)}, u32[]{:S(2)}, u32[]{:S(2)}) async-start(bf16[4,200,1024]{2,1,0:T(8,128)(2,1)} %bitcast.155), calls=%async_computation.1 | async-start | bytes 3276800 | tf_op jit(solution)/shard_map/all_to_all | solution.py:807
  93.7 6.2 %collective-permute-start.7 = (bf16[200,1024]{1,0:T(8,128)(2,1)}, bf16[200,1024]{1,0:T(8,128)(2,1)}, u32[]{:S(2)}, u32[]{:S(2)}) collective-permute-start(bf16[200,1024]{1,0:T(8,128)(2,1)} %get-tuple-element.119), channel_id=1, source_target_pairs={{0,7},{1,6},{2,5},{3,4},{4,3},{5,2},{6,1},{7,0},{8,15},{9,14},{10,... | collective-permute-start | bytes 1228808 | tf_op jit(solution)/shard_map/ppermute | solution.py:717
  102.8 16.7 %slope_rows.1 = (bf16[1600,2816]{1,0:T(8,128)(2,1)}, f32[1600,128]{1,0:T(8,128)}) custom-call(bf16[2816,1024]{1,0:T(8,128)(2,1)} %bitcast.146, bf16[832,1024]{1,0:T(8,128)(2,1)} %bitcast.7.refs_1_.refs_10_, bf16[208,1024]{1,0:T(8,128)(2,1)} %collective-permute-done.refs_2_.refs_11_, bf16[208,1024]{1,0:T(8,128)(2,1)} %collective-permute-done.1.refs_3_.refs_12_, ...), custom_call_target="tpu_custom_call" | custom-call | flops 274877906944 | bytes 268435456 | tf_op jit(solution)/shard_map/slope_rows/pallas_call | solution.py:522
  119.5 32.9 %expert_rows.2 = (bf16[1600,2816]{1,0:T(8,128)(2,1)}, bf16[1600,2816]{1,0:T(8,128)(2,1)}, bf16[1600,2816]{1,0:T(8,128)(2,1)}, f32[800,128]{1,0:T(8,128)}, f32[12...) custom-call(s32[1]{0:T(128)} %bitcast.refs_0_, bf16[1600,2816]{1,0:T(8,128)(2,1)} %get-tuple-element.103.refs_1_, ...), custom_call_target="tpu_custom_call" | custom-call | flops 1048576 | bytes 65536 | tf_op jit(solution)/shard_map/expert_rows/pallas_call | solution.py:476
  161.7 9.0 %collective-permute-done.4.refs_6_ = bf16[200,1024]{1,0:T(8,128)(2,1)} collective-permute-done((bf16[200,1024]{1,0:T(8,128)(2,1)}, bf16[200,1024]{1,0:T(8,128)(2,1)}, u32[]{:S(2)}, u32[]{:S(2)}) %collective-permute-start.4) | collective-permute-done | bytes 409632 | tf_op jit(solution)/shard_map/ppermute | solution.py:717
  170.7 32.9 %expert_rows.3 = (bf16[1600,2816]{1,0:T(8,128)(2,1)}, bf16[1600,2816]{1,0:T(8,128)(2,1)}, bf16[1600,2816]{1,0:T(8,128)(2,1)}, f32[800,128]{1,0:T(8,128)}, f32[12...) custom-call(s32[1]{0:T(128)} %bitcast.refs_0_, ...), custom_call_target="tpu_custom_call", output_to_operand_aliasing={{0}: (10, {}), {1}: (11, {}), {2}: (12, {})} | custom-call | flops 23000000512 | bytes 65536 | tf_op jit(solution)/shard_map/expert_rows/pallas_call | solution.py:476
  209.9 41.3 %weight_grads.1 = bf16[2816,3072]{1,0:T(8,128)(2,1)} custom-call(bf16[1600,2816]{1,0:T(8,128)(2,1)} %get-tuple-element.134.refs_0_.hidden_ref, bf16[1600,2816]{1,0:T(8,128)(2,1)} %get-tuple-element.130.refs_1_, bf16[1600,2816]{1,0:T(8,128)(2,1)} %get-tuple-element.131.refs_2_, f32[800,128]{1,0:T(8,128)} %get-tuple-element.132.refs_3_, ...), custom_call_target="tpu_custom_call" | custom-call | flops 1048576 | bytes 65536 | tf_op jit(solution)/shard_map/weight_grads/pallas_call | solution.py:599
  251.2 21.4 %result_rows.1 = (bf16[800,1024]{1,0:T(8,128)(2,1)}, bf16[200,1024]{1,0:T(8,128)(2,1)}, bf16[200,1024]{1,0:T(8,128)(2,1)}, bf16[200,1024]{1,0:T(8,128)(2,1)}, bf16[200,1024]{1,0:T(8,128)(2,1)}) custom-call(bf16[1600,2816]{1,0:T(8,128)(2,1)} %get-tuple-element.134.refs_0_.hidden_ref, bf16[2816,1024]{1,0:T(8,128)(2,1)} %bitcast.147), custom_call_target="tpu_custom_call" | custom-call | flops 1048576 | bytes 65536 | tf_op jit(solution)/shard_map/result_rows/pallas_call | solution.py:643
  289.9 9.7 %combine_back.1 = (f32[640,1024]{1,0:T(8,128)}, bf16[640,1024]{1,0:T(8,128)(2,1)}, f32[1,1024]{1,0:T(1,128)}) custom-call(s32[640,2]{1,0:T(8,128)} %bitcast.156, f32[640,2]{1,0:T(8,128)} %exponential_divide_fusion.gates_ref, f32[640,1024]{1,0:T(8,128)} %copy-done.6, f32[640,1]{1,0:T(8,128)} %rsqrt.16.scale_ref, f32[1,1024]{1,0:T(1,128)} %bitcast.163, ...), custom_call_target="tpu_custom_call" | custom-call | flops 1048576 | bytes 65536 | tf_op jit(solution)/shard_map/combine_back/pallas_call | solution.py:384
  303.5 22.6 %attention_backward.1 = (bf16[640,3072]{1,0:T(8,128)(2,1)}, f32[8,2,136,384]{3,2,1,0:T(8,128)}) custom-call(s32[1,2]{1,0:T(1,128)} %lengths_ref.3, f32[8,2,512]{2,1,0:T(2,128)} %reshape.371.bias_ref, f32[8,2,640]{2,1,0:T(2,128)} %get-tuple-element.102.stat_ref, bf16[640,3072]{1,0:T(8,128)(2,1)} %convolution_convert_fusion.q_ref.k_ref.v_ref, ...), custom_call_target="tpu_custom_call" | custom-call | flops 1048576 | bytes 65536 | tf_op jit(solution)/shard_map/attention_backward/pallas_call | solution.py:223
  326.1 13.4 %shared_grads.1 = (bf16[512,4096]{1,0:T(8,128)(2,1)}, bf16[512,4096]{1,0:T(8,128)(2,1)}) custom-call(s32[1]{0:T(128)S(6)} %select_n.127.refs_0_, bf16[640,1024]{1,0:T(8,128)(2,1)} %copy-done.7, bf16[640,3072]{1,0:T(8,128)(2,1)} %get-tuple-element.158.refs_2_, bf16[640,1024]{1,0:T(8,128)(2,1)} %get-tuple-element.101.mixed_ref.refs_3_, ...), custom_call_target="tpu_custom_call" | custom-call | flops 1048576 | bytes 65536 | tf_op jit(solution)/shard_map/shared_grads/pallas_call | solution.py:693
  339.6 9.9 %collective-permute-done.13.refs_2_ = bf16[200,1024]{1,0:T(8,128)(2,1)} collective-permute-done((bf16[200,1024]{1,0:T(8,128)(2,1)}, bf16[200,1024]{1,0:T(8,128)(2,1)}, u32[]{:S(2)}, u32[]{:S(2)}) %collective-permute-start.13) | collective-permute-done | bytes 409632 | tf_op jit(solution)/shard_map/ppermute | solution.py:717
  349.5 9.1 %collective-permute-done.12.refs_1_ = bf16[200,1024]{1,0:T(8,128)(2,1)} collective-permute-done((bf16[200,1024]{1,0:T(8,128)(2,1)}, bf16[200,1024]{1,0:T(8,128)(2,1)}, u32[]{:S(2)}, u32[]{:S(2)}) %collective-permute-start.12) | collective-permute-done | bytes 409632 | tf_op jit(solution)/shard_map/ppermute | solution.py:717
  360.1 6.4 %fusion.16 = f32[32,8,2]{0,1,2:T(8,128)S(1)} fusion(f32[8,2,136,384]{3,2,1,0:T(8,128)} %get-tuple-element.159, s32[136,384]{1,0:T(8,128)S(1)} %fusion.39), kind=kOutput, calls=%fused_computation.27 | convolution fusion | flops 322535424 | bytes 3553280 | tf_op jit(solution)/shard_map/ghrc,rcb->bgh/dot_general | solution.py:276
  387.2 6.0 %fusion.14 = (f32[1024]{0:T(1024)S(1)}, f32[640]{0:T(1024)S(1)}, f32[640,1024]{1,0:T(8,128)}) fusion(bf16[640,1024]{1,0:T(8,128)(2,1)S(1)} %copy-done.3, f32[640]{0:T(1024)S(1)} %copy-done.20, f32[1024]{0:T(1024)S(1)} %copy-done.27, bf16[640,3072]{1,0:T(8,128)(2,1)S(1)} %copy-done.11, bf16[1024,3072]{1,0:T(8,128)(2,1)S(1)} %bitcast.165), kind=kOutput, calls=%fused_computation.20 | convolution fusion | flops 4031117824 | bytes 14169088 | tf_op jit(solution)/shard_map/dot_general | solution.py:31
  399.1 7.6 %combine_output.1 = bf16[640,1024]{1,0:T(8,128)(2,1)} custom-call(s32[640,2]{1,0:T(8,128)} %bitcast.157, f32[640,2]{1,0:T(8,128)} %exponential_divide_fusion.gates_ref, f32[640,1024]{1,0:T(8,128)} %copy-done.6, bf16[800,1024]{1,0:T(8,128)(2,1)} %bitcast.17.refs_0_, bf16[200,1024]{1,0:T(8,128)(2,1)} %collective-permute-done.12.refs_1_, ...), custom_call_target="tpu_custom_call" | custom-call | flops 233449996288 | bytes 65536 | tf_op jit(solution)/shard_map/combine_output/pallas_call | solution.py:361
  406.8 5.0 %fusion.13 = f32[640,1024]{1,0:T(8,128)} fusion(f32[640,1024]{1,0:T(8,128)} %get-tuple-element.157, bf16[640,1024]{1,0:T(8,128)(2,1)S(1)} %copy-done.4, f32[640,1024]{1,0:T(8,128)} %get-tuple-element.247, f32[640]{0:T(1024)S(1)} %copy-done.29, f32[1024]{0:T(1024)S(1)} %copy-done.28, f32[640]{0:T(1024)S(1)} %copy-done.21), kind=kLoop, calls=%fused_computation.19 | loop fusion | flops 4587520 | bytes 9184256 | tf_op jit(solution)/shard_map/add | solution.py:869
  411.8 15.2 %all-to-all-done.4 = f32[32,1,336]{2,1,0:T(1,128)} async-done(((f32[32,1,336]{2,1,0:T(1,128)}), f32[32,1,336]{2,1,0:T(1,128)}, u32[]{:S(2)}, u32[]{:S(2)}) %all-to-all-start.4) | async-done | bytes 43040 | tf_op jit(solution)/shard_map/all_to_all | solution.py:879
  (201 shorter events, 125.3 us)
Async XLA Ops:
  13.4 54.2 %collective-permute-start = (bf16[208,1024]{1,0:T(8,128)(2,1)}, bf16[208,1024]{1,0:T(8,128)(2,1)}, u32[]{:S(2)}, u32[]{:S(2)}) collective-permute-start(bf16[208,1024]{1,0:T(8,128)(2,1)} %get-tuple-element.96), channel_id=1, source_target_pairs={{0,4},{1,5},{2,6},{3,7},{4,0},{5,1},{6,2},{7,3},{8,12},{9,13},{10,... | collective-permute-start | bytes 1277960 | tf_op jit(solution)/shard_map/ppermute | solution.py:717
  17.5 55.0 %collective-permute-start.1 = (bf16[208,1024]{1,0:T(8,128)(2,1)}, bf16[208,1024]{1,0:T(8,128)(2,1)}, u32[]{:S(2)}, u32[]{:S(2)}) collective-permute-start(bf16[208,1024]{1,0:T(8,128)(2,1)} %get-tuple-element.97), channel_id=1, source_target_pairs={{0,5},{1,4},{2,7},{3,6},{4,1},{5,0},{6,3},{7,2},{8,13},{9,12},{10,... | collective-permute-start | bytes 1277960 | tf_op jit(solution)/shard_map/ppermute | solution.py:717
  17.5 55.0 %collective-permute-start.2 = (bf16[208,1024]{1,0:T(8,128)(2,1)}, bf16[208,1024]{1,0:T(8,128)(2,1)}, u32[]{:S(2)}, u32[]{:S(2)}) collective-permute-start(bf16[208,1024]{1,0:T(8,128)(2,1)} %get-tuple-element.98), channel_id=1, source_target_pairs={{0,6},{1,7},{2,4},{3,5},{4,2},{5,3},{6,0},{7,1},{8,14},{9,15},{10,... | collective-permute-start | bytes 1277960 | tf_op jit(solution)/shard_map/ppermute | solution.py:717
  20.6 52.0 %collective-permute-start.3 = (bf16[208,1024]{1,0:T(8,128)(2,1)}, bf16[208,1024]{1,0:T(8,128)(2,1)}, u32[]{:S(2)}, u32[]{:S(2)}) collective-permute-start(bf16[208,1024]{1,0:T(8,128)(2,1)} %get-tuple-element.99), channel_id=1, source_target_pairs={{0,7},{1,6},{2,5},{3,4},{4,3},{5,2},{6,1},{7,0},{8,15},{9,14},{10,... | collective-permute-start | bytes 1277960 | tf_op jit(solution)/shard_map/ppermute | solution.py:717
  21.2 61.8 %all-to-all-start = ((bf16[4,208,1024]{2,1,0:T(8,128)(2,1)}), bf16[4,208,1024]{2,1,0:T(8,128)(2,1)}, u32[]{:S(2)}, u32[]{:S(2)}) async-start(bf16[4,208,1024]{2,1,0:T(8,128)(2,1)} %bitcast.152), calls=%async_computation | async-start | bytes 3407872 | tf_op jit(solution)/shard_map/all_to_all | solution.py:807
  93.7 63.3 %collective-permute-start.7 = (bf16[200,1024]{1,0:T(8,128)(2,1)}, bf16[200,1024]{1,0:T(8,128)(2,1)}, u32[]{:S(2)}, u32[]{:S(2)}) collective-permute-start(bf16[200,1024]{1,0:T(8,128)(2,1)} %get-tuple-element.119), channel_id=1, source_target_pairs={{0,7},{1,6},{2,5},{3,4},{4,3},{5,2},{6,1},{7,0},{8,15},{9,14},{10,... | collective-permute-start | bytes 1228808 | tf_op jit(solution)/shard_map/ppermute | solution.py:717
  99.9 57.2 %collective-permute-start.6 = (bf16[200,1024]{1,0:T(8,128)(2,1)}, bf16[200,1024]{1,0:T(8,128)(2,1)}, u32[]{:S(2)}, u32[]{:S(2)}) collective-permute-start(bf16[200,1024]{1,0:T(8,128)(2,1)} %get-tuple-element.117), channel_id=1, source_target_pairs={{0,6},{1,7},{2,4},{3,5},{4,2},{5,3},{6,0},{7,1},{8,14},{9,15},{10,... | collective-permute-start | bytes 1228808 | tf_op jit(solution)/shard_map/ppermute | solution.py:717
  100.3 61.5 %collective-permute-start.5 = (bf16[200,1024]{1,0:T(8,128)(2,1)}, bf16[200,1024]{1,0:T(8,128)(2,1)}, u32[]{:S(2)}, u32[]{:S(2)}) collective-permute-start(bf16[200,1024]{1,0:T(8,128)(2,1)} %get-tuple-element.115), channel_id=1, source_target_pairs={{0,5},{1,4},{2,7},{3,6},{4,1},{5,0},{6,3},{7,2},{8,13},{9,12},{10,... | collective-permute-start | bytes 1228808 | tf_op jit(solution)/shard_map/ppermute | solution.py:717
  100.3 70.5 %collective-permute-start.4 = (bf16[200,1024]{1,0:T(8,128)(2,1)}, bf16[200,1024]{1,0:T(8,128)(2,1)}, u32[]{:S(2)}, u32[]{:S(2)}) collective-permute-start(bf16[200,1024]{1,0:T(8,128)(2,1)} %get-tuple-element.113), channel_id=1, source_target_pairs={{0,4},{1,5},{2,6},{3,7},{4,0},{5,1},{6,2},{7,3},{8,12},{9,13},{10,... | collective-permute-start | bytes 1228808 | tf_op jit(solution)/shard_map/ppermute | solution.py:717
  152.4 57.5 %all-to-all-start.2 = ((bf16[4,200,1024]{2,1,0:T(8,128)(2,1)}), bf16[4,200,1024]{2,1,0:T(8,128)(2,1)}, u32[]{:S(2)}, u32[]{:S(2)}) async-start(bf16[4,200,1024]{2,1,0:T(8,128)(2,1)} %bitcast.154), calls=%async_computation.2 | async-start | bytes 3276800 | tf_op jit(solution)/shard_map/all_to_all | solution.py:807
  156.8 292.8 %reduce-scatter.2.cloned.1.call-start = ((), (), s32[]{:S(2)}) async-start(), calls=%async_computation.6 | async-start | bytes 21626880 | tf_op jit(solution)/shard_map/reduce_scatter | solution.py:848
  203.6 68.9 %collective-permute-start.10 = (bf16[200,1024]{1,0:T(8,128)(2,1)}, bf16[200,1024]{1,0:T(8,128)(2,1)S(1)}, u32[]{:S(2)}, u32[]{:S(2)}) collective-permute-start(bf16[200,1024]{1,0:T(8,128)(2,1)} %get-tuple-element.126), channel_id=1, source_target_pairs={{0,6},{1,7},{2,4},{3,5},{4,2},{5,3},{6,0},{7,1},{8,14},{9,15},{10,... | collective-permute-start | bytes 1228808 | tf_op jit(solution)/shard_map/ppermute | solution.py:717
  207.4 65.1 %collective-permute-start.11 = (bf16[200,1024]{1,0:T(8,128)(2,1)}, bf16[200,1024]{1,0:T(8,128)(2,1)S(1)}, u32[]{:S(2)}, u32[]{:S(2)}) collective-permute-start(bf16[200,1024]{1,0:T(8,128)(2,1)} %get-tuple-element.127), channel_id=1, source_target_pairs={{0,7},{1,6},{2,5},{3,4},{4,3},{5,2},{6,1},{7,0},{8,15},{9,14},{10,... | collective-permute-start | bytes 1228808 | tf_op jit(solution)/shard_map/ppermute | solution.py:717
  207.4 65.2 %collective-permute-start.8 = (bf16[200,1024]{1,0:T(8,128)(2,1)}, bf16[200,1024]{1,0:T(8,128)(2,1)S(1)}, u32[]{:S(2)}, u32[]{:S(2)}) collective-permute-start(bf16[200,1024]{1,0:T(8,128)(2,1)} %get-tuple-element.124), channel_id=1, source_target_pairs={{0,4},{1,5},{2,6},{3,7},{4,0},{5,1},{6,2},{7,3},{8,12},{9,13},{10,... | collective-permute-start | bytes 1228808 | tf_op jit(solution)/shard_map/ppermute | solution.py:717
  207.4 69.6 %collective-permute-start.9 = (bf16[200,1024]{1,0:T(8,128)(2,1)}, bf16[200,1024]{1,0:T(8,128)(2,1)}, u32[]{:S(2)}, u32[]{:S(2)}) collective-permute-start(bf16[200,1024]{1,0:T(8,128)(2,1)} %get-tuple-element.125), channel_id=1, source_target_pairs={{0,5},{1,4},{2,7},{3,6},{4,1},{5,0},{6,3},{7,2},{8,13},{9,12},{10,... | collective-permute-start | bytes 1228808 | tf_op jit(solution)/shard_map/ppermute | solution.py:717
  277.1 81.5 %all-to-all-start.3 = ((bf16[4,200,1024]{2,1,0:T(8,128)(2,1)}), bf16[4,200,1024]{2,1,0:T(8,128)(2,1)}, u32[]{:S(2)}, u32[]{:S(2)}) async-start(bf16[4,200,1024]{2,1,0:T(8,128)(2,1)} %bitcast.153), calls=%async_computation.3 | async-start | bytes 3276800 | tf_op jit(solution)/shard_map/all_to_all | solution.py:807
  283.7 55.9 %collective-permute-start.15 = (bf16[200,1024]{1,0:T(8,128)(2,1)}, bf16[200,1024]{1,0:T(8,128)(2,1)}, u32[]{:S(2)}, u32[]{:S(2)}) collective-permute-start(bf16[200,1024]{1,0:T(8,128)(2,1)} %get-tuple-element.154), channel_id=1, source_target_pairs={{0,7},{1,6},{2,5},{3,4},{4,3},{5,2},{6,1},{7,0},{8,15},{9,14},{10,... | collective-permute-start | bytes 1228808 | tf_op jit(solution)/shard_map/ppermute | solution.py:717
  286.0 53.6 %collective-permute-start.14 = (bf16[200,1024]{1,0:T(8,128)(2,1)}, bf16[200,1024]{1,0:T(8,128)(2,1)}, u32[]{:S(2)}, u32[]{:S(2)}) collective-permute-start(bf16[200,1024]{1,0:T(8,128)(2,1)} %get-tuple-element.152), channel_id=1, source_target_pairs={{0,6},{1,7},{2,4},{3,5},{4,2},{5,3},{6,0},{7,1},{8,14},{9,15},{10,... | collective-permute-start | bytes 1228808 | tf_op jit(solution)/shard_map/ppermute | solution.py:717
  287.6 61.9 %collective-permute-start.13 = (bf16[200,1024]{1,0:T(8,128)(2,1)}, bf16[200,1024]{1,0:T(8,128)(2,1)}, u32[]{:S(2)}, u32[]{:S(2)}) collective-permute-start(bf16[200,1024]{1,0:T(8,128)(2,1)} %get-tuple-element.150), channel_id=1, source_target_pairs={{0,5},{1,4},{2,7},{3,6},{4,1},{5,0},{6,3},{7,2},{8,13},{9,12},{10,... | collective-permute-start | bytes 1228808 | tf_op jit(solution)/shard_map/ppermute | solution.py:717
  287.6 71.0 %collective-permute-start.12 = (bf16[200,1024]{1,0:T(8,128)(2,1)}, bf16[200,1024]{1,0:T(8,128)(2,1)}, u32[]{:S(2)}, u32[]{:S(2)}) collective-permute-start(bf16[200,1024]{1,0:T(8,128)(2,1)} %get-tuple-element.148), channel_id=1, source_target_pairs={{0,4},{1,5},{2,6},{3,7},{4,0},{5,1},{6,2},{7,3},{8,12},{9,13},{10,... | collective-permute-start | bytes 1228808 | tf_op jit(solution)/shard_map/ppermute | solution.py:717
  375.0 52.9 %collective-permute-start.17 = (bf16[2,128,1024]{2,1,0:T(8,128)(2,1)}, bf16[2,128,1024]{2,1,0:T(8,128)(2,1)}, u32[]{:S(2)}, u32[]{:S(2)}) collective-permute-start(bf16[2,128,1024]{2,1,0:T(8,128)(2,1)} %fusion.22), channel_id=1, source_target_pairs={{0,8},{8,0},{16,24},{24,16},{1,9},{9,1},{17,25},{25,17},{2,10},{10... | collective-permute-start | bytes 1572872 | tf_op jit(solution)/shard_map/ppermute | solution.py:717
  381.1 62.8 %collective-permute-start.26 = (bf16[4,32,2048]{2,1,0:T(8,128)(2,1)}, bf16[4,32,2048]{2,1,0:T(8,128)(2,1)}, u32[]{:S(2)}, u32[]{:S(2)}) collective-permute-start(bf16[4,32,2048]{2,1,0:T(8,128)(2,1)} %fusion.27), channel_id=1, source_target_pairs={{0,6},{1,7},{2,4},{3,5},{4,2},{5,3},{6,0},{7,1},{8,14},{9,15},{10,... | collective-permute-start | bytes 1572872 | tf_op jit(solution)/shard_map/ppermute | solution.py:717
  382.9 62.2 %collective-permute-start.24 = (bf16[4,32,2048]{2,1,0:T(8,128)(2,1)}, bf16[4,32,2048]{2,1,0:T(8,128)(2,1)}, u32[]{:S(2)}, u32[]{:S(2)}) collective-permute-start(bf16[4,32,2048]{2,1,0:T(8,128)(2,1)} %get-tuple-element.223), channel_id=1, source_target_pairs={{0,2},{1,3},{2,0},{3,1},{4,6},{5,7},{6,4},{7,5},{8,10},{9,11},{10,... | collective-permute-start | bytes 1572872 | tf_op jit(solution)/shard_map/ppermute | solution.py:717
  382.9 62.2 %collective-permute-start.25 = (bf16[4,32,2048]{2,1,0:T(8,128)(2,1)}, bf16[4,32,2048]{2,1,0:T(8,128)(2,1)}, u32[]{:S(2)}, u32[]{:S(2)}) collective-permute-start(bf16[4,32,2048]{2,1,0:T(8,128)(2,1)} %get-tuple-element.222), channel_id=1, source_target_pairs={{0,4},{1,5},{2,6},{3,7},{4,0},{5,1},{6,2},{7,3},{8,12},{9,13},{10,... | collective-permute-start | bytes 1572872 | tf_op jit(solution)/shard_map/ppermute | solution.py:717
  (47 other events, 638.4 us)
Sparse Core Ops, SparseCore 0:
  251.3 171.1 reduce-scatter.1

commit v6 on v5

--- a/solution.py
+++ b/solution.py
@@ -23,7 +23,7 @@
 EXTRA = 8
 SHORT = pl.CostEstimate(flops=23_000_000_000, bytes_accessed=1 << 16, transcendentals=0)
 SMALL = pl.CostEstimate(flops=1 << 20, bytes_accessed=1 << 16, transcendentals=0)
-MEDIUM = pl.CostEstimate(flops=233_450_000_000, bytes_accessed=1 << 16, transcendentals=0)
+MEDIUM = pl.CostEstimate(flops=235_750_000_000, bytes_accessed=1 << 16, transcendentals=0)
 LARGE = pl.CostEstimate(flops=1 << 38, bytes_accessed=1 << 28, transcendentals=0)
 
 
@@ -871,15 +871,12 @@
     small = (table_grad.reshape(-1), gain_attn_grad, gain_moe_grad, router_grad)
     sizes = [part.size // (copies * ways) for part in small]
     together = jnp.concatenate([part.reshape(copies * ways, -1) for part in small], axis=1)
-    halves = dp_sums(dp_parts, unit, input_grad, output, together)
-    *z_came, _ = lax.optimization_barrier((*sent(z_parts, "expert", 2), halves))
+    *z_came, _ = lax.optimization_barrier((*sent(z_parts, "expert", 2), (input_grad, output, together)))
+    halves = dp_sums(dp_parts, unit, input_grad, output, together, z_came)
     z_sum = total_of(z_came).astype(jnp.bfloat16)
     dp_place = lax.axis_index("dp")
     z_sum = [lax.dynamic_index_in_dim(z_sum, dp_place ^ step, 0, keepdims=False) for step in range(copies)]
     together = lax.all_to_all(together, ("dp", "expert"), split_axis=0, concat_axis=0, tiled=True)
-    together = jnp.sum(together, axis=0)
-    at = [sum(sizes[:k]) for k in range(5)]
-    table_sum, attn_sum, moe_sum, router_sum = [together[at[k] : at[k + 1]] for k in range(4)]
     piece = width // copies
     down_sum = jnp.concatenate(
         [weight_sum[:, 2 * width + k * piece : 2 * width + (k + 1) * piece] for k in range(copies)], axis=0
@@ -890,7 +887,10 @@
         down_sum.astype(jnp.float32)[None],
     )
     low, high = sent(halves, "expert", 2), sent(z_sum, "dp", 1)
-    (low, high), _ = lax.optimization_barrier(((low, high), experts_out))
+    (low, high), together, _ = lax.optimization_barrier(((low, high), together, experts_out))
+    together = jnp.sum(together, axis=0)
+    at = [sum(sizes[:k]) for k in range(5)]
+    table_sum, attn_sum, moe_sum, router_sum = [together[at[k] : at[k + 1]] for k in range(4)]
     sums = jnp.concatenate([total_of(low), total_of(high)], axis=1)
     return (
         output,

time: 473 us -> 475 us (level)
  transfers between devices with their start and end apart: 36 -> 36, of which waited for: 11 -> 11; matrix products, arithmetic and copies ran while one was open for 16% -> 15% of each run, Pallas kernels for 47% -> 47%
where the time goes in v6:
time: 475 us; the launch traced here: 469 us
  Pallas kernels  226 us (48%)
  starting transfers between devices  76.3 us (16%)
  waiting for transfers between devices  74.5 us (16%)
  other arithmetic  30 us (6%)
  matrix products  28.7 us (6%)
  local copies, waits for them, and re-layouts  19.1 us (4%)
  between operations  14.9 us (3%)
    pallas_call x2, Pallas kernels, expert_rows(): pl.pallas_call(lambda *refs: expert_kernel(*refs, ways=ways, parts=parts)...  65.9 us
    ppermute x30, waiting for transfers between devices, swap(): return lax.ppermute(value, axis, [(k, k ^ step) for k in range(size)])  50.7 us
    ppermute x30, starting transfers between devices, swap(): return lax.ppermute(value, axis, [(k, k ^ step) for k in range(size)])  47.8 us
    pallas_call x1, Pallas kernels, weight_grads(): pl.pallas_call(lambda *refs: weight_kernel(*refs, ways=ways, copies=copie...  41.3 us
    all_to_all x4, starting transfers between devices, near(): lax.all_to_all(parts, 'expert', split_axis=0, concat_axis=0, axis_index_g...  24.8 us
    pallas_call x1, Pallas kernels, attention_backward(): pl.pallas_call(attention_backward_kernel, grid=(pairs,), in_specs=[pl.Blo...  22.6 us
    dot_general x5, matrix products, dot(): return lax.dot_general(a, b, dims, preferred_element_type=jnp.float32)  22 us
    pallas_call x1, Pallas kernels, result_rows(): pl.pallas_call(result_kernel, grid=(f // tile,), in_specs=[pl.BlockSpec((...  21.3 us
  transfers between devices with their start and end apart: 36, of which 11 were waited for; matrix products, arithmetic and copies ran while one was open for 15% of the time, Pallas kernels for 47%

profile of v6, /device:TPU:0, one launch (start us, length us, event | category | flops | bytes accessed | tf_op | source)
XLA Modules:
  0.0 469.2 jit_solution(2274670193925535351)
XLA Ops:
  7.2 6.2 %pack_first.1 = (bf16[832,1024]{1,0:T(8,128)(2,1)}, bf16[208,1024]{1,0:T(8,128)(2,1)}, bf16[208,1024]{1,0:T(8,128)(2,1)}, bf16[208,1024]{1,0:T(8,128)(2,1)}, bf1...) custom-call(s32[1]{0:T(128)} %bitcast.refs_0_, s32[2,640]{1,0:T(2,128)} %bitcast.166, bf16[640,1024]{1,0:T(8,128)(2,1)} %upstream_ref.1), custom_call_target="tpu_custom_call" | custom-call | flops 1048576 | bytes 65536 | tf_op jit(solution)/shard_map/pack_first/pallas_call | solution.py:323
  28.9 8.5 %convolution_convert_fusion.q_ref.k_ref.v_ref = bf16[640,3072]{1,0:T(8,128)(2,1)} fusion(bf16[640,1024]{1,0:T(8,128)(2,1)S(1)} %fusion.9.refs_1_, bf16[1024,3072]{1,0:T(8,128)(2,1)} %param.16), kind=kOutput, calls=%fused_computation.3 | convolution fusion | flops 4028497920 | bytes 11534336 | tf_op jit(solution)/shard_map/dot_general | solution.py:31
  37.4 16.0 %attention_forward.1 = (bf16[640,1024]{1,0:T(8,128)(2,1)}, f32[8,2,640]{2,1,0:T(2,128)}) custom-call(s32[1,2]{1,0:T(1,128)} %lengths_ref.3, f32[8,2,512]{2,1,0:T(2,128)} %reshape.371.bias_ref, bf16[640,3072]{1,0:T(8,128)(2,1)} %convolution_convert_fusion.q_ref.k_ref.v_ref, bf16[640,3072]{1,0:T(8,128)(2,1)} %convolution_convert_fusion.q_ref.k_ref.v_ref, ...), custom_call_target="tpu_custom_call" | custom-call | flops 1048576 | bytes 65536 | tf_op jit(solution)/shard_map/attention_forward/pallas_call | solution.py:110
  67.5 5.0 %collective-permute-done.1.refs_3_.refs_12_ = bf16[208,1024]{1,0:T(8,128)(2,1)} collective-permute-done((bf16[208,1024]{1,0:T(8,128)(2,1)}, bf16[208,1024]{1,0:T(8,128)(2,1)}, u32[]{:S(2)}, u32[]{:S(2)}) %collective-permute-start.1) | collective-permute-done | bytes 426016 | tf_op jit(solution)/shard_map/ppermute | solution.py:717
  72.5 10.4 %all-to-all-done = bf16[4,208,1024]{2,1,0:T(8,128)(2,1)} async-done(((bf16[4,208,1024]{2,1,0:T(8,128)(2,1)}), bf16[4,208,1024]{2,1,0:T(8,128)(2,1)}, u32[]{:S(2)}, u32[]{:S(2)}) %all-to-all-start) | async-done | bytes 1703968 | tf_op jit(solution)/shard_map/all_to_all | solution.py:807
  83.0 10.8 %all-to-all-start.1 = ((bf16[4,200,1024]{2,1,0:T(8,128)(2,1)}), bf16[4,200,1024]{2,1,0:T(8,128)(2,1)}, u32[]{:S(2)}, u32[]{:S(2)}) async-start(bf16[4,200,1024]{2,1,0:T(8,128)(2,1)} %bitcast.158), calls=%async_computation.1 | async-start | bytes 3276800 | tf_op jit(solution)/shard_map/all_to_all | solution.py:807
  93.7 6.2 %collective-permute-start.7 = (bf16[200,1024]{1,0:T(8,128)(2,1)}, bf16[200,1024]{1,0:T(8,128)(2,1)}, u32[]{:S(2)}, u32[]{:S(2)}) collective-permute-start(bf16[200,1024]{1,0:T(8,128)(2,1)} %get-tuple-element.120), channel_id=1, source_target_pairs={{0,7},{1,6},{2,5},{3,4},{4,3},{5,2},{6,1},{7,0},{8,15},{9,14},{10,... | collective-permute-start | bytes 1228808 | tf_op jit(solution)/shard_map/ppermute | solution.py:717
  102.8 16.7 %slope_rows.1 = (bf16[1600,2816]{1,0:T(8,128)(2,1)}, f32[1600,128]{1,0:T(8,128)}) custom-call(bf16[2816,1024]{1,0:T(8,128)(2,1)} %bitcast.149, bf16[832,1024]{1,0:T(8,128)(2,1)} %bitcast.7.refs_1_.refs_10_, bf16[208,1024]{1,0:T(8,128)(2,1)} %collective-permute-done.refs_2_.refs_11_, bf16[208,1024]{1,0:T(8,128)(2,1)} %collective-permute-done.1.refs_3_.refs_12_, ...), custom_call_target="tpu_custom_call" | custom-call | flops 274877906944 | bytes 268435456 | tf_op jit(solution)/shard_map/slope_rows/pallas_call | solution.py:522
  119.5 32.9 %expert_rows.2 = (bf16[1600,2816]{1,0:T(8,128)(2,1)}, bf16[1600,2816]{1,0:T(8,128)(2,1)}, bf16[1600,2816]{1,0:T(8,128)(2,1)}, f32[800,128]{1,0:T(8,128)}, f32[12...) custom-call(s32[1]{0:T(128)} %bitcast.refs_0_, bf16[1600,2816]{1,0:T(8,128)(2,1)} %get-tuple-element.104.refs_1_, ...), custom_call_target="tpu_custom_call" | custom-call | flops 1048576 | bytes 65536 | tf_op jit(solution)/shard_map/expert_rows/pallas_call | solution.py:476
  161.7 9.0 %collective-permute-done.4.refs_6_ = bf16[200,1024]{1,0:T(8,128)(2,1)} collective-permute-done((bf16[200,1024]{1,0:T(8,128)(2,1)}, bf16[200,1024]{1,0:T(8,128)(2,1)}, u32[]{:S(2)}, u32[]{:S(2)}) %collective-permute-start.4) | collective-permute-done | bytes 409632 | tf_op jit(solution)/shard_map/ppermute | solution.py:717
  170.7 33.0 %expert_rows.3 = (bf16[1600,2816]{1,0:T(8,128)(2,1)}, bf16[1600,2816]{1,0:T(8,128)(2,1)}, bf16[1600,2816]{1,0:T(8,128)(2,1)}, f32[800,128]{1,0:T(8,128)}, f32[12...) custom-call(s32[1]{0:T(128)} %bitcast.refs_0_, ...), custom_call_target="tpu_custom_call", output_to_operand_aliasing={{0}: (10, {}), {1}: (11, {}), {2}: (12, {})} | custom-call | flops 23000000512 | bytes 65536 | tf_op jit(solution)/shard_map/expert_rows/pallas_call | solution.py:476
  209.9 41.3 %weight_grads.1 = bf16[2816,3072]{1,0:T(8,128)(2,1)} custom-call(bf16[1600,2816]{1,0:T(8,128)(2,1)} %get-tuple-element.135.refs_0_.hidden_ref, bf16[1600,2816]{1,0:T(8,128)(2,1)} %get-tuple-element.131.refs_1_, bf16[1600,2816]{1,0:T(8,128)(2,1)} %get-tuple-element.132.refs_2_, f32[800,128]{1,0:T(8,128)} %get-tuple-element.133.refs_3_, ...), custom_call_target="tpu_custom_call" | custom-call | flops 1048576 | bytes 65536 | tf_op jit(solution)/shard_map/weight_grads/pallas_call | solution.py:599
  251.2 21.3 %result_rows.1 = (bf16[800,1024]{1,0:T(8,128)(2,1)}, bf16[200,1024]{1,0:T(8,128)(2,1)}, bf16[200,1024]{1,0:T(8,128)(2,1)}, bf16[200,1024]{1,0:T(8,128)(2,1)}, bf16[200,1024]{1,0:T(8,128)(2,1)}) custom-call(bf16[1600,2816]{1,0:T(8,128)(2,1)} %get-tuple-element.135.refs_0_.hidden_ref, bf16[2816,1024]{1,0:T(8,128)(2,1)} %bitcast.150), custom_call_target="tpu_custom_call" | custom-call | flops 1048576 | bytes 65536 | tf_op jit(solution)/shard_map/result_rows/pallas_call | solution.py:643
  289.9 9.7 %combine_back.1 = (f32[640,1024]{1,0:T(8,128)}, bf16[640,1024]{1,0:T(8,128)(2,1)}, f32[1,1024]{1,0:T(1,128)}) custom-call(s32[640,2]{1,0:T(8,128)} %bitcast.159, f32[640,2]{1,0:T(8,128)} %exponential_divide_fusion.gates_ref, f32[640,1024]{1,0:T(8,128)} %copy-done.6, f32[640,1]{1,0:T(8,128)} %rsqrt.16.scale_ref, f32[1,1024]{1,0:T(1,128)} %bitcast.167, ...), custom_call_target="tpu_custom_call" | custom-call | flops 1048576 | bytes 65536 | tf_op jit(solution)/shard_map/combine_back/pallas_call | solution.py:384
  303.6 22.6 %attention_backward.1 = (bf16[640,3072]{1,0:T(8,128)(2,1)}, f32[8,2,136,384]{3,2,1,0:T(8,128)}) custom-call(s32[1,2]{1,0:T(1,128)} %lengths_ref.3, f32[8,2,512]{2,1,0:T(2,128)} %reshape.371.bias_ref, f32[8,2,640]{2,1,0:T(2,128)} %get-tuple-element.103.stat_ref, bf16[640,3072]{1,0:T(8,128)(2,1)} %convolution_convert_fusion.q_ref.k_ref.v_ref, ...), custom_call_target="tpu_custom_call" | custom-call | flops 1048576 | bytes 65536 | tf_op jit(solution)/shard_map/attention_backward/pallas_call | solution.py:223
  326.2 13.5 %shared_grads.1 = (bf16[512,4096]{1,0:T(8,128)(2,1)}, bf16[512,4096]{1,0:T(8,128)(2,1)}) custom-call(s32[1]{0:T(128)S(6)} %select_n.127.refs_0_, bf16[640,1024]{1,0:T(8,128)(2,1)} %copy-done.7, bf16[640,3072]{1,0:T(8,128)(2,1)} %get-tuple-element.159.refs_2_, bf16[640,1024]{1,0:T(8,128)(2,1)} %get-tuple-element.102.mixed_ref.refs_3_, ...), custom_call_target="tpu_custom_call" | custom-call | flops 1048576 | bytes 65536 | tf_op jit(solution)/shard_map/shared_grads/pallas_call | solution.py:693
  339.7 9.8 %collective-permute-done.13.refs_2_ = bf16[200,1024]{1,0:T(8,128)(2,1)} collective-permute-done((bf16[200,1024]{1,0:T(8,128)(2,1)}, bf16[200,1024]{1,0:T(8,128)(2,1)}, u32[]{:S(2)}, u32[]{:S(2)}) %collective-permute-start.13) | collective-permute-done | bytes 409632 | tf_op jit(solution)/shard_map/ppermute | solution.py:717
  349.5 9.1 %collective-permute-done.12.refs_1_ = bf16[200,1024]{1,0:T(8,128)(2,1)} collective-permute-done((bf16[200,1024]{1,0:T(8,128)(2,1)}, bf16[200,1024]{1,0:T(8,128)(2,1)}, u32[]{:S(2)}, u32[]{:S(2)}) %collective-permute-start.12) | collective-permute-done | bytes 409632 | tf_op jit(solution)/shard_map/ppermute | solution.py:717
  360.1 6.4 %fusion.16 = f32[32,8,2]{0,1,2:T(8,128)S(1)} fusion(f32[8,2,136,384]{3,2,1,0:T(8,128)} %get-tuple-element.160, s32[136,384]{1,0:T(8,128)S(1)} %fusion.39), kind=kOutput, calls=%fused_computation.27 | convolution fusion | flops 322535424 | bytes 3553280 | tf_op jit(solution)/shard_map/ghrc,rcb->bgh/dot_general | solution.py:276
  387.2 6.0 %fusion.14 = (f32[1024]{0:T(1024)S(1)}, f32[640]{0:T(1024)S(1)}, f32[640,1024]{1,0:T(8,128)}) fusion(bf16[640,1024]{1,0:T(8,128)(2,1)S(1)} %copy-done.3, f32[640]{0:T(1024)S(1)} %copy-done.18, f32[1024]{0:T(1024)S(1)} %copy-done.25, bf16[640,3072]{1,0:T(8,128)(2,1)S(1)} %copy-done.9, bf16[1024,3072]{1,0:T(8,128)(2,1)S(1)} %bitcast.169), kind=kOutput, calls=%fused_computation.20 | convolution fusion | flops 4031117824 | bytes 14169088 | tf_op jit(solution)/shard_map/dot_general | solution.py:31
  399.1 7.6 %combine_output.1 = bf16[640,1024]{1,0:T(8,128)(2,1)} custom-call(s32[640,2]{1,0:T(8,128)} %bitcast.160, f32[640,2]{1,0:T(8,128)} %exponential_divide_fusion.gates_ref, f32[640,1024]{1,0:T(8,128)} %copy-done.6, bf16[800,1024]{1,0:T(8,128)(2,1)} %bitcast.17.refs_0_, bf16[200,1024]{1,0:T(8,128)(2,1)} %collective-permute-done.12.refs_1_, ...), custom_call_target="tpu_custom_call" | custom-call | flops 235749998592 | bytes 65536 | tf_op jit(solution)/shard_map/combine_output/pallas_call | solution.py:361
  406.7 5.0 %fusion.13 = f32[640,1024]{1,0:T(8,128)} fusion(f32[640,1024]{1,0:T(8,128)} %get-tuple-element.158, bf16[640,1024]{1,0:T(8,128)(2,1)S(1)} %copy-done.4, f32[640,1024]{1,0:T(8,128)} %get-tuple-element.249, f32[640]{0:T(1024)S(1)} %copy-done.27, f32[1024]{0:T(1024)S(1)} %copy-done.26, f32[640]{0:T(1024)S(1)} %copy-done.19), kind=kLoop, calls=%fused_computation.19 | loop fusion | flops 4587520 | bytes 9184256 | tf_op jit(solution)/shard_map/add | solution.py:869
  411.7 13.3 %all-to-all-done.4 = f32[32,1,336]{2,1,0:T(1,128)} async-done(((f32[32,1,336]{2,1,0:T(1,128)}), f32[32,1,336]{2,1,0:T(1,128)}, u32[]{:S(2)}, u32[]{:S(2)}) %all-to-all-start.4) | async-done | bytes 43040 | tf_op jit(solution)/shard_map/all_to_all | solution.py:879
  437.2 6.1 %collective-permute-done.22 = bf16[128,1024]{1,0:T(8,128)(2,1)S(1)} collective-permute-done((bf16[128,1024]{1,0:T(8,128)(2,1)S(1)}, bf16[128,1024]{1,0:T(8,128)(2,1)S(1)}, u32[]{:S(2)}, u32[]{:S(2)}) %collective-permute-start.22) | collective-permute-done | bytes 262176 | tf_op jit(solution)/shard_map/ppermute | solution.py:717
  (198 shorter events, 127.8 us)
Async XLA Ops:
  13.4 54.2 %collective-permute-start = (bf16[208,1024]{1,0:T(8,128)(2,1)}, bf16[208,1024]{1,0:T(8,128)(2,1)}, u32[]{:S(2)}, u32[]{:S(2)}) collective-permute-start(bf16[208,1024]{1,0:T(8,128)(2,1)} %get-tuple-element.97), channel_id=1, source_target_pairs={{0,4},{1,5},{2,6},{3,7},{4,0},{5,1},{6,2},{7,3},{8,12},{9,13},{10,... | collective-permute-start | bytes 1277960 | tf_op jit(solution)/shard_map/ppermute | solution.py:717
  17.5 55.0 %collective-permute-start.1 = (bf16[208,1024]{1,0:T(8,128)(2,1)}, bf16[208,1024]{1,0:T(8,128)(2,1)}, u32[]{:S(2)}, u32[]{:S(2)}) collective-permute-start(bf16[208,1024]{1,0:T(8,128)(2,1)} %get-tuple-element.98), channel_id=1, source_target_pairs={{0,5},{1,4},{2,7},{3,6},{4,1},{5,0},{6,3},{7,2},{8,13},{9,12},{10,... | collective-permute-start | bytes 1277960 | tf_op jit(solution)/shard_map/ppermute | solution.py:717
  17.5 55.0 %collective-permute-start.2 = (bf16[208,1024]{1,0:T(8,128)(2,1)}, bf16[208,1024]{1,0:T(8,128)(2,1)}, u32[]{:S(2)}, u32[]{:S(2)}) collective-permute-start(bf16[208,1024]{1,0:T(8,128)(2,1)} %get-tuple-element.99), channel_id=1, source_target_pairs={{0,6},{1,7},{2,4},{3,5},{4,2},{5,3},{6,0},{7,1},{8,14},{9,15},{10,... | collective-permute-start | bytes 1277960 | tf_op jit(solution)/shard_map/ppermute | solution.py:717
  20.6 52.0 %collective-permute-start.3 = (bf16[208,1024]{1,0:T(8,128)(2,1)}, bf16[208,1024]{1,0:T(8,128)(2,1)}, u32[]{:S(2)}, u32[]{:S(2)}) collective-permute-start(bf16[208,1024]{1,0:T(8,128)(2,1)} %get-tuple-element.100), channel_id=1, source_target_pairs={{0,7},{1,6},{2,5},{3,4},{4,3},{5,2},{6,1},{7,0},{8,15},{9,14},{10,... | collective-permute-start | bytes 1277960 | tf_op jit(solution)/shard_map/ppermute | solution.py:717
  21.2 61.8 %all-to-all-start = ((bf16[4,208,1024]{2,1,0:T(8,128)(2,1)}), bf16[4,208,1024]{2,1,0:T(8,128)(2,1)}, u32[]{:S(2)}, u32[]{:S(2)}) async-start(bf16[4,208,1024]{2,1,0:T(8,128)(2,1)} %bitcast.155), calls=%async_computation | async-start | bytes 3407872 | tf_op jit(solution)/shard_map/all_to_all | solution.py:807
  93.7 63.4 %collective-permute-start.7 = (bf16[200,1024]{1,0:T(8,128)(2,1)}, bf16[200,1024]{1,0:T(8,128)(2,1)}, u32[]{:S(2)}, u32[]{:S(2)}) collective-permute-start(bf16[200,1024]{1,0:T(8,128)(2,1)} %get-tuple-element.120), channel_id=1, source_target_pairs={{0,7},{1,6},{2,5},{3,4},{4,3},{5,2},{6,1},{7,0},{8,15},{9,14},{10,... | collective-permute-start | bytes 1228808 | tf_op jit(solution)/shard_map/ppermute | solution.py:717
  99.9 57.2 %collective-permute-start.6 = (bf16[200,1024]{1,0:T(8,128)(2,1)}, bf16[200,1024]{1,0:T(8,128)(2,1)}, u32[]{:S(2)}, u32[]{:S(2)}) collective-permute-start(bf16[200,1024]{1,0:T(8,128)(2,1)} %get-tuple-element.118), channel_id=1, source_target_pairs={{0,6},{1,7},{2,4},{3,5},{4,2},{5,3},{6,0},{7,1},{8,14},{9,15},{10,... | collective-permute-start | bytes 1228808 | tf_op jit(solution)/shard_map/ppermute | solution.py:717
  100.2 61.5 %collective-permute-start.5 = (bf16[200,1024]{1,0:T(8,128)(2,1)}, bf16[200,1024]{1,0:T(8,128)(2,1)}, u32[]{:S(2)}, u32[]{:S(2)}) collective-permute-start(bf16[200,1024]{1,0:T(8,128)(2,1)} %get-tuple-element.116), channel_id=1, source_target_pairs={{0,5},{1,4},{2,7},{3,6},{4,1},{5,0},{6,3},{7,2},{8,13},{9,12},{10,... | collective-permute-start | bytes 1228808 | tf_op jit(solution)/shard_map/ppermute | solution.py:717
  100.2 70.5 %collective-permute-start.4 = (bf16[200,1024]{1,0:T(8,128)(2,1)}, bf16[200,1024]{1,0:T(8,128)(2,1)}, u32[]{:S(2)}, u32[]{:S(2)}) collective-permute-start(bf16[200,1024]{1,0:T(8,128)(2,1)} %get-tuple-element.114), channel_id=1, source_target_pairs={{0,4},{1,5},{2,6},{3,7},{4,0},{5,1},{6,2},{7,3},{8,12},{9,13},{10,... | collective-permute-start | bytes 1228808 | tf_op jit(solution)/shard_map/ppermute | solution.py:717
  152.4 57.5 %all-to-all-start.2 = ((bf16[4,200,1024]{2,1,0:T(8,128)(2,1)}), bf16[4,200,1024]{2,1,0:T(8,128)(2,1)}, u32[]{:S(2)}, u32[]{:S(2)}) async-start(bf16[4,200,1024]{2,1,0:T(8,128)(2,1)} %bitcast.157), calls=%async_computation.2 | async-start | bytes 3276800 | tf_op jit(solution)/shard_map/all_to_all | solution.py:807
  156.8 291.5 %reduce-scatter.2.cloned.1.call-start = ((), (), s32[]{:S(2)}) async-start(), calls=%async_computation.6 | async-start | bytes 21626880 | tf_op jit(solution)/shard_map/reduce_scatter | solution.py:848
  203.7 68.9 %collective-permute-start.10 = (bf16[200,1024]{1,0:T(8,128)(2,1)}, bf16[200,1024]{1,0:T(8,128)(2,1)S(1)}, u32[]{:S(2)}, u32[]{:S(2)}) collective-permute-start(bf16[200,1024]{1,0:T(8,128)(2,1)} %get-tuple-element.127), channel_id=1, source_target_pairs={{0,6},{1,7},{2,4},{3,5},{4,2},{5,3},{6,0},{7,1},{8,14},{9,15},{10,... | collective-permute-start | bytes 1228808 | tf_op jit(solution)/shard_map/ppermute | solution.py:717
  207.5 65.1 %collective-permute-start.11 = (bf16[200,1024]{1,0:T(8,128)(2,1)}, bf16[200,1024]{1,0:T(8,128)(2,1)S(1)}, u32[]{:S(2)}, u32[]{:S(2)}) collective-permute-start(bf16[200,1024]{1,0:T(8,128)(2,1)} %get-tuple-element.128), channel_id=1, source_target_pairs={{0,7},{1,6},{2,5},{3,4},{4,3},{5,2},{6,1},{7,0},{8,15},{9,14},{10,... | collective-permute-start | bytes 1228808 | tf_op jit(solution)/shard_map/ppermute | solution.py:717
  207.5 65.1 %collective-permute-start.8 = (bf16[200,1024]{1,0:T(8,128)(2,1)}, bf16[200,1024]{1,0:T(8,128)(2,1)S(1)}, u32[]{:S(2)}, u32[]{:S(2)}) collective-permute-start(bf16[200,1024]{1,0:T(8,128)(2,1)} %get-tuple-element.125), channel_id=1, source_target_pairs={{0,4},{1,5},{2,6},{3,7},{4,0},{5,1},{6,2},{7,3},{8,12},{9,13},{10,... | collective-permute-start | bytes 1228808 | tf_op jit(solution)/shard_map/ppermute | solution.py:717
  207.5 69.6 %collective-permute-start.9 = (bf16[200,1024]{1,0:T(8,128)(2,1)}, bf16[200,1024]{1,0:T(8,128)(2,1)}, u32[]{:S(2)}, u32[]{:S(2)}) collective-permute-start(bf16[200,1024]{1,0:T(8,128)(2,1)} %get-tuple-element.126), channel_id=1, source_target_pairs={{0,5},{1,4},{2,7},{3,6},{4,1},{5,0},{6,3},{7,2},{8,13},{9,12},{10,... | collective-permute-start | bytes 1228808 | tf_op jit(solution)/shard_map/ppermute | solution.py:717
  277.1 81.5 %all-to-all-start.3 = ((bf16[4,200,1024]{2,1,0:T(8,128)(2,1)}), bf16[4,200,1024]{2,1,0:T(8,128)(2,1)}, u32[]{:S(2)}, u32[]{:S(2)}) async-start(bf16[4,200,1024]{2,1,0:T(8,128)(2,1)} %bitcast.156), calls=%async_computation.3 | async-start | bytes 3276800 | tf_op jit(solution)/shard_map/all_to_all | solution.py:807
  283.7 56.0 %collective-permute-start.15 = (bf16[200,1024]{1,0:T(8,128)(2,1)}, bf16[200,1024]{1,0:T(8,128)(2,1)}, u32[]{:S(2)}, u32[]{:S(2)}) collective-permute-start(bf16[200,1024]{1,0:T(8,128)(2,1)} %get-tuple-element.155), channel_id=1, source_target_pairs={{0,7},{1,6},{2,5},{3,4},{4,3},{5,2},{6,1},{7,0},{8,15},{9,14},{10,... | collective-permute-start | bytes 1228808 | tf_op jit(solution)/shard_map/ppermute | solution.py:717
  286.0 53.7 %collective-permute-start.14 = (bf16[200,1024]{1,0:T(8,128)(2,1)}, bf16[200,1024]{1,0:T(8,128)(2,1)}, u32[]{:S(2)}, u32[]{:S(2)}) collective-permute-start(bf16[200,1024]{1,0:T(8,128)(2,1)} %get-tuple-element.153), channel_id=1, source_target_pairs={{0,6},{1,7},{2,4},{3,5},{4,2},{5,3},{6,0},{7,1},{8,14},{9,15},{10,... | collective-permute-start | bytes 1228808 | tf_op jit(solution)/shard_map/ppermute | solution.py:717
  287.6 61.9 %collective-permute-start.13 = (bf16[200,1024]{1,0:T(8,128)(2,1)}, bf16[200,1024]{1,0:T(8,128)(2,1)}, u32[]{:S(2)}, u32[]{:S(2)}) collective-permute-start(bf16[200,1024]{1,0:T(8,128)(2,1)} %get-tuple-element.151), channel_id=1, source_target_pairs={{0,5},{1,4},{2,7},{3,6},{4,1},{5,0},{6,3},{7,2},{8,13},{9,12},{10,... | collective-permute-start | bytes 1228808 | tf_op jit(solution)/shard_map/ppermute | solution.py:717
  287.6 71.0 %collective-permute-start.12 = (bf16[200,1024]{1,0:T(8,128)(2,1)}, bf16[200,1024]{1,0:T(8,128)(2,1)}, u32[]{:S(2)}, u32[]{:S(2)}) collective-permute-start(bf16[200,1024]{1,0:T(8,128)(2,1)} %get-tuple-element.149), channel_id=1, source_target_pairs={{0,4},{1,5},{2,6},{3,7},{4,0},{5,1},{6,2},{7,3},{8,12},{9,13},{10,... | collective-permute-start | bytes 1228808 | tf_op jit(solution)/shard_map/ppermute | solution.py:717
  375.1 50.8 %collective-permute-start.17 = (bf16[2,128,1024]{2,1,0:T(8,128)(2,1)}, bf16[2,128,1024]{2,1,0:T(8,128)(2,1)}, u32[]{:S(2)}, u32[]{:S(2)}) collective-permute-start(bf16[2,128,1024]{2,1,0:T(8,128)(2,1)} %fusion.22), channel_id=1, source_target_pairs={{0,8},{8,0},{16,24},{24,16},{1,9},{9,1},{17,25},{25,17},{2,10},{10... | collective-permute-start | bytes 1572872 | tf_op jit(solution)/shard_map/ppermute | solution.py:717
  377.6 48.2 %collective-permute-start.21 = (bf16[4,32,2048]{2,1,0:T(8,128)(2,1)}, bf16[4,32,2048]{2,1,0:T(8,128)(2,1)}, u32[]{:S(2)}, u32[]{:S(2)}) collective-permute-start(bf16[4,32,2048]{2,1,0:T(8,128)(2,1)} %fusion.27), channel_id=1, source_target_pairs={{0,6},{1,7},{2,4},{3,5},{4,2},{5,3},{6,0},{7,1},{8,14},{9,15},{10,... | collective-permute-start | bytes 1572872 | tf_op jit(solution)/shard_map/ppermute | solution.py:717
  379.4 46.4 %collective-permute-start.19 = (bf16[4,32,2048]{2,1,0:T(8,128)(2,1)}, bf16[4,32,2048]{2,1,0:T(8,128)(2,1)}, u32[]{:S(2)}, u32[]{:S(2)}) collective-permute-start(bf16[4,32,2048]{2,1,0:T(8,128)(2,1)} %get-tuple-element.225), channel_id=1, source_target_pairs={{0,2},{1,3},{2,0},{3,1},{4,6},{5,7},{6,4},{7,5},{8,10},{9,11},{10,... | collective-permute-start | bytes 1572872 | tf_op jit(solution)/shard_map/ppermute | solution.py:717
  379.4 46.4 %collective-permute-start.20 = (bf16[4,32,2048]{2,1,0:T(8,128)(2,1)}, bf16[4,32,2048]{2,1,0:T(8,128)(2,1)}, u32[]{:S(2)}, u32[]{:S(2)}) collective-permute-start(bf16[4,32,2048]{2,1,0:T(8,128)(2,1)} %get-tuple-element.224), channel_id=1, source_target_pairs={{0,4},{1,5},{2,6},{3,7},{4,0},{5,1},{6,2},{7,3},{8,12},{9,13},{10,... | collective-permute-start | bytes 1572872 | tf_op jit(solution)/shard_map/ppermute | solution.py:717
  (45 other events, 629.3 us)
Sparse Core Ops, SparseCore 0:
  251.3 171.1 reduce-scatter.1

commit v7 on v6

--- a/solution.py
+++ b/solution.py
@@ -23,7 +23,7 @@
 EXTRA = 8
 SHORT = pl.CostEstimate(flops=23_000_000_000, bytes_accessed=1 << 16, transcendentals=0)
 SMALL = pl.CostEstimate(flops=1 << 20, bytes_accessed=1 << 16, transcendentals=0)
-MEDIUM = pl.CostEstimate(flops=235_750_000_000, bytes_accessed=1 << 16, transcendentals=0)
+MEDIUM = pl.CostEstimate(flops=249_550_000_000, bytes_accessed=1 << 16, transcendentals=0)
 LARGE = pl.CostEstimate(flops=1 << 38, bytes_accessed=1 << 28, transcendentals=0)
 
 
@@ -652,19 +652,23 @@
     )(hidden, wd)
 
 
-def shared_kernel(
-    core_ref, first_ref, wide_ref, second_ref, narrow_ref, mine_ref, away_ref, left_ref, *, steps, unit
-):
+def shared_kernel(core_ref, first_ref, wide_ref, second_ref, narrow_ref, *refs, steps, early, unit):
+    low_refs, high_refs, left_ref = refs[:2], refs[2:4], refs[4]
     step = pl.program_id(0)
 
     def store(value):
         own = core_ref[0] == 0
-        for group in range(mine_ref.shape[0] // unit):
-            low = value[2 * group * unit : (2 * group + 1) * unit, :]
-            high = value[(2 * group + 1) * unit : (2 * group + 2) * unit, :]
-            span = slice(group * unit, (group + 1) * unit)
-            mine_ref[span, :] = jnp.where(own, low, high).astype(jnp.bfloat16)
-            away_ref[span, :] = jnp.where(own, high, low).astype(jnp.bfloat16)
+
+        def fill(mine_ref, away_ref):
+            for group in range(mine_ref.shape[0] // unit):
+                low = value[2 * group * unit : (2 * group + 1) * unit, :]
+                high = value[(2 * group + 1) * unit : (2 * group + 2) * unit, :]
+                span = slice(group * unit, (group + 1) * unit)
+                mine_ref[span, :] = jnp.where(own, low, high).astype(jnp.bfloat16)
+                away_ref[span, :] = jnp.where(own, high, low).astype(jnp.bfloat16)
+
+        pl.when(step < early)(lambda: fill(*low_refs))
+        pl.when(step >= early)(lambda: fill(*high_refs))
 
     @pl.when(step == 0)
     def _():
@@ -688,10 +692,12 @@
     tile = 512
     steps, more = wide.shape[1] // tile, narrow.shape[1] // tile
     whole = once((tokens, rows))
-    out = pl.BlockSpec((rows // 2, tile), lambda i: (0, i))
-    shape = jax.ShapeDtypeStruct((rows // 2, wide.shape[1] + narrow.shape[1]), jnp.bfloat16)
+    early = (steps + more) * 5 // 8
+    low = pl.BlockSpec((rows // 2, tile), lambda i: (0, jnp.minimum(i, early - 1)))
+    high = pl.BlockSpec((rows // 2, tile), lambda i: (0, jnp.maximum(i - early, 0)))
+    shapes = [jax.ShapeDtypeStruct((rows // 2, n * tile), jnp.bfloat16) for n in (early, steps + more - early)]
     return pl.pallas_call(
-        lambda *refs: shared_kernel(*refs, steps=steps, unit=unit),
+        lambda *refs: shared_kernel(*refs, steps=steps, early=early, unit=unit),
         grid=(steps + more,),
         in_specs=[
             pl.BlockSpec(memory_space=pltpu.SMEM),
@@ -700,8 +706,8 @@
             whole,
             pl.BlockSpec((tokens, tile), lambda i: (0, jnp.maximum(i - steps, 0))),
         ],
-        out_specs=[out, out],
-        out_shape=[shape, shape],
+        out_specs=[low, low, high, high],
+        out_shape=[shapes[0], shapes[0], shapes[1], shapes[1]],
         scratch_shapes=[pltpu.VMEM((rows, tokens), jnp.bfloat16)],
         cost_estimate=SMALL,
         name="shared_grads",
@@ -856,11 +862,9 @@
     mixed_grad = dot(attn_grad, w_attn_out, NT).astype(jnp.bfloat16)
     proj_grad, tiles = attention_backward(item_lengths, bias, stat, proj, mixed, mixed_grad)
     unit = width // (copies * ways)
-    mine, away = shared_grads(own % 2, attn_in, proj_grad, mixed, attn_grad, unit)
-    both = (mine, swap(after(away, *returned), "expert", 1))
-    cut = mine.shape[1] // 2
-    dp_parts = dp_halves([part[:, :cut] for part in both], unit)
-    z_parts = chip_parts([part[:, cut:] for part in both], unit)
+    low, low_away, high, high_away = shared_grads(own % 2, attn_in, proj_grad, mixed, attn_grad, unit)
+    dp_parts = dp_halves((low, swap(after(low_away, *returned), "expert", 1)), unit)
+    z_parts = chip_parts((high, swap(after(high_away, *returned), "expert", 1)), unit)
     proj_grad, _ = lax.optimization_barrier((proj_grad, (dp_parts, z_parts)))
     table_grad = table_sums(tiles, buckets)
     router_grad = (near_router + far_router)[:experts].T

time: 475 us -> 471 us (level)
  waiting for transfers between devices: 74.5 us -> 63.7 us
    all_to_all x1, waiting for transfers between devices: 13.3 us -> 0.01 us  [on_device(): lax.all_to_all(together, ('dp', 'expert'), split_axis=0, concat_axis=0, t...]
    slice x2 -> x0, local copies, waits for them, and re-layouts: 5.6 us -> none  [on_device(): z_parts = chip_parts([part[:, cut:] for part in both], unit)]
    ppermute x30 -> x31, waiting for transfers between devices: 50.7 us -> 53.5 us  [swap(): return lax.ppermute(value, axis, [(k, k ^ step) for k in range(size)])]
    ppermute x30 -> x31, starting transfers between devices: 47.8 us -> 49.1 us  [swap(): return lax.ppermute(value, axis, [(k, k ^ step) for k in range(size)])]
  transfers between devices with their start and end apart: 36 -> 37, of which waited for: 11 -> 9; matrix products, arithmetic and copies ran while one was open for 15% -> 16% of each run, Pallas kernels for 47% -> 47%
where the time goes in v7:
time: 471 us; the launch traced here: 465 us
  Pallas kernels  227 us (48%)
  starting transfers between devices  77.7 us (16%)
  waiting for transfers between devices  63.7 us (14%)
  matrix products  31.6 us (7%)
  other arithmetic  31.4 us (7%)
  local copies, waits for them, and re-layouts  18.5 us (4%)
  between operations  14.9 us (3%)
    pallas_call x2, Pallas kernels, expert_rows(): pl.pallas_call(lambda *refs: expert_kernel(*refs, ways=ways, parts=parts)...  65.8 us
    ppermute x31, waiting for transfers between devices, swap(): return lax.ppermute(value, axis, [(k, k ^ step) for k in range(size)])  53.5 us
    ppermute x31, starting transfers between devices, swap(): return lax.ppermute(value, axis, [(k, k ^ step) for k in range(size)])  49.1 us
    pallas_call x1, Pallas kernels, weight_grads(): pl.pallas_call(lambda *refs: weight_kernel(*refs, ways=ways, copies=copie...  41.3 us
    all_to_all x4, starting transfers between devices, near(): lax.all_to_all(parts, 'expert', split_axis=0, concat_axis=0, axis_index_g...  25.1 us
    dot_general x5, matrix products, dot(): return lax.dot_general(a, b, dims, preferred_element_type=jnp.float32)  25 us
    pallas_call x1, Pallas kernels, attention_backward(): pl.pallas_call(attention_backward_kernel, grid=(pairs,), in_specs=[pl.Blo...  22.7 us
    pallas_call x1, Pallas kernels, result_rows(): pl.pallas_call(result_kernel, grid=(f // tile,), in_specs=[pl.BlockSpec((...  21.3 us
  transfers between devices with their start and end apart: 37, of which 9 were waited for; matrix products, arithmetic and copies ran while one was open for 16% of the time, Pallas kernels for 47%

profile of v7, /device:TPU:0, one launch (start us, length us, event | category | flops | bytes accessed | tf_op | source)
XLA Modules:
  0.0 464.5 jit_solution(5738709834007410232)
XLA Ops:
  7.2 6.2 %pack_first.1 = (bf16[832,1024]{1,0:T(8,128)(2,1)}, bf16[208,1024]{1,0:T(8,128)(2,1)}, bf16[208,1024]{1,0:T(8,128)(2,1)}, bf16[208,1024]{1,0:T(8,128)(2,1)}, bf1...) custom-call(s32[1]{0:T(128)} %bitcast.refs_0_, s32[2,640]{1,0:T(2,128)} %bitcast.163, bf16[640,1024]{1,0:T(8,128)(2,1)} %upstream_ref.1), custom_call_target="tpu_custom_call" | custom-call | flops 1048576 | bytes 65536 | tf_op jit(solution)/shard_map/pack_first/pallas_call | solution.py:323
  28.7 8.5 %convolution_convert_fusion.q_ref.k_ref.v_ref = bf16[640,3072]{1,0:T(8,128)(2,1)} fusion(bf16[640,1024]{1,0:T(8,128)(2,1)S(1)} %fusion.9.refs_1_, bf16[1024,3072]{1,0:T(8,128)(2,1)} %param.16), kind=kOutput, calls=%fused_computation.3 | convolution fusion | flops 4028497920 | bytes 11534336 | tf_op jit(solution)/shard_map/dot_general | solution.py:31
  37.2 16.0 %attention_forward.1 = (bf16[640,1024]{1,0:T(8,128)(2,1)}, f32[8,2,640]{2,1,0:T(2,128)}) custom-call(s32[1,2]{1,0:T(1,128)} %lengths_ref.3, f32[8,2,512]{2,1,0:T(2,128)} %reshape.371.bias_ref, bf16[640,3072]{1,0:T(8,128)(2,1)} %convolution_convert_fusion.q_ref.k_ref.v_ref, bf16[640,3072]{1,0:T(8,128)(2,1)} %convolution_convert_fusion.q_ref.k_ref.v_ref, ...), custom_call_target="tpu_custom_call" | custom-call | flops 1048576 | bytes 65536 | tf_op jit(solution)/shard_map/attention_forward/pallas_call | solution.py:110
  59.5 4.9 %pack_rows.1 = (bf16[800,1024]{1,0:T(8,128)(2,1)}, bf16[200,1024]{1,0:T(8,128)(2,1)}, bf16[200,1024]{1,0:T(8,128)(2,1)}, bf16[200,1024]{1,0:T(8,128)(2,1)}, bf16[200,1024]{1,0:T(8,128)(2,1)}) custom-call(s32[2,640]{1,0:T(2,128)} %get-tuple-element.98.refs_0_, bf16[640,1024]{1,0:T(8,128)(2,1)} %copy-done.5), custom_call_target="tpu_custom_call" | custom-call | flops 1048576 | bytes 65536 | tf_op jit(solution)/shard_map/pack_rows/pallas_call | solution.py:334
  67.4 5.2 %collective-permute-done.1.refs_3_.refs_12_ = bf16[208,1024]{1,0:T(8,128)(2,1)} collective-permute-done((bf16[208,1024]{1,0:T(8,128)(2,1)}, bf16[208,1024]{1,0:T(8,128)(2,1)}, u32[]{:S(2)}, u32[]{:S(2)}) %collective-permute-start.1) | collective-permute-done | bytes 426016 | tf_op jit(solution)/shard_map/ppermute | solution.py:723
  72.5 10.2 %all-to-all-done = bf16[4,208,1024]{2,1,0:T(8,128)(2,1)} async-done(((bf16[4,208,1024]{2,1,0:T(8,128)(2,1)}), bf16[4,208,1024]{2,1,0:T(8,128)(2,1)}, u32[]{:S(2)}, u32[]{:S(2)}) %all-to-all-start) | async-done | bytes 1703968 | tf_op jit(solution)/shard_map/all_to_all | solution.py:813
  82.8 11.4 %all-to-all-start.1 = ((bf16[4,200,1024]{2,1,0:T(8,128)(2,1)}), bf16[4,200,1024]{2,1,0:T(8,128)(2,1)}, u32[]{:S(2)}, u32[]{:S(2)}) async-start(bf16[4,200,1024]{2,1,0:T(8,128)(2,1)} %bitcast.153), calls=%async_computation.1 | async-start | bytes 3276800 | tf_op jit(solution)/shard_map/all_to_all | solution.py:813
  94.2 6.2 %collective-permute-start.7 = (bf16[200,1024]{1,0:T(8,128)(2,1)}, bf16[200,1024]{1,0:T(8,128)(2,1)}, u32[]{:S(2)}, u32[]{:S(2)}) collective-permute-start(bf16[200,1024]{1,0:T(8,128)(2,1)} %get-tuple-element.123), channel_id=1, source_target_pairs={{0,7},{1,6},{2,5},{3,4},{4,3},{5,2},{6,1},{7,0},{8,15},{9,14},{10,... | collective-permute-start | bytes 1228808 | tf_op jit(solution)/shard_map/ppermute | solution.py:723
  103.2 16.7 %slope_rows.1 = (bf16[1600,2816]{1,0:T(8,128)(2,1)}, f32[1600,128]{1,0:T(8,128)}) custom-call(bf16[2816,1024]{1,0:T(8,128)(2,1)} %bitcast.143, bf16[832,1024]{1,0:T(8,128)(2,1)} %bitcast.7.refs_1_.refs_10_, bf16[208,1024]{1,0:T(8,128)(2,1)} %collective-permute-done.refs_2_.refs_11_, bf16[208,1024]{1,0:T(8,128)(2,1)} %collective-permute-done.1.refs_3_.refs_12_, ...), custom_call_target="tpu_custom_call" | custom-call | flops 274877906944 | bytes 268435456 | tf_op jit(solution)/shard_map/slope_rows/pallas_call | solution.py:522
  119.9 32.9 %expert_rows.2 = (bf16[1600,2816]{1,0:T(8,128)(2,1)}, bf16[1600,2816]{1,0:T(8,128)(2,1)}, bf16[1600,2816]{1,0:T(8,128)(2,1)}, f32[800,128]{1,0:T(8,128)}, f32[12...) custom-call(s32[1]{0:T(128)} %bitcast.refs_0_, bf16[1600,2816]{1,0:T(8,128)(2,1)} %get-tuple-element.107.refs_1_, ...), custom_call_target="tpu_custom_call" | custom-call | flops 1048576 | bytes 65536 | tf_op jit(solution)/shard_map/expert_rows/pallas_call | solution.py:476
  162.1 9.0 %collective-permute-done.4.refs_6_ = bf16[200,1024]{1,0:T(8,128)(2,1)} collective-permute-done((bf16[200,1024]{1,0:T(8,128)(2,1)}, bf16[200,1024]{1,0:T(8,128)(2,1)}, u32[]{:S(2)}, u32[]{:S(2)}) %collective-permute-start.4) | collective-permute-done | bytes 409632 | tf_op jit(solution)/shard_map/ppermute | solution.py:723
  171.1 32.9 %expert_rows.3 = (bf16[1600,2816]{1,0:T(8,128)(2,1)}, bf16[1600,2816]{1,0:T(8,128)(2,1)}, bf16[1600,2816]{1,0:T(8,128)(2,1)}, f32[800,128]{1,0:T(8,128)}, f32[12...) custom-call(s32[1]{0:T(128)} %bitcast.refs_0_, ...), custom_call_target="tpu_custom_call", output_to_operand_aliasing={{0}: (10, {}), {1}: (11, {}), {2}: (12, {})} | custom-call | flops 23000000512 | bytes 65536 | tf_op jit(solution)/shard_map/expert_rows/pallas_call | solution.py:476
  210.3 41.3 %weight_grads.1 = bf16[2816,3072]{1,0:T(8,128)(2,1)} custom-call(bf16[1600,2816]{1,0:T(8,128)(2,1)} %get-tuple-element.138.refs_0_.hidden_ref, bf16[1600,2816]{1,0:T(8,128)(2,1)} %get-tuple-element.134.refs_1_, bf16[1600,2816]{1,0:T(8,128)(2,1)} %get-tuple-element.135.refs_2_, f32[800,128]{1,0:T(8,128)} %get-tuple-element.136.refs_3_, ...), custom_call_target="tpu_custom_call" | custom-call | flops 1048576 | bytes 65536 | tf_op jit(solution)/shard_map/weight_grads/pallas_call | solution.py:599
  251.6 21.3 %result_rows.1 = (bf16[800,1024]{1,0:T(8,128)(2,1)}, bf16[200,1024]{1,0:T(8,128)(2,1)}, bf16[200,1024]{1,0:T(8,128)(2,1)}, bf16[200,1024]{1,0:T(8,128)(2,1)}, bf16[200,1024]{1,0:T(8,128)(2,1)}) custom-call(bf16[1600,2816]{1,0:T(8,128)(2,1)} %get-tuple-element.138.refs_0_.hidden_ref, bf16[2816,1024]{1,0:T(8,128)(2,1)} %bitcast.144), custom_call_target="tpu_custom_call" | custom-call | flops 1048576 | bytes 65536 | tf_op jit(solution)/shard_map/result_rows/pallas_call | solution.py:643
  290.0 9.7 %combine_back.1 = (f32[640,1024]{1,0:T(8,128)}, bf16[640,1024]{1,0:T(8,128)(2,1)}, f32[1,1024]{1,0:T(1,128)}) custom-call(s32[640,2]{1,0:T(8,128)} %bitcast.156, f32[640,2]{1,0:T(8,128)} %exponential_divide_fusion.gates_ref, f32[640,1024]{1,0:T(8,128)} %copy-done.6, f32[640,1]{1,0:T(8,128)} %rsqrt.16.scale_ref, f32[1,1024]{1,0:T(1,128)} %bitcast.164, ...), custom_call_target="tpu_custom_call" | custom-call | flops 1048576 | bytes 65536 | tf_op jit(solution)/shard_map/combine_back/pallas_call | solution.py:384
  303.6 22.7 %attention_backward.1 = (bf16[640,3072]{1,0:T(8,128)(2,1)}, f32[8,2,136,384]{3,2,1,0:T(8,128)}) custom-call(s32[1,2]{1,0:T(1,128)} %lengths_ref.3, f32[8,2,512]{2,1,0:T(2,128)} %reshape.371.bias_ref, f32[8,2,640]{2,1,0:T(2,128)} %get-tuple-element.106.stat_ref, bf16[640,3072]{1,0:T(8,128)(2,1)} %convolution_convert_fusion.q_ref.k_ref.v_ref, ...), custom_call_target="tpu_custom_call" | custom-call | flops 1048576 | bytes 65536 | tf_op jit(solution)/shard_map/attention_backward/pallas_call | solution.py:223
  326.3 14.8 %shared_grads.1 = (bf16[512,2560]{1,0:T(8,128)(2,1)}, bf16[512,2560]{1,0:T(8,128)(2,1)}, bf16[512,1536]{1,0:T(8,128)(2,1)}, bf16[512,1536]{1,0:T(8,128)(2,1)}) custom-call(s32[1]{0:T(128)S(6)} %select_n.128.refs_0_, bf16[640,1024]{1,0:T(8,128)(2,1)} %copy-done.11, bf16[640,3072]{1,0:T(8,128)(2,1)} %get-tuple-element.165.refs_2_, ...), custom_call_target="tpu_custom_call" | custom-call | flops 1048576 | bytes 65536 | tf_op jit(solution)/shard_map/shared_grads/pallas_call | solution.py:699
  341.2 8.5 %collective-permute-done.13.refs_2_ = bf16[200,1024]{1,0:T(8,128)(2,1)} collective-permute-done((bf16[200,1024]{1,0:T(8,128)(2,1)}, bf16[200,1024]{1,0:T(8,128)(2,1)}, u32[]{:S(2)}, u32[]{:S(2)}) %collective-permute-start.13) | collective-permute-done | bytes 409632 | tf_op jit(solution)/shard_map/ppermute | solution.py:723
  349.7 9.1 %collective-permute-done.12.refs_1_ = bf16[200,1024]{1,0:T(8,128)(2,1)} collective-permute-done((bf16[200,1024]{1,0:T(8,128)(2,1)}, bf16[200,1024]{1,0:T(8,128)(2,1)}, u32[]{:S(2)}, u32[]{:S(2)}) %collective-permute-start.12) | collective-permute-done | bytes 409632 | tf_op jit(solution)/shard_map/ppermute | solution.py:723
  360.8 6.2 %fusion.17 = f32[32,8,2]{0,1,2:T(8,128)S(1)} fusion(f32[8,2,136,384]{3,2,1,0:T(8,128)} %get-tuple-element.166, s32[136,384]{1,0:T(8,128)S(1)} %fusion.39), kind=kOutput, calls=%fused_computation.32 | convolution fusion | flops 322535424 | bytes 3553280 | tf_op jit(solution)/shard_map/ghrc,rcb->bgh/dot_general | solution.py:276
  387.5 9.2 %fusion.14 = (f32[1024]{0:T(1024)S(1)}, f32[640]{0:T(1024)S(1)}, f32[640,1024]{1,0:T(8,128)}) fusion(bf16[640,1024]{1,0:T(8,128)(2,1)S(1)} %copy-done.3, f32[640]{0:T(1024)S(1)} %copy-done.24, f32[1024]{0:T(1024)S(1)} %copy-done.31, bf16[640,3072]{1,0:T(8,128)(2,1)S(1)} %copy-done.13, bf16[1024,3072]{1,0:T(8,128)(2,1)} %param.16), kind=kOutput, calls=%fused_computation.20 | convolution fusion | flops 4031117824 | bytes 14169088 | tf_op jit(solution)/shard_map/dot_general | solution.py:31
  401.5 7.3 %combine_output.1 = bf16[640,1024]{1,0:T(8,128)(2,1)} custom-call(s32[640,2]{1,0:T(8,128)} %bitcast.157, f32[640,2]{1,0:T(8,128)} %exponential_divide_fusion.gates_ref, f32[640,1024]{1,0:T(8,128)} %copy-done.6, bf16[800,1024]{1,0:T(8,128)(2,1)} %bitcast.17.refs_0_, bf16[200,1024]{1,0:T(8,128)(2,1)} %collective-permute-done.12.refs_1_, ...), custom_call_target="tpu_custom_call" | custom-call | flops 249549996032 | bytes 65536 | tf_op jit(solution)/shard_map/combine_output/pallas_call | solution.py:361
  408.9 4.8 %fusion.13 = f32[640,1024]{1,0:T(8,128)} fusion(f32[640,1024]{1,0:T(8,128)} %get-tuple-element.161, bf16[640,1024]{1,0:T(8,128)(2,1)S(1)} %copy-done.4, f32[640,1024]{1,0:T(8,128)} %get-tuple-element.251, f32[640]{0:T(1024)S(1)} %copy-done.33, f32[1024]{0:T(1024)S(1)} %copy-done.32, f32[640]{0:T(1024)S(1)} %copy-done.25), kind=kLoop, calls=%fused_computation.19 | loop fusion | flops 4587520 | bytes 9184256 | tf_op jit(solution)/shard_map/add | solution.py:873
  426.2 9.2 %collective-permute-done.24 = bf16[128,1280]{1,0:T(8,128)(2,1)S(1)} collective-permute-done((bf16[128,1280]{1,0:T(8,128)(2,1)S(1)}, bf16[128,1280]{1,0:T(8,128)(2,1)S(1)}, u32[]{:S(2)}, u32[]{:S(2)}) %collective-permute-start.24) | collective-permute-done | bytes 327712 | tf_op jit(solution)/shard_map/ppermute | solution.py:723
  (206 shorter events, 125.4 us)
Async XLA Ops:
  13.4 54.0 %collective-permute-start = (bf16[208,1024]{1,0:T(8,128)(2,1)}, bf16[208,1024]{1,0:T(8,128)(2,1)}, u32[]{:S(2)}, u32[]{:S(2)}) collective-permute-start(bf16[208,1024]{1,0:T(8,128)(2,1)} %get-tuple-element.100), channel_id=1, source_target_pairs={{0,4},{1,5},{2,6},{3,7},{4,0},{5,1},{6,2},{7,3},{8,12},{9,13},{10,... | collective-permute-start | bytes 1277960 | tf_op jit(solution)/shard_map/ppermute | solution.py:723
  17.5 55.0 %collective-permute-start.1 = (bf16[208,1024]{1,0:T(8,128)(2,1)}, bf16[208,1024]{1,0:T(8,128)(2,1)}, u32[]{:S(2)}, u32[]{:S(2)}) collective-permute-start(bf16[208,1024]{1,0:T(8,128)(2,1)} %get-tuple-element.101), channel_id=1, source_target_pairs={{0,5},{1,4},{2,7},{3,6},{4,1},{5,0},{6,3},{7,2},{8,13},{9,12},{10,... | collective-permute-start | bytes 1277960 | tf_op jit(solution)/shard_map/ppermute | solution.py:723
  17.5 55.0 %collective-permute-start.2 = (bf16[208,1024]{1,0:T(8,128)(2,1)}, bf16[208,1024]{1,0:T(8,128)(2,1)}, u32[]{:S(2)}, u32[]{:S(2)}) collective-permute-start(bf16[208,1024]{1,0:T(8,128)(2,1)} %get-tuple-element.102), channel_id=1, source_target_pairs={{0,6},{1,7},{2,4},{3,5},{4,2},{5,3},{6,0},{7,1},{8,14},{9,15},{10,... | collective-permute-start | bytes 1277960 | tf_op jit(solution)/shard_map/ppermute | solution.py:723
  20.6 52.0 %collective-permute-start.3 = (bf16[208,1024]{1,0:T(8,128)(2,1)}, bf16[208,1024]{1,0:T(8,128)(2,1)}, u32[]{:S(2)}, u32[]{:S(2)}) collective-permute-start(bf16[208,1024]{1,0:T(8,128)(2,1)} %get-tuple-element.103), channel_id=1, source_target_pairs={{0,7},{1,6},{2,5},{3,4},{4,3},{5,2},{6,1},{7,0},{8,15},{9,14},{10,... | collective-permute-start | bytes 1277960 | tf_op jit(solution)/shard_map/ppermute | solution.py:723
  21.2 61.6 %all-to-all-start = ((bf16[4,208,1024]{2,1,0:T(8,128)(2,1)}), bf16[4,208,1024]{2,1,0:T(8,128)(2,1)}, u32[]{:S(2)}, u32[]{:S(2)}) async-start(bf16[4,208,1024]{2,1,0:T(8,128)(2,1)} %bitcast.150), calls=%async_computation | async-start | bytes 3407872 | tf_op jit(solution)/shard_map/all_to_all | solution.py:813
  82.8 37.2 %all-to-all-start.1 = ((bf16[4,200,1024]{2,1,0:T(8,128)(2,1)}), bf16[4,200,1024]{2,1,0:T(8,128)(2,1)}, u32[]{:S(2)}, u32[]{:S(2)}) async-start(bf16[4,200,1024]{2,1,0:T(8,128)(2,1)} %bitcast.153), calls=%async_computation.1 | async-start | bytes 3276800 | tf_op jit(solution)/shard_map/all_to_all | solution.py:813
  94.2 63.3 %collective-permute-start.7 = (bf16[200,1024]{1,0:T(8,128)(2,1)}, bf16[200,1024]{1,0:T(8,128)(2,1)}, u32[]{:S(2)}, u32[]{:S(2)}) collective-permute-start(bf16[200,1024]{1,0:T(8,128)(2,1)} %get-tuple-element.123), channel_id=1, source_target_pairs={{0,7},{1,6},{2,5},{3,4},{4,3},{5,2},{6,1},{7,0},{8,15},{9,14},{10,... | collective-permute-start | bytes 1228808 | tf_op jit(solution)/shard_map/ppermute | solution.py:723
  100.3 57.1 %collective-permute-start.6 = (bf16[200,1024]{1,0:T(8,128)(2,1)}, bf16[200,1024]{1,0:T(8,128)(2,1)}, u32[]{:S(2)}, u32[]{:S(2)}) collective-permute-start(bf16[200,1024]{1,0:T(8,128)(2,1)} %get-tuple-element.121), channel_id=1, source_target_pairs={{0,6},{1,7},{2,4},{3,5},{4,2},{5,3},{6,0},{7,1},{8,14},{9,15},{10,... | collective-permute-start | bytes 1228808 | tf_op jit(solution)/shard_map/ppermute | solution.py:723
  100.7 61.5 %collective-permute-start.5 = (bf16[200,1024]{1,0:T(8,128)(2,1)}, bf16[200,1024]{1,0:T(8,128)(2,1)}, u32[]{:S(2)}, u32[]{:S(2)}) collective-permute-start(bf16[200,1024]{1,0:T(8,128)(2,1)} %get-tuple-element.119), channel_id=1, source_target_pairs={{0,5},{1,4},{2,7},{3,6},{4,1},{5,0},{6,3},{7,2},{8,13},{9,12},{10,... | collective-permute-start | bytes 1228808 | tf_op jit(solution)/shard_map/ppermute | solution.py:723
  100.7 70.5 %collective-permute-start.4 = (bf16[200,1024]{1,0:T(8,128)(2,1)}, bf16[200,1024]{1,0:T(8,128)(2,1)}, u32[]{:S(2)}, u32[]{:S(2)}) collective-permute-start(bf16[200,1024]{1,0:T(8,128)(2,1)} %get-tuple-element.117), channel_id=1, source_target_pairs={{0,4},{1,5},{2,6},{3,7},{4,0},{5,1},{6,2},{7,3},{8,12},{9,13},{10,... | collective-permute-start | bytes 1228808 | tf_op jit(solution)/shard_map/ppermute | solution.py:723
  152.8 57.5 %all-to-all-start.2 = ((bf16[4,200,1024]{2,1,0:T(8,128)(2,1)}), bf16[4,200,1024]{2,1,0:T(8,128)(2,1)}, u32[]{:S(2)}, u32[]{:S(2)}) async-start(bf16[4,200,1024]{2,1,0:T(8,128)(2,1)} %bitcast.152), calls=%async_computation.2 | async-start | bytes 3276800 | tf_op jit(solution)/shard_map/all_to_all | solution.py:813
  157.2 284.5 %reduce-scatter.2.cloned.1.call-start = ((), (), s32[]{:S(2)}) async-start(), calls=%async_computation.6 | async-start | bytes 21626880 | tf_op jit(solution)/shard_map/reduce_scatter | solution.py:854
  204.1 68.9 %collective-permute-start.10 = (bf16[200,1024]{1,0:T(8,128)(2,1)}, bf16[200,1024]{1,0:T(8,128)(2,1)S(1)}, u32[]{:S(2)}, u32[]{:S(2)}) collective-permute-start(bf16[200,1024]{1,0:T(8,128)(2,1)} %get-tuple-element.130), channel_id=1, source_target_pairs={{0,6},{1,7},{2,4},{3,5},{4,2},{5,3},{6,0},{7,1},{8,14},{9,15},{10,... | collective-permute-start | bytes 1228808 | tf_op jit(solution)/shard_map/ppermute | solution.py:723
  207.8 65.2 %collective-permute-start.11 = (bf16[200,1024]{1,0:T(8,128)(2,1)}, bf16[200,1024]{1,0:T(8,128)(2,1)S(1)}, u32[]{:S(2)}, u32[]{:S(2)}) collective-permute-start(bf16[200,1024]{1,0:T(8,128)(2,1)} %get-tuple-element.131), channel_id=1, source_target_pairs={{0,7},{1,6},{2,5},{3,4},{4,3},{5,2},{6,1},{7,0},{8,15},{9,14},{10,... | collective-permute-start | bytes 1228808 | tf_op jit(solution)/shard_map/ppermute | solution.py:723
  207.8 65.2 %collective-permute-start.8 = (bf16[200,1024]{1,0:T(8,128)(2,1)}, bf16[200,1024]{1,0:T(8,128)(2,1)S(1)}, u32[]{:S(2)}, u32[]{:S(2)}) collective-permute-start(bf16[200,1024]{1,0:T(8,128)(2,1)} %get-tuple-element.128), channel_id=1, source_target_pairs={{0,4},{1,5},{2,6},{3,7},{4,0},{5,1},{6,2},{7,3},{8,12},{9,13},{10,... | collective-permute-start | bytes 1228808 | tf_op jit(solution)/shard_map/ppermute | solution.py:723
  207.8 69.6 %collective-permute-start.9 = (bf16[200,1024]{1,0:T(8,128)(2,1)}, bf16[200,1024]{1,0:T(8,128)(2,1)}, u32[]{:S(2)}, u32[]{:S(2)}) collective-permute-start(bf16[200,1024]{1,0:T(8,128)(2,1)} %get-tuple-element.129), channel_id=1, source_target_pairs={{0,5},{1,4},{2,7},{3,6},{4,1},{5,0},{6,3},{7,2},{8,13},{9,12},{10,... | collective-permute-start | bytes 1228808 | tf_op jit(solution)/shard_map/ppermute | solution.py:723
  277.5 81.3 %all-to-all-start.3 = ((bf16[4,200,1024]{2,1,0:T(8,128)(2,1)}), bf16[4,200,1024]{2,1,0:T(8,128)(2,1)}, u32[]{:S(2)}, u32[]{:S(2)}) async-start(bf16[4,200,1024]{2,1,0:T(8,128)(2,1)} %bitcast.151), calls=%async_computation.3 | async-start | bytes 3276800 | tf_op jit(solution)/shard_map/all_to_all | solution.py:813
  283.9 57.4 %collective-permute-start.15 = (bf16[200,1024]{1,0:T(8,128)(2,1)}, bf16[200,1024]{1,0:T(8,128)(2,1)}, u32[]{:S(2)}, u32[]{:S(2)}) collective-permute-start(bf16[200,1024]{1,0:T(8,128)(2,1)} %get-tuple-element.158), channel_id=1, source_target_pairs={{0,7},{1,6},{2,5},{3,4},{4,3},{5,2},{6,1},{7,0},{8,15},{9,14},{10,... | collective-permute-start | bytes 1228808 | tf_op jit(solution)/shard_map/ppermute | solution.py:723
  286.2 55.0 %collective-permute-start.14 = (bf16[200,1024]{1,0:T(8,128)(2,1)}, bf16[200,1024]{1,0:T(8,128)(2,1)}, u32[]{:S(2)}, u32[]{:S(2)}) collective-permute-start(bf16[200,1024]{1,0:T(8,128)(2,1)} %get-tuple-element.156), channel_id=1, source_target_pairs={{0,6},{1,7},{2,4},{3,5},{4,2},{5,3},{6,0},{7,1},{8,14},{9,15},{10,... | collective-permute-start | bytes 1228808 | tf_op jit(solution)/shard_map/ppermute | solution.py:723
  287.8 61.9 %collective-permute-start.13 = (bf16[200,1024]{1,0:T(8,128)(2,1)}, bf16[200,1024]{1,0:T(8,128)(2,1)}, u32[]{:S(2)}, u32[]{:S(2)}) collective-permute-start(bf16[200,1024]{1,0:T(8,128)(2,1)} %get-tuple-element.154), channel_id=1, source_target_pairs={{0,5},{1,4},{2,7},{3,6},{4,1},{5,0},{6,3},{7,2},{8,13},{9,12},{10,... | collective-permute-start | bytes 1228808 | tf_op jit(solution)/shard_map/ppermute | solution.py:723
  287.8 71.0 %collective-permute-start.12 = (bf16[200,1024]{1,0:T(8,128)(2,1)}, bf16[200,1024]{1,0:T(8,128)(2,1)}, u32[]{:S(2)}, u32[]{:S(2)}) collective-permute-start(bf16[200,1024]{1,0:T(8,128)(2,1)} %get-tuple-element.152), channel_id=1, source_target_pairs={{0,4},{1,5},{2,6},{3,7},{4,0},{5,1},{6,2},{7,3},{8,12},{9,13},{10,... | collective-permute-start | bytes 1228808 | tf_op jit(solution)/shard_map/ppermute | solution.py:723
  372.7 40.9 %collective-permute-start.22 = (bf16[4,32,1536]{2,1,0:T(8,128)(2,1)}, bf16[4,32,1536]{2,1,0:T(8,128)(2,1)}, u32[]{:S(2)}, u32[]{:S(2)}) collective-permute-start(bf16[4,32,1536]{2,1,0:T(8,128)(2,1)} %fusion.35), channel_id=1, source_target_pairs={{0,6},{1,7},{2,4},{3,5},{4,2},{5,3},{6,0},{7,1},{8,14},{9,15},{10,... | collective-permute-start | bytes 1179656 | tf_op jit(solution)/shard_map/ppermute | solution.py:723
  375.8 37.9 %collective-permute-start.20 = (bf16[4,32,1536]{2,1,0:T(8,128)(2,1)}, bf16[4,32,1536]{2,1,0:T(8,128)(2,1)}, u32[]{:S(2)}, u32[]{:S(2)}) collective-permute-start(bf16[4,32,1536]{2,1,0:T(8,128)(2,1)} %get-tuple-element.231), channel_id=1, source_target_pairs={{0,2},{1,3},{2,0},{3,1},{4,6},{5,7},{6,4},{7,5},{8,10},{9,11},{10,... | collective-permute-start | bytes 1179656 | tf_op jit(solution)/shard_map/ppermute | solution.py:723
  375.8 37.9 %collective-permute-start.21 = (bf16[4,32,1536]{2,1,0:T(8,128)(2,1)}, bf16[4,32,1536]{2,1,0:T(8,128)(2,1)}, u32[]{:S(2)}, u32[]{:S(2)}) collective-permute-start(bf16[4,32,1536]{2,1,0:T(8,128)(2,1)} %get-tuple-element.230), channel_id=1, source_target_pairs={{0,4},{1,5},{2,6},{3,7},{4,0},{5,1},{6,2},{7,3},{8,12},{9,13},{10,... | collective-permute-start | bytes 1179656 | tf_op jit(solution)/shard_map/ppermute | solution.py:723
  (50 other events, 632.5 us)
Sparse Core Ops, SparseCore 0:
  251.8 178.8 reduce-scatter.1

commit v8 on v7

--- a/solution.py
+++ b/solution.py
@@ -23,7 +23,7 @@
 EXTRA = 8
 SHORT = pl.CostEstimate(flops=23_000_000_000, bytes_accessed=1 << 16, transcendentals=0)
 SMALL = pl.CostEstimate(flops=1 << 20, bytes_accessed=1 << 16, transcendentals=0)
-MEDIUM = pl.CostEstimate(flops=249_550_000_000, bytes_accessed=1 << 16, transcendentals=0)
+MEDIUM = pl.CostEstimate(flops=265_650_000_000, bytes_accessed=1 << 16, transcendentals=0)
 LARGE = pl.CostEstimate(flops=1 << 38, bytes_accessed=1 << 28, transcendentals=0)
 
 
@@ -692,7 +692,7 @@
     tile = 512
     steps, more = wide.shape[1] // tile, narrow.shape[1] // tile
     whole = once((tokens, rows))
-    early = (steps + more) * 5 // 8
+    early = (steps + more) // 2
     low = pl.BlockSpec((rows // 2, tile), lambda i: (0, jnp.minimum(i, early - 1)))
     high = pl.BlockSpec((rows // 2, tile), lambda i: (0, jnp.maximum(i - early, 0)))
     shapes = [jax.ShapeDtypeStruct((rows // 2, n * tile), jnp.bfloat16) for n in (early, steps + more - early)]

time: 471 us -> 473 us (level)
  waiting for transfers between devices: 63.7 us -> 69.5 us
    all_to_all x1, waiting for transfers between devices: 0.01 us -> 8.87 us  [on_device(): lax.all_to_all(together, ('dp', 'expert'), split_axis=0, concat_axis=0, t...]
  transfers between devices with their start and end apart: 37 -> 37, of which waited for: 9 -> 11; matrix products, arithmetic and copies ran while one was open for 16% -> 16% of each run, Pallas kernels for 47% -> 47%
where the time goes in v8:
time: 473 us; the launch traced here: 467 us
  Pallas kernels  226 us (48%)
  starting transfers between devices  76.2 us (16%)
  waiting for transfers between devices  69.5 us (15%)
  other arithmetic  32.4 us (7%)
  matrix products  31.2 us (7%)
  local copies, waits for them, and re-layouts  16.5 us (3%)
  between operations  14.9 us (3%)
    pallas_call x2, Pallas kernels, expert_rows(): pl.pallas_call(lambda *refs: expert_kernel(*refs, ways=ways, parts=parts)...  65.9 us
    ppermute x31, waiting for transfers between devices, swap(): return lax.ppermute(value, axis, [(k, k ^ step) for k in range(size)])  50.2 us
    ppermute x31, starting transfers between devices, swap(): return lax.ppermute(value, axis, [(k, k ^ step) for k in range(size)])  47.7 us
    pallas_call x1, Pallas kernels, weight_grads(): pl.pallas_call(lambda *refs: weight_kernel(*refs, ways=ways, copies=copie...  41.3 us
    all_to_all x4, starting transfers between devices, near(): lax.all_to_all(parts, 'expert', split_axis=0, concat_axis=0, axis_index_g...  24.8 us
    dot_general x5, matrix products, dot(): return lax.dot_general(a, b, dims, preferred_element_type=jnp.float32)  24.8 us
    pallas_call x1, Pallas kernels, attention_backward(): pl.pallas_call(attention_backward_kernel, grid=(pairs,), in_specs=[pl.Blo...  22.7 us
    pallas_call x1, Pallas kernels, result_rows(): pl.pallas_call(result_kernel, grid=(f // tile,), in_specs=[pl.BlockSpec((...  21.3 us
  transfers between devices with their start and end apart: 37, of which 11 were waited for; matrix products, arithmetic and copies ran while one was open for 16% of the time, Pallas kernels for 47%

profile of v8, /device:TPU:0, one launch (start us, length us, event | category | flops | bytes accessed | tf_op | source)
XLA Modules:
  0.0 467.2 jit_solution(9584847815438317365)
XLA Ops:
  7.2 6.2 %pack_first.1 = (bf16[832,1024]{1,0:T(8,128)(2,1)}, bf16[208,1024]{1,0:T(8,128)(2,1)}, bf16[208,1024]{1,0:T(8,128)(2,1)}, bf16[208,1024]{1,0:T(8,128)(2,1)}, bf1...) custom-call(s32[1]{0:T(128)} %bitcast.refs_0_, s32[2,640]{1,0:T(2,128)} %bitcast.163, bf16[640,1024]{1,0:T(8,128)(2,1)} %upstream_ref.1), custom_call_target="tpu_custom_call" | custom-call | flops 1048576 | bytes 65536 | tf_op jit(solution)/shard_map/pack_first/pallas_call | solution.py:323
  28.9 8.5 %convolution_convert_fusion.q_ref.k_ref.v_ref = bf16[640,3072]{1,0:T(8,128)(2,1)} fusion(bf16[640,1024]{1,0:T(8,128)(2,1)S(1)} %fusion.9.refs_1_, bf16[1024,3072]{1,0:T(8,128)(2,1)} %param.16), kind=kOutput, calls=%fused_computation.3 | convolution fusion | flops 4028497920 | bytes 11534336 | tf_op jit(solution)/shard_map/dot_general | solution.py:31
  37.4 16.0 %attention_forward.1 = (bf16[640,1024]{1,0:T(8,128)(2,1)}, f32[8,2,640]{2,1,0:T(2,128)}) custom-call(s32[1,2]{1,0:T(1,128)} %lengths_ref.3, f32[8,2,512]{2,1,0:T(2,128)} %reshape.371.bias_ref, bf16[640,3072]{1,0:T(8,128)(2,1)} %convolution_convert_fusion.q_ref.k_ref.v_ref, bf16[640,3072]{1,0:T(8,128)(2,1)} %convolution_convert_fusion.q_ref.k_ref.v_ref, ...), custom_call_target="tpu_custom_call" | custom-call | flops 1048576 | bytes 65536 | tf_op jit(solution)/shard_map/attention_forward/pallas_call | solution.py:110
  67.6 5.0 %collective-permute-done.1.refs_3_.refs_12_ = bf16[208,1024]{1,0:T(8,128)(2,1)} collective-permute-done((bf16[208,1024]{1,0:T(8,128)(2,1)}, bf16[208,1024]{1,0:T(8,128)(2,1)}, u32[]{:S(2)}, u32[]{:S(2)}) %collective-permute-start.1) | collective-permute-done | bytes 426016 | tf_op jit(solution)/shard_map/ppermute | solution.py:723
  72.5 10.4 %all-to-all-done = bf16[4,208,1024]{2,1,0:T(8,128)(2,1)} async-done(((bf16[4,208,1024]{2,1,0:T(8,128)(2,1)}), bf16[4,208,1024]{2,1,0:T(8,128)(2,1)}, u32[]{:S(2)}, u32[]{:S(2)}) %all-to-all-start) | async-done | bytes 1703968 | tf_op jit(solution)/shard_map/all_to_all | solution.py:813
  83.0 10.8 %all-to-all-start.1 = ((bf16[4,200,1024]{2,1,0:T(8,128)(2,1)}), bf16[4,200,1024]{2,1,0:T(8,128)(2,1)}, u32[]{:S(2)}, u32[]{:S(2)}) async-start(bf16[4,200,1024]{2,1,0:T(8,128)(2,1)} %bitcast.155), calls=%async_computation.1 | async-start | bytes 3276800 | tf_op jit(solution)/shard_map/all_to_all | solution.py:813
  93.7 6.2 %collective-permute-start.7 = (bf16[200,1024]{1,0:T(8,128)(2,1)}, bf16[200,1024]{1,0:T(8,128)(2,1)}, u32[]{:S(2)}, u32[]{:S(2)}) collective-permute-start(bf16[200,1024]{1,0:T(8,128)(2,1)} %get-tuple-element.123), channel_id=1, source_target_pairs={{0,7},{1,6},{2,5},{3,4},{4,3},{5,2},{6,1},{7,0},{8,15},{9,14},{10,... | collective-permute-start | bytes 1228808 | tf_op jit(solution)/shard_map/ppermute | solution.py:723
  102.8 16.7 %slope_rows.1 = (bf16[1600,2816]{1,0:T(8,128)(2,1)}, f32[1600,128]{1,0:T(8,128)}) custom-call(bf16[2816,1024]{1,0:T(8,128)(2,1)} %bitcast.143, bf16[832,1024]{1,0:T(8,128)(2,1)} %bitcast.7.refs_1_.refs_10_, bf16[208,1024]{1,0:T(8,128)(2,1)} %collective-permute-done.refs_2_.refs_11_, bf16[208,1024]{1,0:T(8,128)(2,1)} %collective-permute-done.1.refs_3_.refs_12_, ...), custom_call_target="tpu_custom_call" | custom-call | flops 274877906944 | bytes 268435456 | tf_op jit(solution)/shard_map/slope_rows/pallas_call | solution.py:522
  119.5 32.9 %expert_rows.2 = (bf16[1600,2816]{1,0:T(8,128)(2,1)}, bf16[1600,2816]{1,0:T(8,128)(2,1)}, bf16[1600,2816]{1,0:T(8,128)(2,1)}, f32[800,128]{1,0:T(8,128)}, f32[12...) custom-call(s32[1]{0:T(128)} %bitcast.refs_0_, bf16[1600,2816]{1,0:T(8,128)(2,1)} %get-tuple-element.107.refs_1_, ...), custom_call_target="tpu_custom_call" | custom-call | flops 1048576 | bytes 65536 | tf_op jit(solution)/shard_map/expert_rows/pallas_call | solution.py:476
  161.7 9.0 %collective-permute-done.4.refs_6_ = bf16[200,1024]{1,0:T(8,128)(2,1)} collective-permute-done((bf16[200,1024]{1,0:T(8,128)(2,1)}, bf16[200,1024]{1,0:T(8,128)(2,1)}, u32[]{:S(2)}, u32[]{:S(2)}) %collective-permute-start.4) | collective-permute-done | bytes 409632 | tf_op jit(solution)/shard_map/ppermute | solution.py:723
  170.7 33.0 %expert_rows.3 = (bf16[1600,2816]{1,0:T(8,128)(2,1)}, bf16[1600,2816]{1,0:T(8,128)(2,1)}, bf16[1600,2816]{1,0:T(8,128)(2,1)}, f32[800,128]{1,0:T(8,128)}, f32[12...) custom-call(s32[1]{0:T(128)} %bitcast.refs_0_, ...), custom_call_target="tpu_custom_call", output_to_operand_aliasing={{0}: (10, {}), {1}: (11, {}), {2}: (12, {})} | custom-call | flops 23000000512 | bytes 65536 | tf_op jit(solution)/shard_map/expert_rows/pallas_call | solution.py:476
  209.9 41.3 %weight_grads.1 = bf16[2816,3072]{1,0:T(8,128)(2,1)} custom-call(bf16[1600,2816]{1,0:T(8,128)(2,1)} %get-tuple-element.138.refs_0_.hidden_ref, bf16[1600,2816]{1,0:T(8,128)(2,1)} %get-tuple-element.134.refs_1_, bf16[1600,2816]{1,0:T(8,128)(2,1)} %get-tuple-element.135.refs_2_, f32[800,128]{1,0:T(8,128)} %get-tuple-element.136.refs_3_, ...), custom_call_target="tpu_custom_call" | custom-call | flops 1048576 | bytes 65536 | tf_op jit(solution)/shard_map/weight_grads/pallas_call | solution.py:599
  251.2 21.3 %result_rows.1 = (bf16[800,1024]{1,0:T(8,128)(2,1)}, bf16[200,1024]{1,0:T(8,128)(2,1)}, bf16[200,1024]{1,0:T(8,128)(2,1)}, bf16[200,1024]{1,0:T(8,128)(2,1)}, bf16[200,1024]{1,0:T(8,128)(2,1)}) custom-call(bf16[1600,2816]{1,0:T(8,128)(2,1)} %get-tuple-element.138.refs_0_.hidden_ref, bf16[2816,1024]{1,0:T(8,128)(2,1)} %bitcast.144), custom_call_target="tpu_custom_call" | custom-call | flops 1048576 | bytes 65536 | tf_op jit(solution)/shard_map/result_rows/pallas_call | solution.py:643
  289.8 9.7 %combine_back.1 = (f32[640,1024]{1,0:T(8,128)}, bf16[640,1024]{1,0:T(8,128)(2,1)}, f32[1,1024]{1,0:T(1,128)}) custom-call(s32[640,2]{1,0:T(8,128)} %bitcast.156, f32[640,2]{1,0:T(8,128)} %exponential_divide_fusion.gates_ref, f32[640,1024]{1,0:T(8,128)} %copy-done.6, f32[640,1]{1,0:T(8,128)} %rsqrt.16.scale_ref, f32[1,1024]{1,0:T(1,128)} %bitcast.164, ...), custom_call_target="tpu_custom_call" | custom-call | flops 1048576 | bytes 65536 | tf_op jit(solution)/shard_map/combine_back/pallas_call | solution.py:384
  303.5 22.7 %attention_backward.1 = (bf16[640,3072]{1,0:T(8,128)(2,1)}, f32[8,2,136,384]{3,2,1,0:T(8,128)}) custom-call(s32[1,2]{1,0:T(1,128)} %lengths_ref.3, f32[8,2,512]{2,1,0:T(2,128)} %reshape.371.bias_ref, f32[8,2,640]{2,1,0:T(2,128)} %get-tuple-element.106.stat_ref, bf16[640,3072]{1,0:T(8,128)(2,1)} %convolution_convert_fusion.q_ref.k_ref.v_ref, ...), custom_call_target="tpu_custom_call" | custom-call | flops 1048576 | bytes 65536 | tf_op jit(solution)/shard_map/attention_backward/pallas_call | solution.py:223
  326.2 14.5 %shared_grads.1 = (bf16[512,2048]{1,0:T(8,128)(2,1)}, bf16[512,2048]{1,0:T(8,128)(2,1)}, bf16[512,2048]{1,0:T(8,128)(2,1)}, bf16[512,2048]{1,0:T(8,128)(2,1)}) custom-call(s32[1]{0:T(128)S(6)} %select_n.127.refs_0_, bf16[640,1024]{1,0:T(8,128)(2,1)} %copy-done.7, bf16[640,3072]{1,0:T(8,128)(2,1)} %get-tuple-element.165.refs_2_, ...), custom_call_target="tpu_custom_call" | custom-call | flops 1048576 | bytes 65536 | tf_op jit(solution)/shard_map/shared_grads/pallas_call | solution.py:699
  340.7 8.8 %collective-permute-done.13.refs_2_ = bf16[200,1024]{1,0:T(8,128)(2,1)} collective-permute-done((bf16[200,1024]{1,0:T(8,128)(2,1)}, bf16[200,1024]{1,0:T(8,128)(2,1)}, u32[]{:S(2)}, u32[]{:S(2)}) %collective-permute-start.13) | collective-permute-done | bytes 409632 | tf_op jit(solution)/shard_map/ppermute | solution.py:723
  349.5 9.1 %collective-permute-done.12.refs_1_ = bf16[200,1024]{1,0:T(8,128)(2,1)} collective-permute-done((bf16[200,1024]{1,0:T(8,128)(2,1)}, bf16[200,1024]{1,0:T(8,128)(2,1)}, u32[]{:S(2)}, u32[]{:S(2)}) %collective-permute-start.12) | collective-permute-done | bytes 409632 | tf_op jit(solution)/shard_map/ppermute | solution.py:723
  360.6 6.1 %fusion.16 = f32[32,8,2]{0,1,2:T(8,128)S(1)} fusion(f32[8,2,136,384]{3,2,1,0:T(8,128)} %get-tuple-element.166, s32[136,384]{1,0:T(8,128)S(1)} %fusion.39), kind=kOutput, calls=%fused_computation.27 | convolution fusion | flops 322535424 | bytes 3553280 | tf_op jit(solution)/shard_map/ghrc,rcb->bgh/dot_general | solution.py:276
  387.1 8.9 %fusion.14 = (f32[1024]{0:T(1024)S(1)}, f32[640]{0:T(1024)S(1)}, f32[640,1024]{1,0:T(8,128)}) fusion(bf16[640,1024]{1,0:T(8,128)(2,1)S(1)} %copy-done.3, f32[640]{0:T(1024)S(1)} %copy-done.19, f32[1024]{0:T(1024)S(1)} %copy-done.26, bf16[640,3072]{1,0:T(8,128)(2,1)S(1)} %copy-done.9, bf16[1024,3072]{1,0:T(8,128)(2,1)} %param.16), kind=kOutput, calls=%fused_computation.20 | convolution fusion | flops 4031117824 | bytes 14169088 | tf_op jit(solution)/shard_map/dot_general | solution.py:31
  401.9 7.3 %combine_output.1 = bf16[640,1024]{1,0:T(8,128)(2,1)} custom-call(s32[640,2]{1,0:T(8,128)} %bitcast.157, f32[640,2]{1,0:T(8,128)} %exponential_divide_fusion.gates_ref, f32[640,1024]{1,0:T(8,128)} %copy-done.6, bf16[800,1024]{1,0:T(8,128)(2,1)} %bitcast.17.refs_0_, bf16[200,1024]{1,0:T(8,128)(2,1)} %collective-permute-done.12.refs_1_, ...), custom_call_target="tpu_custom_call" | custom-call | flops 265649995776 | bytes 65536 | tf_op jit(solution)/shard_map/combine_output/pallas_call | solution.py:361
  409.3 5.0 %fusion.13 = f32[640,1024]{1,0:T(8,128)} fusion(f32[640,1024]{1,0:T(8,128)} %get-tuple-element.161, bf16[640,1024]{1,0:T(8,128)(2,1)S(1)} %copy-done.4, f32[640,1024]{1,0:T(8,128)} %get-tuple-element.251, f32[640]{0:T(1024)S(1)} %copy-done.28, f32[1024]{0:T(1024)S(1)} %copy-done.27, f32[640]{0:T(1024)S(1)} %copy-done.20), kind=kLoop, calls=%fused_computation.19 | loop fusion | flops 4587520 | bytes 9184256 | tf_op jit(solution)/shard_map/add | solution.py:873
  414.4 8.9 %all-to-all-done.4 = f32[32,1,336]{2,1,0:T(1,128)} async-done(((f32[32,1,336]{2,1,0:T(1,128)}), f32[32,1,336]{2,1,0:T(1,128)}, u32[]{:S(2)}, u32[]{:S(2)}) %all-to-all-start.4) | async-done | bytes 43040 | tf_op jit(solution)/shard_map/all_to_all | solution.py:883
  435.4 6.1 %collective-permute-done.23 = bf16[128,1024]{1,0:T(8,128)(2,1)S(1)} collective-permute-done((bf16[128,1024]{1,0:T(8,128)(2,1)S(1)}, bf16[128,1024]{1,0:T(8,128)(2,1)S(1)}, u32[]{:S(2)}, u32[]{:S(2)}) %collective-permute-start.23) | collective-permute-done | bytes 262176 | tf_op jit(solution)/shard_map/ppermute | solution.py:723
  (195 shorter events, 128.0 us)
Async XLA Ops:
  13.4 54.2 %collective-permute-start = (bf16[208,1024]{1,0:T(8,128)(2,1)}, bf16[208,1024]{1,0:T(8,128)(2,1)}, u32[]{:S(2)}, u32[]{:S(2)}) collective-permute-start(bf16[208,1024]{1,0:T(8,128)(2,1)} %get-tuple-element.100), channel_id=1, source_target_pairs={{0,4},{1,5},{2,6},{3,7},{4,0},{5,1},{6,2},{7,3},{8,12},{9,13},{10,... | collective-permute-start | bytes 1277960 | tf_op jit(solution)/shard_map/ppermute | solution.py:723
  17.5 55.0 %collective-permute-start.1 = (bf16[208,1024]{1,0:T(8,128)(2,1)}, bf16[208,1024]{1,0:T(8,128)(2,1)}, u32[]{:S(2)}, u32[]{:S(2)}) collective-permute-start(bf16[208,1024]{1,0:T(8,128)(2,1)} %get-tuple-element.101), channel_id=1, source_target_pairs={{0,5},{1,4},{2,7},{3,6},{4,1},{5,0},{6,3},{7,2},{8,13},{9,12},{10,... | collective-permute-start | bytes 1277960 | tf_op jit(solution)/shard_map/ppermute | solution.py:723
  17.5 55.0 %collective-permute-start.2 = (bf16[208,1024]{1,0:T(8,128)(2,1)}, bf16[208,1024]{1,0:T(8,128)(2,1)}, u32[]{:S(2)}, u32[]{:S(2)}) collective-permute-start(bf16[208,1024]{1,0:T(8,128)(2,1)} %get-tuple-element.102), channel_id=1, source_target_pairs={{0,6},{1,7},{2,4},{3,5},{4,2},{5,3},{6,0},{7,1},{8,14},{9,15},{10,... | collective-permute-start | bytes 1277960 | tf_op jit(solution)/shard_map/ppermute | solution.py:723
  20.6 52.0 %collective-permute-start.3 = (bf16[208,1024]{1,0:T(8,128)(2,1)}, bf16[208,1024]{1,0:T(8,128)(2,1)}, u32[]{:S(2)}, u32[]{:S(2)}) collective-permute-start(bf16[208,1024]{1,0:T(8,128)(2,1)} %get-tuple-element.103), channel_id=1, source_target_pairs={{0,7},{1,6},{2,5},{3,4},{4,3},{5,2},{6,1},{7,0},{8,15},{9,14},{10,... | collective-permute-start | bytes 1277960 | tf_op jit(solution)/shard_map/ppermute | solution.py:723
  21.2 61.8 %all-to-all-start = ((bf16[4,208,1024]{2,1,0:T(8,128)(2,1)}), bf16[4,208,1024]{2,1,0:T(8,128)(2,1)}, u32[]{:S(2)}, u32[]{:S(2)}) async-start(bf16[4,208,1024]{2,1,0:T(8,128)(2,1)} %bitcast.152), calls=%async_computation | async-start | bytes 3407872 | tf_op jit(solution)/shard_map/all_to_all | solution.py:813
  93.7 63.3 %collective-permute-start.7 = (bf16[200,1024]{1,0:T(8,128)(2,1)}, bf16[200,1024]{1,0:T(8,128)(2,1)}, u32[]{:S(2)}, u32[]{:S(2)}) collective-permute-start(bf16[200,1024]{1,0:T(8,128)(2,1)} %get-tuple-element.123), channel_id=1, source_target_pairs={{0,7},{1,6},{2,5},{3,4},{4,3},{5,2},{6,1},{7,0},{8,15},{9,14},{10,... | collective-permute-start | bytes 1228808 | tf_op jit(solution)/shard_map/ppermute | solution.py:723
  99.9 57.2 %collective-permute-start.6 = (bf16[200,1024]{1,0:T(8,128)(2,1)}, bf16[200,1024]{1,0:T(8,128)(2,1)}, u32[]{:S(2)}, u32[]{:S(2)}) collective-permute-start(bf16[200,1024]{1,0:T(8,128)(2,1)} %get-tuple-element.121), channel_id=1, source_target_pairs={{0,6},{1,7},{2,4},{3,5},{4,2},{5,3},{6,0},{7,1},{8,14},{9,15},{10,... | collective-permute-start | bytes 1228808 | tf_op jit(solution)/shard_map/ppermute | solution.py:723
  100.2 61.5 %collective-permute-start.5 = (bf16[200,1024]{1,0:T(8,128)(2,1)}, bf16[200,1024]{1,0:T(8,128)(2,1)}, u32[]{:S(2)}, u32[]{:S(2)}) collective-permute-start(bf16[200,1024]{1,0:T(8,128)(2,1)} %get-tuple-element.119), channel_id=1, source_target_pairs={{0,5},{1,4},{2,7},{3,6},{4,1},{5,0},{6,3},{7,2},{8,13},{9,12},{10,... | collective-permute-start | bytes 1228808 | tf_op jit(solution)/shard_map/ppermute | solution.py:723
  100.2 70.5 %collective-permute-start.4 = (bf16[200,1024]{1,0:T(8,128)(2,1)}, bf16[200,1024]{1,0:T(8,128)(2,1)}, u32[]{:S(2)}, u32[]{:S(2)}) collective-permute-start(bf16[200,1024]{1,0:T(8,128)(2,1)} %get-tuple-element.117), channel_id=1, source_target_pairs={{0,4},{1,5},{2,6},{3,7},{4,0},{5,1},{6,2},{7,3},{8,12},{9,13},{10,... | collective-permute-start | bytes 1228808 | tf_op jit(solution)/shard_map/ppermute | solution.py:723
  152.4 57.5 %all-to-all-start.2 = ((bf16[4,200,1024]{2,1,0:T(8,128)(2,1)}), bf16[4,200,1024]{2,1,0:T(8,128)(2,1)}, u32[]{:S(2)}, u32[]{:S(2)}) async-start(bf16[4,200,1024]{2,1,0:T(8,128)(2,1)} %bitcast.154), calls=%async_computation.2 | async-start | bytes 3276800 | tf_op jit(solution)/shard_map/all_to_all | solution.py:813
  156.8 289.5 %reduce-scatter.2.cloned.1.call-start = ((), (), s32[]{:S(2)}) async-start(), calls=%async_computation.6 | async-start | bytes 21626880 | tf_op jit(solution)/shard_map/reduce_scatter | solution.py:854
  203.7 68.9 %collective-permute-start.10 = (bf16[200,1024]{1,0:T(8,128)(2,1)}, bf16[200,1024]{1,0:T(8,128)(2,1)S(1)}, u32[]{:S(2)}, u32[]{:S(2)}) collective-permute-start(bf16[200,1024]{1,0:T(8,128)(2,1)} %get-tuple-element.130), channel_id=1, source_target_pairs={{0,6},{1,7},{2,4},{3,5},{4,2},{5,3},{6,0},{7,1},{8,14},{9,15},{10,... | collective-permute-start | bytes 1228808 | tf_op jit(solution)/shard_map/ppermute | solution.py:723
  207.4 65.1 %collective-permute-start.11 = (bf16[200,1024]{1,0:T(8,128)(2,1)}, bf16[200,1024]{1,0:T(8,128)(2,1)S(1)}, u32[]{:S(2)}, u32[]{:S(2)}) collective-permute-start(bf16[200,1024]{1,0:T(8,128)(2,1)} %get-tuple-element.131), channel_id=1, source_target_pairs={{0,7},{1,6},{2,5},{3,4},{4,3},{5,2},{6,1},{7,0},{8,15},{9,14},{10,... | collective-permute-start | bytes 1228808 | tf_op jit(solution)/shard_map/ppermute | solution.py:723
  207.4 65.2 %collective-permute-start.8 = (bf16[200,1024]{1,0:T(8,128)(2,1)}, bf16[200,1024]{1,0:T(8,128)(2,1)S(1)}, u32[]{:S(2)}, u32[]{:S(2)}) collective-permute-start(bf16[200,1024]{1,0:T(8,128)(2,1)} %get-tuple-element.128), channel_id=1, source_target_pairs={{0,4},{1,5},{2,6},{3,7},{4,0},{5,1},{6,2},{7,3},{8,12},{9,13},{10,... | collective-permute-start | bytes 1228808 | tf_op jit(solution)/shard_map/ppermute | solution.py:723
  207.4 69.6 %collective-permute-start.9 = (bf16[200,1024]{1,0:T(8,128)(2,1)}, bf16[200,1024]{1,0:T(8,128)(2,1)}, u32[]{:S(2)}, u32[]{:S(2)}) collective-permute-start(bf16[200,1024]{1,0:T(8,128)(2,1)} %get-tuple-element.129), channel_id=1, source_target_pairs={{0,5},{1,4},{2,7},{3,6},{4,1},{5,0},{6,3},{7,2},{8,13},{9,12},{10,... | collective-permute-start | bytes 1228808 | tf_op jit(solution)/shard_map/ppermute | solution.py:723
  277.1 81.5 %all-to-all-start.3 = ((bf16[4,200,1024]{2,1,0:T(8,128)(2,1)}), bf16[4,200,1024]{2,1,0:T(8,128)(2,1)}, u32[]{:S(2)}, u32[]{:S(2)}) async-start(bf16[4,200,1024]{2,1,0:T(8,128)(2,1)} %bitcast.153), calls=%async_computation.3 | async-start | bytes 3276800 | tf_op jit(solution)/shard_map/all_to_all | solution.py:813
  283.7 57.0 %collective-permute-start.15 = (bf16[200,1024]{1,0:T(8,128)(2,1)}, bf16[200,1024]{1,0:T(8,128)(2,1)}, u32[]{:S(2)}, u32[]{:S(2)}) collective-permute-start(bf16[200,1024]{1,0:T(8,128)(2,1)} %get-tuple-element.158), channel_id=1, source_target_pairs={{0,7},{1,6},{2,5},{3,4},{4,3},{5,2},{6,1},{7,0},{8,15},{9,14},{10,... | collective-permute-start | bytes 1228808 | tf_op jit(solution)/shard_map/ppermute | solution.py:723
  286.0 54.7 %collective-permute-start.14 = (bf16[200,1024]{1,0:T(8,128)(2,1)}, bf16[200,1024]{1,0:T(8,128)(2,1)}, u32[]{:S(2)}, u32[]{:S(2)}) collective-permute-start(bf16[200,1024]{1,0:T(8,128)(2,1)} %get-tuple-element.156), channel_id=1, source_target_pairs={{0,6},{1,7},{2,4},{3,5},{4,2},{5,3},{6,0},{7,1},{8,14},{9,15},{10,... | collective-permute-start | bytes 1228808 | tf_op jit(solution)/shard_map/ppermute | solution.py:723
  287.6 61.9 %collective-permute-start.13 = (bf16[200,1024]{1,0:T(8,128)(2,1)}, bf16[200,1024]{1,0:T(8,128)(2,1)}, u32[]{:S(2)}, u32[]{:S(2)}) collective-permute-start(bf16[200,1024]{1,0:T(8,128)(2,1)} %get-tuple-element.154), channel_id=1, source_target_pairs={{0,5},{1,4},{2,7},{3,6},{4,1},{5,0},{6,3},{7,2},{8,13},{9,12},{10,... | collective-permute-start | bytes 1228808 | tf_op jit(solution)/shard_map/ppermute | solution.py:723
  287.6 71.0 %collective-permute-start.12 = (bf16[200,1024]{1,0:T(8,128)(2,1)}, bf16[200,1024]{1,0:T(8,128)(2,1)}, u32[]{:S(2)}, u32[]{:S(2)}) collective-permute-start(bf16[200,1024]{1,0:T(8,128)(2,1)} %get-tuple-element.152), channel_id=1, source_target_pairs={{0,4},{1,5},{2,6},{3,7},{4,0},{5,1},{6,2},{7,3},{8,12},{9,13},{10,... | collective-permute-start | bytes 1228808 | tf_op jit(solution)/shard_map/ppermute | solution.py:723
  372.8 51.2 %collective-permute-start.18 = (bf16[2,128,1024]{2,1,0:T(8,128)(2,1)}, bf16[2,128,1024]{2,1,0:T(8,128)(2,1)}, u32[]{:S(2)}, u32[]{:S(2)}) collective-permute-start(bf16[2,128,1024]{2,1,0:T(8,128)(2,1)} %fusion.22), channel_id=1, source_target_pairs={{0,8},{8,0},{16,24},{24,16},{1,9},{9,1},{17,25},{25,17},{2,10},{10... | collective-permute-start | bytes 1572872 | tf_op jit(solution)/shard_map/ppermute | solution.py:723
  376.4 47.6 %collective-permute-start.22 = (bf16[4,32,2048]{2,1,0:T(8,128)(2,1)}, bf16[4,32,2048]{2,1,0:T(8,128)(2,1)}, u32[]{:S(2)}, u32[]{:S(2)}) collective-permute-start(bf16[4,32,2048]{2,1,0:T(8,128)(2,1)} %fusion.27), channel_id=1, source_target_pairs={{0,6},{1,7},{2,4},{3,5},{4,2},{5,3},{6,0},{7,1},{8,14},{9,15},{10,... | collective-permute-start | bytes 1572872 | tf_op jit(solution)/shard_map/ppermute | solution.py:723
  379.8 44.2 %collective-permute-start.20 = (bf16[4,32,2048]{2,1,0:T(8,128)(2,1)}, bf16[4,32,2048]{2,1,0:T(8,128)(2,1)}, u32[]{:S(2)}, u32[]{:S(2)}) collective-permute-start(bf16[4,32,2048]{2,1,0:T(8,128)(2,1)} %get-tuple-element.231), channel_id=1, source_target_pairs={{0,2},{1,3},{2,0},{3,1},{4,6},{5,7},{6,4},{7,5},{8,10},{9,11},{10,... | collective-permute-start | bytes 1572872 | tf_op jit(solution)/shard_map/ppermute | solution.py:723
  379.9 44.1 %collective-permute-start.21 = (bf16[4,32,2048]{2,1,0:T(8,128)(2,1)}, bf16[4,32,2048]{2,1,0:T(8,128)(2,1)}, u32[]{:S(2)}, u32[]{:S(2)}) collective-permute-start(bf16[4,32,2048]{2,1,0:T(8,128)(2,1)} %get-tuple-element.230), channel_id=1, source_target_pairs={{0,4},{1,5},{2,6},{3,7},{4,0},{5,1},{6,2},{7,3},{8,12},{9,13},{10,... | collective-permute-start | bytes 1572872 | tf_op jit(solution)/shard_map/ppermute | solution.py:723
  (45 other events, 595.9 us)
Sparse Core Ops, SparseCore 0:
  251.3 171.0 reduce-scatter.1
